TPU v7x, 32 devices: a whole 2x2x4 slice. The times are simulated.
32 devices in a mesh: gx: 4 (over y, x), gy: 8 (over z, core).
Axes of the slice: x: 2, y: 2, z: 4, core: 2. Of those that a mesh axis runs over, the one named last changes fastest.
Arguments:
- stream_in: bfloat16 [256, 4096], P('gx', 'gy'), may hold values from -6 to 6
- queries: bfloat16 [256, 4096], P('gx'), may hold values from -28 to 28
- suffix_keys: bfloat16 [256, 1024], P('gx'), may hold values from -6 to 6
- suffix_values: bfloat16 [256, 1024], P('gx'), may hold values from -6 to 6
- prefix_keys: bfloat16 [4, 4096, 1024], P('gx', 'gy'), may hold values from -16 to 16
- prefix_values: bfloat16 [4, 4096, 1024], P('gx', 'gy'), may hold values from -6 to 6
- lengths: int32 [4, 4], P('gx'), may hold values from 1 to 32, 64 in all within a row
- req_group: int32 [4, 4], P('gx'), may hold values from 0 to 2
- owners: int32 [3], replicated, may hold values from 0 to 3, as said below
- out_proj: bfloat16 [4096, 4096], P(None, 'gy'), may hold values from -0.09375 to 0.09375
- norm_gain: float32 [4096], P('gy'), may hold values from 0.1 to 1.9
- w_gate: bfloat16 [8, 4096, 8192], P(None, 'gy', 'gx'), may hold values from -0.09375 to 0.09375
- w_up: bfloat16 [8, 4096, 8192], P(None, 'gy', 'gx'), may hold values from -0.09375 to 0.09375
- w_down: bfloat16 [8, 8192, 4096], P(None, 'gx', 'gy'), may hold values from -0.0625 to 0.0625
- routes: int32 [256, 2], replicated, may hold values from 0 to 7, all different within a row; in each aligned block of 256 rows (0 to 255, 256 to 511, ...) at most 96 rows name the same one
- route_logits: float32 [256, 2], replicated, may hold values from -6 to 6
Outputs:
- layer_out: bfloat16 [256, 4096], P('gx', 'gy')
Inputs may be any that keep to these rules, and one draw needn't show every extreme that they name: `owners`: the 3 entries are different. `routes`: the two entries of a row differ; at most 96 rows name one expert. `lengths`: each row sums to 64; its largest entry is 32.
All inputs are finite; a program needn't handle non-finite values.
Results may differ from a plain program's by a relative error of at most 0.008.
Values may be sent and summed in bfloat16 or wider, within the bound.
No kernel may reach another device: no remote copies, remote signals or barrier semaphores. Data moves between devices by JAX's collectives and lax.ppermute only.
A program may use at most 192 MiB of HBM per device.

v0:
```python
import math

import jax
import jax.numpy as jnp
from jax import lax
from jax.sharding import PartitionSpec as P

D = 4096
HD = 128
GROUPS = 3


NEGATIVE = -1e30
EPSILON = 1e-05


def spread(value, axis, source):
    kept = jnp.where(lax.axis_index(axis) == source, value, 0).astype(value.dtype)
    return lax.psum(kept, axis)


def combined_all(value, axis, join):
    pieces = jax.tree.map(lambda part: lax.all_gather(part, axis), value)
    head = jax.tree.map(lambda part: part[0], pieces)
    tail = jax.tree.map(lambda part: part[1:], pieces)
    total, _ = lax.scan(lambda total, section: (join(total, section), None), head, tail)
    return total


def combine_parts(first, second):
    first_max, first_total, first_acc = first
    second_max, second_total, second_acc = second
    joined = jnp.maximum(first_max, second_max)
    first_factor = jnp.exp(first_max - joined)
    second_factor = jnp.exp(second_max - joined)
    return (
        joined,
        first_total * first_factor + second_total * second_factor,
        first_acc * first_factor[..., None] + second_acc * second_factor[..., None],
    )


def body(
    stream_in,
    queries,
    suffix_keys,
    suffix_values,
    prefix_keys,
    prefix_values,
    lengths,
    req_group,
    owners,
    out_proj,
    norm_gain,
    w_gate,
    w_up,
    w_down,
    routes,
    route_logits,
):
    highest = lax.Precision.HIGHEST
    tok_dev = queries.shape[0]
    kv_heads = suffix_keys.shape[1] // HD
    per_kv = queries.shape[1] // suffix_keys.shape[1]
    scaling = 1.0 / math.sqrt(HD)
    gy_index = lax.axis_index("gy")
    places = jnp.arange(tok_dev, dtype=jnp.int32)
    ends = jnp.cumsum(lengths[0])
    requests = jnp.sum((ends[None, :] <= places[:, None]).astype(jnp.int32), axis=1)
    picks = (requests[:, None] == jnp.arange(ends.shape[0], dtype=jnp.int32)[None, :]).astype(
        jnp.int32
    )
    group_ids = jnp.sum(picks * req_group[0][None, :], axis=1)
    query_blocks = queries.reshape(tok_dev, kv_heads, per_kv, HD)
    allowed = (
        (requests[:, None] == requests[None, :])
        & (places[None, :] <= places[:, None])
        & (gy_index == 0)
    )
    suffix_k = suffix_keys.reshape(tok_dev, kv_heads, HD)
    suffix_v = suffix_values.reshape(tok_dev, kv_heads, HD)
    suffix_scores = (
        jnp.einsum("tcqd,scd->tcqs", query_blocks, suffix_k, preferred_element_type=jnp.float32)
        * scaling
    )
    suffix_masked = jnp.where(allowed[:, None, None, :], suffix_scores, NEGATIVE)
    slab_rows = prefix_keys.shape[1]
    score_init = jnp.full((GROUPS, tok_dev, kv_heads, per_kv, slab_rows), NEGATIVE, jnp.float32)
    value_init = jnp.zeros((GROUPS, slab_rows, kv_heads, HD), prefix_values.dtype)

    def one_group(group_id, carry):
        score_stack, value_stack = carry
        holder = lax.dynamic_index_in_dim(owners, group_id, 0, keepdims=False)
        slab_keys, slab_values = (
            spread(prefix_keys[0], "gx", holder),
            spread(prefix_values[0], "gx", holder),
        )
        slab_keys = slab_keys.reshape(-1, kv_heads, HD)
        group_scores = (
            jnp.einsum(
                "tcqd,pcd->tcqp", query_blocks, slab_keys, preferred_element_type=jnp.float32
            )
            * scaling
        )
        masked = jnp.where((group_ids == group_id)[:, None, None, None], group_scores, NEGATIVE)
        score_stack = lax.dynamic_update_index_in_dim(score_stack, masked, group_id, 0)
        value_stack = lax.dynamic_update_index_in_dim(
            value_stack, slab_values.reshape(-1, kv_heads, HD), group_id, 0
        )
        return (score_stack, value_stack)

    score_stack, value_stack = lax.fori_loop(0, GROUPS, one_group, (score_init, value_init))
    prefix_scores = jnp.moveaxis(score_stack, 0, 3).reshape(
        tok_dev, kv_heads, per_kv, GROUPS * slab_rows
    )
    all_scores = jnp.concatenate([suffix_masked, prefix_scores], axis=3)
    all_values = jnp.concatenate(
        [suffix_v, value_stack.reshape(GROUPS * slab_rows, kv_heads, HD)], axis=0
    ).astype(jnp.float32)
    local_max = jnp.max(all_scores, axis=3)
    probs = jnp.exp(all_scores - local_max[..., None])
    local_total = jnp.sum(probs, axis=3)
    local_acc = jnp.einsum("tcqp,pcd->tcqd", probs, all_values, precision=highest)
    merged_max, merged_total, merged_acc = combined_all(
        (local_max, local_total, local_acc), "gy", combine_parts
    )
    attention = (merged_acc / merged_total[..., None]).reshape(tok_dev, -1).astype(jnp.bfloat16)
    resid = (
        stream_in.astype(jnp.float32)
        + jnp.dot(attention, out_proj, preferred_element_type=jnp.float32)
    ).astype(jnp.bfloat16)
    resid_all = lax.all_gather(resid, "gx", axis=0, tiled=True)
    resid_all_f = resid_all.astype(jnp.float32)
    scaled_all = (resid_all_f * norm_gain[None, :]).astype(jnp.bfloat16)
    squares_all = jnp.sum(resid_all_f * resid_all_f, axis=1)
    tokens = resid_all.shape[0]
    experts = w_gate.shape[0]
    width = w_gate.shape[2]
    top_count = routes.shape[1]
    capacity = tokens * 3 // 8
    flat_routes = routes.reshape(-1)
    onehot = (flat_routes[:, None] == jnp.arange(experts, dtype=jnp.int32)[None, :]).astype(
        jnp.int32
    )
    earlier = jnp.cumsum(onehot, axis=0) - onehot
    position = jnp.sum(earlier * onehot, axis=1)
    slot_of_pair = flat_routes * capacity + position
    pair_token = jnp.arange(flat_routes.shape[0], dtype=jnp.int32) // top_count
    matches = slot_of_pair[:, None] == jnp.arange(experts * capacity, dtype=jnp.int32)[None, :]
    slot_token = jnp.sum(jnp.where(matches, pair_token[:, None], 0), axis=0)
    pair_weight = jax.nn.softmax(route_logits, axis=1)
    slot_pairs = slot_of_pair.reshape(tokens, top_count)
    rows_in = jnp.take(scaled_all, slot_token, axis=0).reshape(experts, capacity, -1)
    squares_in = jnp.take(squares_all, slot_token)
    gate_part = jnp.einsum(
        "ecd,edf->ecf", rows_in, w_gate, preferred_element_type=jnp.float32
    ).reshape(experts * capacity, width)
    up_part = jnp.einsum("ecd,edf->ecf", rows_in, w_up, preferred_element_type=jnp.float32).reshape(
        experts * capacity, width
    )
    gate_sum, up_sum, square_sum = lax.psum((gate_part, up_part, squares_in), "gy")
    inverse = 1.0 / jnp.sqrt(square_sum / D + EPSILON)
    hidden = (jax.nn.silu(gate_sum * inverse[:, None]) * (up_sum * inverse[:, None])).astype(
        jnp.bfloat16
    )
    expert_rows = jnp.einsum(
        "ecf,efd->ecd",
        hidden.reshape(experts, capacity, width),
        w_down,
        preferred_element_type=jnp.float32,
    ).reshape(experts * capacity, -1)
    picked = jnp.take(expert_rows, slot_pairs, axis=0)
    expert_out = lax.psum_scatter(
        jnp.sum(picked * pair_weight[..., None], axis=1).astype(jnp.bfloat16),
        "gx",
        scatter_dimension=0,
        tiled=True,
    ).astype(jnp.float32)
    return (resid.astype(jnp.float32) + expert_out).astype(jnp.bfloat16)


def solution(mesh):
    placed = (
        P("gx", "gy"),
        P("gx", None),
        P("gx", None),
        P("gx", None),
        P("gx", "gy", None),
        P("gx", "gy", None),
        P("gx", None),
        P("gx", None),
        P(),
        P(None, "gy"),
        P("gy"),
        P(None, "gy", "gx"),
        P(None, "gy", "gx"),
        P(None, "gx", "gy"),
        P(),
        P(),
    )
    return jax.shard_map(body, mesh=mesh, in_specs=placed, out_specs=P("gx", "gy"), check_vma=False)
```

profile of v0, /device:TPU:0, one launch (start us, length us, event | category | flops | bytes accessed | tf_op | source)
XLA Modules:
  0.0 801.7 jit_solution(16958359620942076055)
XLA Ops:
  7.4 1.4 reshape.214
  8.8 1.0 copy.141
  9.9 0.8 reduce-window.18
  10.8 1.5 copy.142
  12.3 1.5 copy.144
  13.9 243.7 %while.31 = (s32[]{:T(128)}, f32[3,64,8,4,512]{4,1,3,2,0:T(8,128)}, bf16[3,512,8,128]{3,1,0,2:T(8,128)(2,1)}, s32[64]{0:T(128)S(1)}, s32[3]{0:T(128)S(1)}, /*ind...) while((s32[]{:T(128)}, f32[3,64,8,4,512]{4,1,3,2,0:T(8,128)}, ...), condition=%wide.region_7.8_spmd, body=%wide.region_4.7_spmd.sunk | while | flops 272629824 | bytes 28836440 | solution.py:112
  15.3 1.1 broadcast_select_fusion.6
  16.4 1.3 copy.208
  17.8 72.3 %all-reduce.9.cloned.1.call-done = (bf16[512,8,128]{2,0,1:T(8,128)(2,1)}, bf16[1,512,8,128]{1,3,2,0:T(8,128)(2,1)}) async-done(((bf16[512,8,128]{2,0,1:T(8,128)(2,1)}, bf16[1,512,8,128]{1,3,2,0:T(8,128)(2,1)}), (bf16[512,8,128]{2,0,1:T(8,128)(2,1)}, bf16[1,512,8,128]{1,3,2,0:T(8,128)(2,1)})) %all-reduce.9.cloned.1.call-update) | async-done | bytes 2097168 | tf_op jit(solution)/shard_map/while/body/eval_jaxpr/psum | solution.py:19
  90.1 1.6 copy.209
  91.7 1.2 constant_dynamic-update-slice_fusion.2
  93.0 4.0 bitcast_dynamic-update-slice_fusion.2
  98.3 1.1 broadcast_select_fusion.6
  99.4 1.3 copy.208
  100.8 69.6 %all-reduce.9.cloned.1.call-done = (bf16[512,8,128]{2,0,1:T(8,128)(2,1)}, bf16[1,512,8,128]{1,3,2,0:T(8,128)(2,1)}) async-done(((bf16[512,8,128]{2,0,1:T(8,128)(2,1)}, bf16[1,512,8,128]{1,3,2,0:T(8,128)(2,1)}), (bf16[512,8,128]{2,0,1:T(8,128)(2,1)}, bf16[1,512,8,128]{1,3,2,0:T(8,128)(2,1)})) %all-reduce.9.cloned.1.call-update) | async-done | bytes 2097168 | tf_op jit(solution)/shard_map/while/body/eval_jaxpr/psum | solution.py:19
  170.4 1.6 copy.209
  172.0 1.2 constant_dynamic-update-slice_fusion.2
  173.2 4.0 bitcast_dynamic-update-slice_fusion.2
  178.6 1.1 broadcast_select_fusion.6
  179.7 1.3 copy.208
  181.1 69.6 %all-reduce.9.cloned.1.call-done = (bf16[512,8,128]{2,0,1:T(8,128)(2,1)}, bf16[1,512,8,128]{1,3,2,0:T(8,128)(2,1)}) async-done(((bf16[512,8,128]{2,0,1:T(8,128)(2,1)}, bf16[1,512,8,128]{1,3,2,0:T(8,128)(2,1)}), (bf16[512,8,128]{2,0,1:T(8,128)(2,1)}, bf16[1,512,8,128]{1,3,2,0:T(8,128)(2,1)})) %all-reduce.9.cloned.1.call-update) | async-done | bytes 2097168 | tf_op jit(solution)/shard_map/while/body/eval_jaxpr/psum | solution.py:19
  250.7 1.6 copy.209
  252.3 1.2 constant_dynamic-update-slice_fusion.2
  253.5 4.0 bitcast_dynamic-update-slice_fusion.2
  257.6 5.3 bitcast_reduce_fusion
  263.7 18.0 %copy.148 = f32[64,8,4,3,512]{4,3,1,2,0:T(4,128)} copy(f32[64,8,4,3,512]{4,0,2,1,3:T(8,128)} %bitcast.101) | data formatting | bytes 25165824 | tf_op jit(solution)/shard_map/transpose | solution.py:113
  281.7 21.0 %reshape.215 = f32[64,8,4,1536]{3,1,2,0:T(8,128)} reshape(f32[64,8,4,3,512]{4,3,1,2,0:T(4,128)} %copy.148) | data formatting | bytes 25165824 | tf_op jit(solution)/shard_map/reshape | solution.py:113
  303.3 8.1 %fusion.39 = (f32[64,8,4]{1,2,0:T(4,128)S(1)}, f32[64,8,4,1600]{3,1,2,0:T(8,128)S(1)}) fusion(f32[64,8,4]{1,2,0:T(4,128)S(1)} %copy.147, f32[64,8,4,1536]{3,1,2,0:T(8,128)} %reshape.215, f32[64,8,4,64]{3,1,2,0:T(8,128)S(1)} %copy.149), kind=kLoop, calls=%fused_computation.91 | loop fusion | flops 9828352 | bytes 26230784 | tf_op jit(solution)/shard_map/reduce_sum | solution.py:122
  311.4 15.1 %fusion.10 = f32[64,8,4,128]{3,0,2,1:T(8,128)} fusion(f32[64,8,4,1600]{3,1,2,0:T(8,128)S(1)} %get-tuple-element.369, bf16[1536,8,128]{2,0,1:T(8,128)(2,1)S(1)} %bitcast.110, bf16[64,8,128]{2,0,1:T(8,128)(2,1)S(1)} %copy_bitcast_fusion.1), kind=kOutput, calls=%fused_computation.29 | convolution fusion | flops 5039718400 | bytes 17432576 | tf_op jit(solution)/shard_map/tcqp,pcd->tcqd/dot_general | solution.py:123
  326.6 19.6 %all-gather.1 = f32[512,8,4]{1,2,0:T(4,128)S(1)} all-gather(f32[64,8,4]{1,2,0:T(4,128)S(1)} %get-tuple-element.368), channel_id=3, replica_groups=mesh['gx'=4,'gy'=8] {'gy'}, dimensions={0}, use_global_device_ids=true | all-gather | bytes 73728 | tf_op jit(solution)/shard_map/all_gather | solution.py:23
  346.3 24.0 %all-gather = f32[512,8,4]{1,2,0:T(4,128)S(1)} all-gather(f32[64,8,4]{1,2,0:T(4,128)S(1)} %copy.147), channel_id=2, replica_groups=mesh['gx'=4,'gy'=8] {'gy'}, dimensions={0}, use_global_device_ids=true | all-gather | bytes 73728 | tf_op jit(solution)/shard_map/all_gather | solution.py:23
  371.6 1.2 reduce-window.19
  373.5 45.6 %all-gather.5.cloned.1.call-done = f32[512,8,4,128]{3,0,2,1:T(8,128)} async-done(((f32[64,8,4,128]{3,0,2,1:T(8,128)}), f32[512,8,4,128]{3,0,2,1:T(8,128)}) %all-gather.5.cloned.1.call-update) | async-done | bytes 8388624 | tf_op jit(solution)/shard_map/all_gather | solution.py:23
  419.1 1.3 slice.46
  421.1 6.9 slice.49
  428.0 28.2 %while.32 = (s32[]{:T(128)}, f32[64,8,4]{0,2,1:T(4,128)S(1)}, f32[64,8,4]{0,2,1:T(4,128)S(1)}, f32[64,8,4,128]{3,2,1,0:T(4,128)S(1)}, f32[7,64,8,4]{1,3,2,0:T(4,...) while((s32[]{:T(128)}, f32[64,8,4]{0,2,1:T(4,128)S(1)}, ...), condition=%wide.region_11.12_spmd, body=%wide.region_10.11_spmd.sunk | while | flops 798722 | bytes 5357661 | solution.py:26
  428.4 1.3 constant_dynamic-slice_fusion.2
  429.7 2.3 fusion.58
  432.4 1.3 constant_dynamic-slice_fusion.2
  433.7 2.3 fusion.58
  436.4 1.3 constant_dynamic-slice_fusion.2
  437.8 2.3 fusion.58
  440.4 1.3 constant_dynamic-slice_fusion.2
  441.8 2.3 fusion.58
  444.5 1.3 constant_dynamic-slice_fusion.2
  445.8 2.3 fusion.58
  448.5 1.3 constant_dynamic-slice_fusion.2
  449.8 2.3 fusion.58
  452.5 1.3 constant_dynamic-slice_fusion.2
  453.9 2.3 fusion.58
  457.5 3.0 fusion.15
  460.5 8.9 %all_gather.24 = bf16[256,512]{1,0:T(8,128)(2,1)S(1)} all-gather(bf16[64,512]{1,0:T(8,128)(2,1)S(1)} %fusion.15), channel_id=1, replica_groups=mesh['gx'=4,'gy'=8] {'gx'}, dimensions={0}, use_global_device_ids=true | all-gather | bytes 327680 | tf_op jit(solution)/shard_map/all_gather | solution.py:132
  469.6 2.9 gather_fusion
  472.5 11.2 %fusion.17 = f32[8,96,2048]{2,1,0:T(8,128)} fusion(bf16[8,512,2048]{2,1,0:T(8,128)(2,1)} %param.31, bf16[8,96,512]{2,1,0:T(8,128)(2,1)S(1)} %bitcast.106, pred[8,96]{1,0:T(8,128)(4,1)S(1)} %compare_and_fusion), kind=kOutput, calls=%fused_computation.39 | convolution fusion | flops 1611005952 | bytes 23855872 | tf_op jit(solution)/shard_map/ecd,edf->ecf/dot_general | solution.py:155
  483.8 11.2 %fusion.16 = f32[8,96,2048]{2,1,0:T(8,128)} fusion(bf16[8,512,2048]{2,1,0:T(8,128)(2,1)} %param.32, bf16[8,96,512]{2,1,0:T(8,128)(2,1)S(1)} %bitcast.107, pred[8,96]{1,0:T(8,128)(4,1)S(1)} %compare_and_fusion), kind=kOutput, calls=%fused_computation.38 | convolution fusion | flops 1611005952 | bytes 23855872 | tf_op jit(solution)/shard_map/ecd,edf->ecf/dot_general | solution.py:158
  496.0 5.0 gather_fusion.1
  501.0 14.4 %psum.50 = f32[768]{0:T(1024)S(1)} all-reduce(f32[768]{0:T(1024)S(1)} %and_select_fusion), channel_id=1, replica_groups=mesh['gx'=4,'gy'=8] {'gy'}, use_global_device_ids=true, to_apply=%region_18.19 | all-reduce | flops 768 | bytes 6144 | tf_op jit(solution)/shard_map/psum | solution.py:161
  515.5 232.6 %all-reduce.7.cloned.1.call-done = (f32[768,2048]{1,0:T(8,128)}, f32[768,2048]{1,0:T(8,128)}) async-done(((f32[768,2048]{1,0:T(8,128)}, f32[768,2048]{1,0:T(8,128)}), (f32[768,2048]{1,0:T(8,128)}, f32[768,2048]{1,0:T(8,128)})) %all-reduce.7.cloned.1.call-update) | async-done | bytes 12582928 | tf_op jit(solution)/shard_map/psum | solution.py:161
  748.1 6.0 multiply_convert_fusion
  754.1 8.5 %fusion.42 = f32[8,96,512]{2,1,0:T(8,128)S(1)} fusion(bf16[8,96,2048]{2,1,0:T(8,128)(2,1)S(1)} %bitcast.105, bf16[8,2048,512]{2,1,0:T(8,128)(2,1)} %param.33), kind=kOutput, calls=%fused_computation.93 | convolution fusion | flops 1610612736 | bytes 21495808 | tf_op jit(solution)/shard_map/ecf,efd->ecd/dot_general | solution.py:166
  762.7 1.6 gather_fusion.2
  764.9 2.8 multiply_reduce_fusion
  767.8 24.6 %reduce-scatter.2.cloned.1.call-done = bf16[64,512]{1,0:T(8,128)(2,1)} async-done(((bf16[256,512]{1,0:T(8,128)(2,1)}), bf16[64,512]{1,0:T(8,128)(2,1)}) %reduce-scatter.2.cloned.1.call-update) | async-done | bytes 65552 | tf_op jit(solution)/shard_map/reduce_scatter | solution.py:173
  792.4 1.5 add_convert_fusion
  (115 shorter events, 12.2 us)
Async XLA Ops:
  7.4 295.9 %copy-start = (bf16[64,1024]{1,0:T(8,128)(2,1)S(1)}, bf16[64,1024]{1,0:T(8,128)(2,1)}, u32[]{:S(2)}) copy-start(bf16[64,1024]{1,0:T(8,128)(2,1)} %param.23) | copy-start | bytes 393220
  7.4 6.4 copy-start.10
  7.4 6.5 copy-start.11
  8.8 1.9 copy-start.3
  13.9 76.2 %all-reduce.9.cloned.1.call-start = ((), (), s32[]{:S(2)}) async-start(), calls=%async_computation.4 | async-start | bytes 4194304 | tf_op jit(solution)/shard_map/while/body/eval_jaxpr/psum | solution.py:19
  97.0 73.5 %all-reduce.9.cloned.1.call-start = ((), (), s32[]{:S(2)}) async-start(), calls=%async_computation.4 | async-start | bytes 4194304 | tf_op jit(solution)/shard_map/while/body/eval_jaxpr/psum | solution.py:19
  177.2 73.5 %all-reduce.9.cloned.1.call-start = ((), (), s32[]{:S(2)}) async-start(), calls=%async_computation.4 | async-start | bytes 4194304 | tf_op jit(solution)/shard_map/while/body/eval_jaxpr/psum | solution.py:19
  257.6 161.5 %all-gather.5.cloned.1.call-start = ((), (), s32[]{:S(2)}) async-start(), calls=%async_computation.2 | async-start | bytes 9437184 | tf_op jit(solution)/shard_map/all_gather | solution.py:23
  257.6 5.4 copy-start.5
  257.6 5.4 copy-start.4
  303.3 8.1 %copy-start.2 = (bf16[3,512,8,128]{3,1,0,2:T(8,128)(2,1)S(1)}, bf16[3,512,8,128]{3,1,0,2:T(8,128)(2,1)}, u32[]{:S(2)}) copy-start(bf16[3,512,8,128]{3,1,0,2:T(8,128)(2,1)} %get-tuple-element.243) | copy-start | bytes 9437188
  326.5 43.9 %copy-start.8 = (s32[256,2]{0,1:T(2,128)S(1)}, s32[256,2]{0,1:T(2,128)}, u32[]{:S(2)}) copy-start(s32[256,2]{0,1:T(2,128)} %param.34) | copy-start | bytes 6148
  326.5 421.6 %all-reduce.7.cloned.1.call-start = ((), (), s32[]{:S(2)}) async-start(), calls=%async_computation.3 | async-start | bytes 25165824 | tf_op jit(solution)/shard_map/psum | solution.py:161
  428.0 29.5 %copy-start.6 = (bf16[64,512]{1,0:T(8,128)(2,1)S(1)}, bf16[64,512]{1,0:T(8,128)(2,1)}, u32[]{:S(2)}) copy-start(bf16[64,512]{1,0:T(8,128)(2,1)} %param.20) | copy-start | bytes 196612
  456.1 13.3 %copy-start.9 = (f32[512]{0:T(512)S(1)}, f32[512]{0:T(512)}, u32[]{:S(2)}) copy-start(f32[512]{0:T(512)} %param.30) | copy-start | bytes 6148
  495.0 0.8 copy-start.7
  495.0 297.4 %reduce-scatter.2.cloned.1.call-start = ((), (), s32[]{:S(2)}) async-start(), calls=%async_computation.1 | async-start | bytes 327680 | tf_op jit(solution)/shard_map/reduce_scatter | solution.py:173
  762.7 31.2 %copy-start.1 = (bf16[64,1024]{1,0:T(8,128)(2,1)S(1)}, bf16[64,1024]{1,0:T(8,128)(2,1)}, u32[]{:S(2)}) copy-start(bf16[64,1024]{1,0:T(8,128)(2,1)} %param.23) | copy-start | bytes 393220
Sparse Core Ops, SparseCore 0:
  17.9 72.1 all-reduce.8
  100.9 69.4 all-reduce.8
  181.2 69.4 all-reduce.8
Sparse Core Ops, SparseCore 1:
  326.6 92.4 all-gather.4
  495.1 252.9 all-reduce.6
  767.9 24.5 reduce-scatter.1
where the time goes:
time: 810 us; the launch traced here: 802 us
  waiting for transfers between devices  515 us (64%)
  local copies, waits for them, and re-layouts  93.5 us (12%)
  blocking collectives  67 us (8%)
  matrix products  61.7 us (8%)
  other arithmetic  46.8 us (6%)
  between operations  15.7 us (2%)
    psum x1, waiting for transfers between devices, body(): lax.psum((gate_part, up_part, squares_in), 'gy')  233 us
    psum x3, waiting for transfers between devices, spread(): return lax.psum(kept, axis)  212 us
    all_gather x1, waiting for transfers between devices, combined_all(): pieces = jax.tree.map(lambda part: lax.all_gather(part, axis), value)  45.6 us
    all_gather x2, blocking collectives, combined_all(): pieces = jax.tree.map(lambda part: lax.all_gather(part, axis), value)  43.6 us
    reduce_scatter x1, waiting for transfers between devices, body(): lax.psum_scatter(jnp.sum(picked * pair_weight[..., None], axis=1).astype(...  24.6 us
    reshape x1, local copies, waits for them, and re-layouts, body(): jnp.moveaxis(score_stack, 0, 3)  21 us
    transpose x1, local copies, waits for them, and re-layouts, body(): jnp.moveaxis(score_stack, 0, 3)  18 us
  transfers between devices with their start and end apart: 6, of which 6 were waited for; matrix products, arithmetic and copies ran while one was open for 1% of the time, Pallas kernels for 0%

commit v1 on v0

--- a/solution.py
+++ b/solution.py
@@ -3,11 +3,16 @@
 import jax
 import jax.numpy as jnp
 from jax import lax
+from jax.experimental import pallas as pl
+from jax.experimental.pallas import tpu as pltpu
 from jax.sharding import PartitionSpec as P
 
 D = 4096
 HD = 128
 GROUPS = 3
+LANES = 128
+ROWS = 8
+CHUNKS = 2
 
 
 NEGATIVE = -1e30
@@ -179,6 +184,507 @@
     return (resid.astype(jnp.float32) + expert_out).astype(jnp.bfloat16)
 
 
+def flip(value, axis, size, bit):
+    return lax.ppermute(value, axis, [(i, i ^ bit) for i in range(size)])
+
+
+def attend_kernel(core_ref, q_ref, k_own_ref, v_own_ref, k_far_ref, v_far_ref, out_ref):
+    head = pl.program_id(0)
+    per_kv = q_ref.shape[1] // HD
+    rows = q_ref.shape[0]
+    scaling = 1.0 / math.sqrt(HD)
+    q = jnp.concatenate([q_ref[:, j * HD : (j + 1) * HD] for j in range(per_kv)], axis=0)
+    contract = (((1,), (1,)), ((), ()))
+    near = lax.dot_general(q, k_own_ref[0], contract, preferred_element_type=jnp.float32)
+    far = lax.dot_general(q, k_far_ref[...], contract, preferred_element_type=jnp.float32)
+    top = jnp.maximum(
+        jnp.max(near, axis=1, keepdims=True), jnp.max(far, axis=1, keepdims=True)
+    )
+    factor = scaling * math.log2(math.e)
+    near = jnp.exp2((near - top) * factor)
+    far = jnp.exp2((far - top) * factor)
+    total = jnp.sum(near, axis=1, keepdims=True) + jnp.sum(far, axis=1, keepdims=True)
+    acc = jnp.dot(
+        near.astype(jnp.bfloat16), v_own_ref[0], preferred_element_type=jnp.float32
+    ) + jnp.dot(far.astype(jnp.bfloat16), v_far_ref[...], preferred_element_type=jnp.float32)
+    acc = acc / total
+    lse = top * scaling + jnp.log(total)
+    lanes = lax.broadcasted_iota(jnp.int32, (rows, LANES), 1)
+    heads = pl.num_programs(0) * per_kv
+    stats = jnp.zeros((rows, LANES), jnp.float32)
+    for j in range(per_kv):
+        part = lse[j * rows : (j + 1) * rows]
+        high = part.astype(jnp.bfloat16).astype(jnp.float32)
+        middle = (part - high).astype(jnp.bfloat16).astype(jnp.float32)
+        low = part - high - middle
+        place = head * per_kv + j
+        stats = jnp.where(lanes == place, high, stats)
+        stats = jnp.where(lanes == heads + place, middle, stats)
+        stats = jnp.where(lanes == 2 * heads + place, low, stats)
+        where = pl.multiple_of((head * per_kv + j) * HD, HD)
+        out_ref[:, pl.ds(where, HD)] = acc[j * rows : (j + 1) * rows].astype(jnp.bfloat16)
+    width = out_ref.shape[1] - LANES
+
+    @pl.when(head == 0)
+    def _():
+        out_ref[:, width:] = stats.astype(jnp.bfloat16)
+
+    @pl.when(head > 0)
+    def _():
+        out_ref[:, width:] = (out_ref[:, width:].astype(jnp.float32) + stats).astype(jnp.bfloat16)
+
+
+def attend(core, q, keys, values, far):
+    rows, width = q.shape
+    slab = keys.shape[1]
+    heads = far.shape[1] // 2 // HD
+    span = width // heads
+    return pl.pallas_call(
+        attend_kernel,
+        grid_spec=pltpu.PrefetchScalarGridSpec(
+            num_scalar_prefetch=1,
+            grid=(heads,),
+            in_specs=[
+                pl.BlockSpec((rows, span), lambda h, s: (0, h)),
+                pl.BlockSpec((1, slab, HD), lambda h, s: (0, 0, s[0] * heads + h)),
+                pl.BlockSpec((1, slab, HD), lambda h, s: (0, 0, s[0] * heads + h)),
+                pl.BlockSpec((slab, HD), lambda h, s: (0, h)),
+                pl.BlockSpec((slab, HD), lambda h, s: (0, heads + h)),
+            ],
+            out_specs=pl.BlockSpec((rows, width + LANES), lambda h, s: (0, 0)),
+        ),
+        out_shape=jax.ShapeDtypeStruct((rows, width + LANES), jnp.bfloat16),
+        name="attend",
+    )(core, q, keys, values, far, far)
+
+
+def choose_kernel(z_ref, pick_ref, a_ref, b_ref, c_ref, d_ref, *outs):
+    pick = pick_ref[...]
+    width = a_ref.shape[1] - LANES
+    span = outs[0].shape[1] - LANES
+
+    def chosen(where, size):
+        first = jnp.where(pick == 1, b_ref[:, where].astype(jnp.float32), a_ref[:, where].astype(jnp.float32))
+        second = jnp.where(pick == 3, d_ref[:, where].astype(jnp.float32), c_ref[:, where].astype(jnp.float32))
+        return jnp.where(pick >= 2, second, first).astype(jnp.bfloat16)
+
+    stats = chosen(pl.ds(width, LANES), LANES)
+    for s, out in enumerate(outs):
+        start = pl.multiple_of((z_ref[0] ^ s) * span, LANES)
+        out[:, :span] = chosen(pl.ds(start, span), span)
+        out[:, span:] = stats
+
+
+def choose(z, pick, pieces, count):
+    rows, width = pieces[0].shape
+    span = (width - LANES) // count
+    shape = jax.ShapeDtypeStruct((rows, span + LANES), jnp.bfloat16)
+    whole = pl.BlockSpec((rows, width), lambda i, s: (0, 0))
+    return pl.pallas_call(
+        choose_kernel,
+        grid_spec=pltpu.PrefetchScalarGridSpec(
+            num_scalar_prefetch=1,
+            grid=(1,),
+            in_specs=[pl.BlockSpec((rows, 1), lambda i, s: (0, 0))] + [whole] * 4,
+            out_specs=[pl.BlockSpec((rows, span + LANES), lambda i, s: (0, 0))] * count,
+        ),
+        out_shape=[shape] * count,
+        name="choose",
+    )(z, pick, *pieces)
+
+
+def merge_kernel(place_ref, mask_ref, q_ref, k_ref, v_ref, *refs):
+    pieces, out_ref = refs[:-1], refs[-1]
+    per_kv = q_ref.shape[1] // HD
+    heads = per_kv * len(pieces)
+    scaling = 1.0 / math.sqrt(HD)
+    allowed = mask_ref[...] > 0
+    lanes = lax.broadcasted_iota(jnp.int32, (q_ref.shape[0], LANES), 1)
+    stats = [piece[:, per_kv * HD :].astype(jnp.float32) for piece in pieces]
+    for j in range(per_kv):
+        cols = slice(j * HD, (j + 1) * HD)
+        scores = (
+            lax.dot_general(
+                q_ref[:, cols],
+                k_ref[...],
+                (((1,), (1,)), ((), ())),
+                preferred_element_type=jnp.float32,
+            )
+            * scaling
+        )
+        scores = jnp.where(allowed, scores, NEGATIVE)
+        top = jnp.max(scores, axis=1, keepdims=True)
+        probs = jnp.exp(scores - top)
+        base = place_ref[1] * per_kv + j
+        mine = (lanes == base) | (lanes == heads + base) | (lanes == 2 * heads + base)
+        sizes = [jnp.sum(jnp.where(mine, part, 0.0), axis=1, keepdims=True) for part in stats]
+        peak = top
+        for size in sizes:
+            peak = jnp.maximum(peak, size)
+        share = jnp.exp(top - peak)
+        total = jnp.sum(probs, axis=1, keepdims=True) * share
+        acc = (
+            jnp.dot(probs.astype(jnp.bfloat16), v_ref[...], preferred_element_type=jnp.float32)
+            * share
+        )
+        for size, piece in zip(sizes, pieces):
+            weight = jnp.exp(size - peak)
+            total = total + weight
+            acc = acc + weight * piece[:, cols].astype(jnp.float32)
+        out_ref[:, cols] = (acc / total).astype(jnp.bfloat16)
+
+
+def merge(place, mask, queries, suffix_keys, suffix_values, pieces):
+    rows = queries.shape[0]
+    span = pieces[0].shape[1] - LANES
+    piece = pl.BlockSpec((rows, span + LANES), lambda i, s: (0, 0))
+    return pl.pallas_call(
+        merge_kernel,
+        grid_spec=pltpu.PrefetchScalarGridSpec(
+            num_scalar_prefetch=1,
+            grid=(1,),
+            in_specs=[
+                pl.BlockSpec((rows, rows), lambda i, s: (0, 0)),
+                pl.BlockSpec((rows, span), lambda i, s: (0, s[0])),
+                pl.BlockSpec((rows, HD), lambda i, s: (0, s[0])),
+                pl.BlockSpec((rows, HD), lambda i, s: (0, s[0])),
+            ]
+            + [piece] * len(pieces),
+            out_specs=pl.BlockSpec((rows, span), lambda i, s: (0, 0)),
+        ),
+        out_shape=jax.ShapeDtypeStruct((rows, span), jnp.bfloat16),
+        name="merge",
+    )(place, mask, queries, suffix_keys, suffix_values, *pieces)
+
+
+def project_kernel(order_ref, stream_ref, weight_ref, *refs):
+    pieces, out_ref, acc_ref = refs[:-2], refs[-2], refs[-1]
+    step = pl.program_id(0)
+
+    @pl.when(step == 0)
+    def _():
+        acc_ref[...] = stream_ref[...].astype(jnp.float32)
+
+    for k, piece in enumerate(pieces):
+
+        @pl.when(step == k)
+        def _(piece=piece):
+            acc_ref[...] += jnp.dot(
+                piece[...], weight_ref[...], preferred_element_type=jnp.float32
+            )
+
+    @pl.when(step == len(pieces) - 1)
+    def _():
+        out_ref[...] = acc_ref[...].astype(jnp.bfloat16)
+
+
+def project(order, stream, weight, pieces):
+    rows, width = stream.shape
+    span = pieces[0].shape[1]
+    return pl.pallas_call(
+        project_kernel,
+        grid_spec=pltpu.PrefetchScalarGridSpec(
+            num_scalar_prefetch=1,
+            grid=(len(pieces),),
+            in_specs=[
+                pl.BlockSpec((rows, width), lambda i, s: (0, 0)),
+                pl.BlockSpec((span, width), lambda i, s: (s[i], 0)),
+            ]
+            + [pl.BlockSpec((rows, span), lambda i, s: (0, 0))] * len(pieces),
+            out_specs=pl.BlockSpec((rows, width), lambda i, s: (0, 0)),
+            scratch_shapes=[pltpu.VMEM((rows, width), jnp.float32)],
+        ),
+        out_shape=jax.ShapeDtypeStruct((rows, width), jnp.bfloat16),
+        name="project",
+    )(order, stream, weight, *pieces)
+
+
+def widen_kernel(table_ref, rows_ref, gate_ref, up_ref, out_ref, acc_ref):
+    expert = pl.program_id(0)
+    capacity = rows_ref.shape[1]
+    width = gate_ref.shape[2]
+    here = pl.ds(pl.multiple_of(table_ref[1 + expert], ROWS), capacity)
+
+    @pl.when(expert == 0)
+    def _():
+        acc_ref[...] = jnp.zeros(acc_ref.shape, jnp.float32)
+
+    acc_ref[here, :width] = jnp.dot(
+        rows_ref[0], gate_ref[0], preferred_element_type=jnp.float32
+    )
+    acc_ref[here, width:] = jnp.dot(rows_ref[0], up_ref[0], preferred_element_type=jnp.float32)
+
+    @pl.when(expert == pl.num_programs(0) - 1)
+    def _():
+        out_ref[...] = acc_ref[: out_ref.shape[0], :].astype(jnp.bfloat16)
+
+
+def widen(table, rows_in, w_gate, w_up, parts, slots):
+    experts, capacity, depth = rows_in.shape
+    width = w_gate.shape[2] // parts
+    weight = pl.BlockSpec((1, depth, width), lambda e, s: (e, 0, s[0]))
+    return pl.pallas_call(
+        widen_kernel,
+        grid_spec=pltpu.PrefetchScalarGridSpec(
+            num_scalar_prefetch=1,
+            grid=(experts,),
+            in_specs=[
+                pl.BlockSpec((1, capacity, depth), lambda e, s: (e, 0, 0)),
+                weight,
+                weight,
+            ],
+            out_specs=pl.BlockSpec((slots, 2 * width), lambda e, s: (0, 0)),
+            scratch_shapes=[pltpu.VMEM((slots + capacity, 2 * width), jnp.float32)],
+        ),
+        out_shape=jax.ShapeDtypeStruct((slots, 2 * width), jnp.bfloat16),
+        name="widen",
+    )(table, rows_in, w_gate, w_up)
+
+
+def narrow_kernel(table_ref, own_ref, far_ref, near_w_ref, far_w_ref, pick_ref, scale_ref, init_ref, out_ref, own_f, far_f):
+    expert = pl.program_id(0)
+    slots = own_ref.shape[0]
+    capacity = pick_ref.shape[1]
+
+    @pl.when(expert == 0)
+    def _():
+        own_f[:slots, :] = own_ref[...].astype(jnp.float32)
+        far_f[:slots, :] = far_ref[...].astype(jnp.float32)
+        own_f[slots:, :] = jnp.zeros((capacity, own_f.shape[1]), jnp.float32)
+        far_f[slots:, :] = jnp.zeros((capacity, far_f.shape[1]), jnp.float32)
+        out_ref[...] = init_ref[...]
+
+    here = pl.ds(pl.multiple_of(table_ref[2 + expert], ROWS), capacity)
+    rows = jnp.dot(
+        own_f[here, :].astype(jnp.bfloat16), near_w_ref[0], preferred_element_type=jnp.float32
+    ) + jnp.dot(
+        far_f[here, :].astype(jnp.bfloat16), far_w_ref[0], preferred_element_type=jnp.float32
+    )
+    rows = (rows * scale_ref[0]).astype(jnp.bfloat16)
+    out_ref[...] += lax.dot_general(
+        pick_ref[0], rows, (((0,), (0,)), ((), ())), preferred_element_type=jnp.float32
+    )
+
+
+def narrow(table, own, far, w_down, pick, scale, init):
+    slots, width = own.shape
+    experts, capacity, tokens = pick.shape
+    cols = w_down.shape[2]
+    return pl.pallas_call(
+        narrow_kernel,
+        grid_spec=pltpu.PrefetchScalarGridSpec(
+            num_scalar_prefetch=1,
+            grid=(experts,),
+            in_specs=[
+                pl.BlockSpec((slots, width), lambda e, s: (0, 0)),
+                pl.BlockSpec((slots, width), lambda e, s: (0, 0)),
+                pl.BlockSpec((1, width, cols), lambda e, s: (e, s[0], 0)),
+                pl.BlockSpec((1, width, cols), lambda e, s: (e, s[1], 0)),
+                pl.BlockSpec((1, capacity, tokens), lambda e, s: (e, 0, 0)),
+                pl.BlockSpec((1, capacity, 1), lambda e, s: (e, 0, 0)),
+                pl.BlockSpec((tokens, cols), lambda e, s: (0, 0)),
+            ],
+            out_specs=pl.BlockSpec((tokens, cols), lambda e, s: (0, 0)),
+            scratch_shapes=[
+                pltpu.VMEM((slots + capacity, width), jnp.float32),
+                pltpu.VMEM((slots + capacity, width), jnp.float32),
+            ],
+        ),
+        out_shape=jax.ShapeDtypeStruct((tokens, cols), jnp.float32),
+        name="narrow",
+    )(table, own, far, w_down, w_down, pick, scale, init)
+
+
+def take_block(value, index, size, axis):
+    return lax.dynamic_slice_in_dim(value, index * size, size, axis)
+
+
+def square_body(
+    stream_in,
+    queries,
+    suffix_keys,
+    suffix_values,
+    prefix_keys,
+    prefix_values,
+    lengths,
+    req_group,
+    owners,
+    out_proj,
+    norm_gain,
+    w_gate,
+    w_up,
+    w_down,
+    routes,
+    route_logits,
+):
+    n_gx, n_gy = 4, 8
+    gx_index = lax.axis_index("gx")
+    gy_index = lax.axis_index("gy")
+    z_index = gy_index // 2
+    core = gy_index % 2
+    levels = n_gy // 2
+    tok_dev = queries.shape[0]
+    half_q = queries.shape[1] // 2
+    half_kv = prefix_keys.shape[2] // 2
+    i32 = jnp.int32
+    as_vector = lambda *items: jnp.stack([jnp.asarray(item, i32) for item in items])
+
+    mine_q = take_block(queries, core, half_q, 1)
+    far_kv = flip(
+        jnp.concatenate(
+            [
+                take_block(prefix_keys[0], 1 - core, half_kv, 1),
+                take_block(prefix_values[0], 1 - core, half_kv, 1),
+            ],
+            axis=1,
+        ),
+        "gy",
+        n_gy,
+        1,
+    )
+    all_q = [mine_q] + [flip(mine_q, "gx", n_gx, b) for b in range(1, n_gx)]
+    core_vec = as_vector(core)
+    partial = [attend(core_vec, q, prefix_keys, prefix_values, far_kv) for q in all_q]
+    pieces = [partial[0]] + [flip(partial[b], "gx", n_gx, b) for b in range(1, n_gx)]
+
+    places = jnp.arange(tok_dev, dtype=i32)
+    lens = lengths[0]
+    ends = jnp.sum(
+        jnp.where(jnp.arange(lens.shape[0])[:, None] >= jnp.arange(lens.shape[0])[None, :], lens[None, :], 0),
+        axis=1,
+    )
+    requests = jnp.sum((ends[None, :] <= places[:, None]).astype(i32), axis=1)
+    holders = jnp.sum(
+        jnp.where(req_group[0][:, None] == jnp.arange(GROUPS, dtype=i32)[None, :], owners[None, :], 0),
+        axis=1,
+    )
+    holder = jnp.sum(
+        jnp.where(requests[:, None] == jnp.arange(lens.shape[0], dtype=i32)[None, :], holders[None, :], 0),
+        axis=1,
+    )
+    pick = (holder ^ gx_index)[:, None]
+    allowed = (
+        (requests[:, None] == requests[None, :]) & (places[None, :] <= places[:, None])
+    ).astype(jnp.float32)
+
+    chosen = choose(as_vector(z_index), pick, pieces, levels)
+    shares = [chosen[0]] + [flip(chosen[s], "gy", n_gy, 2 * s) for s in range(1, levels)]
+    block = core * levels + z_index
+    heads = merge(
+        as_vector(block, z_index), allowed, queries, suffix_keys, suffix_values, shares
+    )
+    near = [heads] + [flip(heads, "gy", n_gy, 2 * s) for s in range(1, levels)]
+    far = flip(jnp.concatenate(near, axis=1), "gy", n_gy, 1)
+    span = heads.shape[1]
+    features = near + [far[:, s * span : (s + 1) * span] for s in range(levels)]
+    order = as_vector(
+        *[core * levels + (z_index ^ s) for s in range(levels)],
+        *[(1 - core) * levels + (z_index ^ s) for s in range(levels)],
+    )
+    resid = project(order, stream_in, out_proj, features)
+
+    tokens = n_gx * tok_dev
+    experts = w_gate.shape[0]
+    capacity = tokens * 3 // 8
+    slots = routes.shape[0] * routes.shape[1] + experts * ROWS
+    relative = lambda table: jnp.concatenate(
+        [take_block(table, gx_index ^ b, tok_dev, 0) for b in range(n_gx)], axis=0
+    )
+    routes_rel = relative(routes)
+    weights_rel = jax.nn.softmax(relative(route_logits), axis=1)
+    named = routes_rel[:, :, None] == jnp.arange(experts, dtype=i32)[None, None, :]
+    hits = jnp.sum(named.astype(jnp.float32), axis=1)
+    weight_of = jnp.sum(jnp.where(named, weights_rel[:, :, None], 0.0), axis=1)
+    steps = jnp.arange(tokens, dtype=i32)
+    before = (steps[:, None] > steps[None, :]).astype(jnp.bfloat16)
+    position = jnp.dot(
+        before, hits.astype(jnp.bfloat16), preferred_element_type=jnp.float32
+    ).astype(i32)
+    counts = jnp.sum(hits, axis=0).astype(i32)
+    kinds = jnp.arange(experts, dtype=i32)
+    padded = (counts + ROWS - 1) // ROWS * ROWS
+    starts = jnp.sum(jnp.where(kinds[:, None] > kinds[None, :], padded[None, :], 0), axis=1)
+    place_of = jnp.where(hits > 0, position, -1)
+    chosen_row = place_of.T[:, None, :] == jnp.arange(capacity, dtype=i32)[None, :, None]
+    row_pick = chosen_row.astype(jnp.bfloat16)
+    row_weight = jnp.sum(jnp.where(chosen_row, weight_of.T[:, None, :], 0.0), axis=2)[:, :, None]
+
+    all_resid = jnp.concatenate(
+        [resid] + [flip(resid, "gx", n_gx, b) for b in range(1, n_gx)], axis=0
+    ).astype(jnp.float32)
+    scaled = (all_resid * norm_gain[None, :]).astype(jnp.bfloat16)
+    squares = jnp.sum(all_resid * all_resid, axis=1).reshape(-1, LANES)
+    for bit in (1, 2, 4):
+        squares = squares + flip(squares, "gy", n_gy, bit)
+    rstd = 1.0 / jnp.sqrt(squares.reshape(-1) / D + EPSILON)
+    rows_in = (
+        jnp.dot(
+            row_pick.reshape(experts * capacity, tokens),
+            scaled,
+            preferred_element_type=jnp.float32,
+        )
+        .astype(jnp.bfloat16)
+        .reshape(experts, capacity, -1)
+    )
+
+    half_id = (z_index ^ (z_index >> 1)) & 1
+    low_id = z_index >> 1
+    quarter = half_id * 2 + low_id
+    row_ids = quarter * (slots // 4) + jnp.arange(slots // 4, dtype=i32)
+    slot_of = jnp.where(hits > 0, starts[None, :] + position, -1)
+    owner_mask = jnp.any(row_ids[:, None, None] == slot_of.T[None, :, :], axis=1)
+    row_rstd = jnp.sum(jnp.where(owner_mask, rstd[None, :], 0.0), axis=1, keepdims=True)
+
+    f32 = jnp.float32
+    parts = 2 * CHUNKS
+    rounded = lambda a, b: (a.astype(f32) + b.astype(f32)).astype(jnp.bfloat16)
+    sums = []
+    for chunk in range(CHUNKS):
+        outs = []
+        for side in (1 - core, core):
+            table = jnp.concatenate([as_vector(2 * chunk + side), starts])
+            outs.append(widen(table, rows_in, w_gate, w_up, parts, slots))
+        sums.append((outs[1], flip(outs[0], "gy", n_gy, 1)))
+    hidden = []
+    for keep, seen in sums:
+        part = rounded(keep, seen)
+        seen = flip(take_block(part, 1 - half_id, slots // 2, 0), "gy", n_gy, 2)
+        part = rounded(take_block(part, half_id, slots // 2, 0), seen)
+        seen = flip(take_block(part, 1 - low_id, slots // 4, 0), "gy", n_gy, 6)
+        part = take_block(part, low_id, slots // 4, 0).astype(f32) + seen.astype(f32)
+        width = part.shape[1] // 2
+        gate = part[:, :width] * row_rstd
+        up = part[:, width:] * row_rstd
+        hidden.append((jax.nn.silu(gate) * up).astype(jnp.bfloat16))
+    total = jnp.zeros((tokens, w_down.shape[2]), f32)
+    for chunk, part in enumerate(hidden):
+        seen = flip(part, "gy", n_gy, 6)
+        first = low_id == 0
+        part = jnp.concatenate([jnp.where(first, part, seen), jnp.where(first, seen, part)], axis=0)
+        seen = flip(part, "gy", n_gy, 2)
+        first = half_id == 0
+        part = jnp.concatenate([jnp.where(first, part, seen), jnp.where(first, seen, part)], axis=0)
+        seen = flip(part, "gy", n_gy, 1)
+        table = jnp.concatenate([as_vector(2 * chunk + core, 2 * chunk + 1 - core), starts])
+        total = narrow(table, part, seen, w_down, row_pick, row_weight, total)
+    total = total.astype(jnp.bfloat16)
+    back = [total[:tok_dev]] + [
+        flip(total[b * tok_dev : (b + 1) * tok_dev], "gx", n_gx, b) for b in range(1, n_gx)
+    ]
+    expert_out = sum(piece.astype(f32) for piece in back)
+    return (resid.astype(f32) + expert_out).astype(jnp.bfloat16)
+
+
+def fits(mesh, args):
+    queries, suffix_keys, prefix_keys = args[1], args[2], args[4]
+    return (
+        dict(mesh.shape) == {"gx": 4, "gy": 8}
+        and suffix_keys.shape[1] == 8 * HD
+        and queries.shape[1] % (8 * HD) == 0
+        and prefix_keys.shape[2] == 8 * HD
+    )
+
+
 def solution(mesh):
     placed = (
         P("gx", "gy"),
@@ -198,4 +704,11 @@
         P(),
         P(),
     )
-    return jax.shard_map(body, mesh=mesh, in_specs=placed, out_specs=P("gx", "gy"), check_vma=False)
+
+    def run(*args):
+        chosen = square_body if fits(mesh, args) else body
+        return jax.shard_map(
+            chosen, mesh=mesh, in_specs=placed, out_specs=P("gx", "gy"), check_vma=False
+        )(*args)
+
+    return run

time: 810 us -> 241 us (0.30)
  waiting for transfers between devices: 515 us -> 75 us
  Pallas kernels: 0 us -> 88.3 us
  local copies, waits for them, and re-layouts: 93.5 us -> 12.9 us
  blocking collectives: 67 us -> 0 us
  matrix products: 61.7 us -> 2.31 us
  starting transfers between devices: 0.14 us -> 48.1 us
  other arithmetic: 46.8 us -> 12.3 us
  between operations: 15.7 us -> 0.54 us
    psum x4 -> x0, waiting for transfers between devices: 444 us -> none  [the longest x1 233 us: body(): lax.psum((gate_part, up_part, squares_in), 'gy')]
    pallas_call x0 -> x13, Pallas kernels: none -> 88.3 us  [the longest x4 35.2 us: widen(): pl.pallas_call(widen_kernel, grid_spec=pltpu.PrefetchScalarGridSpec(num_s...]
    ppermute x0 -> x35, waiting for transfers between devices: none -> 75 us  [flip(): return lax.ppermute(value, axis, [(i, i ^ bit) for i in range(size)])]
    dot_general x9 -> x2, matrix products: 61.7 us -> 2.31 us  [the longest x1 2.14 us: square_body(): jnp.dot(row_pick.reshape(experts * capacity, tokens), scaled, preferred_e...]
    all_gather x3 -> x0, blocking collectives: 52.6 us -> none  [the longest x2 43.6 us: combined_all(): pieces = jax.tree.map(lambda part: lax.all_gather(part, axis), value)]
    ppermute x0 -> x35, starting transfers between devices: none -> 48.1 us  [flip(): return lax.ppermute(value, axis, [(i, i ^ bit) for i in range(size)])]
    all_gather x1 -> x0, waiting for transfers between devices: 45.6 us -> none  [combined_all(): pieces = jax.tree.map(lambda part: lax.all_gather(part, axis), value)]
    reshape x7 -> x0, local copies, waits for them, and re-layouts: 27.4 us -> none  [the longest x1 21 us: body(): jnp.moveaxis(score_stack, 0, 3)]
  transfers between devices with their start and end apart: 6 -> 35, of which waited for: 6 -> 21; matrix products, arithmetic and copies ran while one was open for 1% -> 6% of each run, Pallas kernels for 0% -> 24%
where the time goes in v1:
time: 241 us; the launch traced here: 239 us
  Pallas kernels  88.3 us (37%)
  waiting for transfers between devices  75 us (31%)
  starting transfers between devices  48.1 us (20%)
  local copies, waits for them, and re-layouts  12.9 us (5%)
  other arithmetic  12.3 us (5%)
    ppermute x35, waiting for transfers between devices, flip(): return lax.ppermute(value, axis, [(i, i ^ bit) for i in range(size)])  75 us
    ppermute x35, starting transfers between devices, flip(): return lax.ppermute(value, axis, [(i, i ^ bit) for i in range(size)])  48.1 us
    pallas_call x4, Pallas kernels, widen(): pl.pallas_call(widen_kernel, grid_spec=pltpu.PrefetchScalarGridSpec(num_s...  35.2 us
    pallas_call x2, Pallas kernels, narrow(): pl.pallas_call(narrow_kernel, grid_spec=pltpu.PrefetchScalarGridSpec(num_...  20.2 us
    pallas_call x4, Pallas kernels, attend(): pl.pallas_call(attend_kernel, grid_spec=pltpu.PrefetchScalarGridSpec(num_...  20.2 us
    pallas_call x1, Pallas kernels, project(): pl.pallas_call(project_kernel, grid_spec=pltpu.PrefetchScalarGridSpec(num...  6.98 us
    unnamed x66, local copies, waits for them, and re-layouts  6.31 us
  transfers between devices with their start and end apart: 35, of which 21 were waited for; matrix products, arithmetic and copies ran while one was open for 6% of the time, Pallas kernels for 24%

profile of v1, /device:TPU:0, one launch (start us, length us, event | category | flops | bytes accessed | tf_op | source)
XLA Modules:
  0.0 239.4 jit_solution(3781457525692829611)
XLA Ops:
  0.0 1.0 constant_dynamic-slice_fusion.12.q_ref
  1.0 3.1 %collective-permute-start.3 = (bf16[64,2048]{1,0:T(8,128)(2,1)S(1)}, bf16[64,2048]{1,0:T(8,128)(2,1)S(1)}, u32[]{:S(2)}, u32[]{:S(2)}) collective-permute-start(bf16[64,2048]{1,0:T(8,128)(2,1)S(1)} %constant_dynamic-slice_fusion.12.q_ref), channel_id=1, source_target_pairs={{0,16},{8,24},{16,0},{24,8},{1,17},{9,25},{17,1},{25,9},{2,18},{10... | collective-permute-start | bytes 786440 | tf_op jit(solution)/shard_map/ppermute | solution.py:188
  4.0 1.4 collective-permute-start.5
  5.6 1.3 dynamic-slice_bitcast_fusion
  8.5 7.4 %collective-permute-done.3.q_ref = bf16[64,2048]{1,0:T(8,128)(2,1)S(1)} collective-permute-done((bf16[64,2048]{1,0:T(8,128)(2,1)S(1)}, bf16[64,2048]{1,0:T(8,128)(2,1)S(1)}, u32[]{:S(2)}, u32[]{:S(2)}) %collective-permute-start.3) | collective-permute-done | bytes 262176 | tf_op jit(solution)/shard_map/ppermute | solution.py:188
  16.0 0.7 copy-done.18
  17.0 5.0 %attend.6 = bf16[64,2176]{1,0:T(8,128)(2,1)} custom-call(s32[1]{0:T(128)} %bitcast.12.core_ref, bf16[64,2048]{1,0:T(8,128)(2,1)} %copy-done.18, bf16[1,512,1024]{2,1,0:T(8,128)(2,1)} %k_own_ref.7, bf16[1,512,1024]{2,1,0:T(8,128)(2,1)} %v_own_ref.7, bf16[512,1024]{1,0:T(8,128)(2,1)} %copy-done, bf16[512,1024]{1,0:T(8,128)(2,1)} %copy-done), custom_call_target="tpu_custom_call" | custom-call | tf_op jit(solution)/shard_map/attend/pallas_call | solution.py:242
  22.1 1.7 collective-permute-start.4
  23.8 0.7 copy-done.17
  24.5 5.0 %attend.7 = bf16[64,2176]{1,0:T(8,128)(2,1)} custom-call(s32[1]{0:T(128)} %bitcast.12.core_ref, bf16[64,2048]{1,0:T(8,128)(2,1)} %copy-done.17, bf16[1,512,1024]{2,1,0:T(8,128)(2,1)} %k_own_ref.7, bf16[1,512,1024]{2,1,0:T(8,128)(2,1)} %v_own_ref.7, bf16[512,1024]{1,0:T(8,128)(2,1)} %copy-done, bf16[512,1024]{1,0:T(8,128)(2,1)} %copy-done), custom_call_target="tpu_custom_call" | custom-call | tf_op jit(solution)/shard_map/attend/pallas_call | solution.py:242
  29.6 1.4 collective-permute-start.6
  31.0 0.7 copy-done.16
  31.7 5.0 %attend.5 = bf16[64,2176]{1,0:T(8,128)(2,1)} custom-call(s32[1]{0:T(128)} %bitcast.12.core_ref, bf16[64,2048]{1,0:T(8,128)(2,1)} %copy-done.16, bf16[1,512,1024]{2,1,0:T(8,128)(2,1)} %k_own_ref.7, bf16[1,512,1024]{2,1,0:T(8,128)(2,1)} %v_own_ref.7, bf16[512,1024]{1,0:T(8,128)(2,1)} %copy-done, bf16[512,1024]{1,0:T(8,128)(2,1)} %copy-done), custom_call_target="tpu_custom_call" | custom-call | tf_op jit(solution)/shard_map/attend/pallas_call | solution.py:242
  37.1 0.7 copy.25.pick_ref
  38.5 5.1 %attend.4.a_ref = bf16[64,2176]{1,0:T(8,128)(2,1)} custom-call(s32[1]{0:T(128)} %bitcast.12.core_ref, bf16[64,2048]{1,0:T(8,128)(2,1)} %copy-done.5, bf16[1,512,1024]{2,1,0:T(8,128)(2,1)} %k_own_ref.7, bf16[1,512,1024]{2,1,0:T(8,128)(2,1)} %v_own_ref.7, bf16[512,1024]{1,0:T(8,128)(2,1)} %copy-done, bf16[512,1024]{1,0:T(8,128)(2,1)} %copy-done), custom_call_target="tpu_custom_call" | custom-call | tf_op jit(solution)/shard_map/attend/pallas_call | solution.py:242
  44.7 2.2 choose.1
  46.9 1.6 collective-permute-start.7
  48.5 2.6 %collective-permute-start.8 = (bf16[64,640]{1,0:T(8,128)(2,1)}, bf16[64,640]{1,0:T(8,128)(2,1)S(1)}, u32[]{:S(2)}, u32[]{:S(2)}) collective-permute-start(bf16[64,640]{1,0:T(8,128)(2,1)} %get-tuple-element.11), channel_id=1, source_target_pairs={{0,4},{1,5},{2,6},{3,7},{4,0},{5,1},{6,2},{7,3},{8,12},{9,13},{10,... | collective-permute-start | bytes 245768 | tf_op jit(solution)/shard_map/ppermute | solution.py:188
  51.9 3.9 %collective-permute-done.8.refs_2_ = bf16[64,640]{1,0:T(8,128)(2,1)S(1)} collective-permute-done((bf16[64,640]{1,0:T(8,128)(2,1)}, bf16[64,640]{1,0:T(8,128)(2,1)S(1)}, u32[]{:S(2)}, u32[]{:S(2)}) %collective-permute-start.8) | collective-permute-done | bytes 81952 | tf_op jit(solution)/shard_map/ppermute | solution.py:188
  55.8 1.8 collective-permute-done.9.refs_3_
  58.2 3.4 %merge.1.refs_0_ = bf16[64,512]{1,0:T(8,128)(2,1)} custom-call(s32[2]{0:T(128)} %pad_add_fusion.1.place_ref, f32[64,64]{1,0:T(8,128)} %fusion.10.mask_ref, bf16[64,4096]{1,0:T(8,128)(2,1)} %q_ref.1, bf16[64,1024]{1,0:T(8,128)(2,1)} %k_ref.1, bf16[64,1024]{1,0:T(8,128)(2,1)} %v_ref.1, bf16[64,640]{1,0:T(8,128)(2,1)} %get-tuple-element.9.refs_0_, ...), custom_call_target="tpu_custom_call" | custom-call | tf_op jit(solution)/shard_map/merge/pallas_call | solution.py:341
  61.6 1.8 collective-permute-start.11
  63.4 2.6 %collective-permute-start.12 = (bf16[64,512]{1,0:T(8,128)(2,1)}, bf16[64,512]{1,0:T(8,128)(2,1)S(1)}, u32[]{:S(2)}, u32[]{:S(2)}) collective-permute-start(bf16[64,512]{1,0:T(8,128)(2,1)} %merge.1.refs_0_), channel_id=1, source_target_pairs={{0,6},{1,7},{2,4},{3,5},{4,2},{5,3},{6,0},{7,1},{8,14},{9,15},{10,... | collective-permute-start | bytes 196616 | tf_op jit(solution)/shard_map/ppermute | solution.py:188
  66.2 0.9 collective-permute-done.11.refs_2_
  67.0 2.8 %collective-permute-done.12.refs_3_ = bf16[64,512]{1,0:T(8,128)(2,1)S(1)} collective-permute-done((bf16[64,512]{1,0:T(8,128)(2,1)}, bf16[64,512]{1,0:T(8,128)(2,1)S(1)}, u32[]{:S(2)}, u32[]{:S(2)}) %collective-permute-start.12) | collective-permute-done | bytes 65568 | tf_op jit(solution)/shard_map/ppermute | solution.py:188
  69.8 0.9 pad_maximum_fusion.5
  73.0 7.0 %project.1 = bf16[64,512]{1,0:T(8,128)(2,1)} custom-call(s32[8]{0:T(128)} %stack.60.order_ref, bf16[64,512]{1,0:T(8,128)(2,1)} %stream_ref.1, bf16[4096,512]{1,0:T(8,128)(2,1)} %weight_ref.1, bf16[64,512]{1,0:T(8,128)(2,1)} %merge.1.refs_0_, bf16[64,512]{1,0:T(8,128)(2,1)} %copy-done.13, bf16[64,512]{1,0:T(8,128)(2,1)} %copy-done.14, ...), custom_call_target="tpu_custom_call" | custom-call | tf_op jit(solution)/shard_map/project/pallas_call | solution.py:384
  80.0 1.5 collective-permute-start.14
  81.5 1.5 collective-permute-start.15
  84.5 1.5 collective-permute-done.15
  86.0 2.4 collective-permute-done.16
  88.4 2.1 convolution_convert_fusion
  90.5 8.7 %widen.5 = bf16[576,1024]{1,0:T(8,128)(2,1)} custom-call(s32[9]{0:T(128)} %get-tuple-element.46.table_ref, bf16[8,96,512]{2,1,0:T(8,128)(2,1)} %bitcast.36, bf16[8,512,2048]{2,1,0:T(8,128)(2,1)} %gate_ref.7, bf16[8,512,2048]{2,1,0:T(8,128)(2,1)} %up_ref.7), custom_call_target="tpu_custom_call" | custom-call | tf_op jit(solution)/shard_map/widen/pallas_call | solution.py:426
  99.3 8.9 %widen.7 = bf16[576,1024]{1,0:T(8,128)(2,1)} custom-call(s32[9]{0:T(128)} %get-tuple-element.47.table_ref, bf16[8,96,512]{2,1,0:T(8,128)(2,1)} %bitcast.37, bf16[8,512,2048]{2,1,0:T(8,128)(2,1)} %gate_ref.7, bf16[8,512,2048]{2,1,0:T(8,128)(2,1)} %up_ref.7), custom_call_target="tpu_custom_call" | custom-call | tf_op jit(solution)/shard_map/widen/pallas_call | solution.py:426
  108.9 1.1 compare_reduce_fusion
  110.0 1.4 collective-permute-done.20
  112.6 8.7 %widen.4 = bf16[576,1024]{1,0:T(8,128)(2,1)} custom-call(s32[9]{0:T(128)} %get-tuple-element.48.table_ref, bf16[8,96,512]{2,1,0:T(8,128)(2,1)} %bitcast.38, bf16[8,512,2048]{2,1,0:T(8,128)(2,1)} %gate_ref.7, bf16[8,512,2048]{2,1,0:T(8,128)(2,1)} %up_ref.7), custom_call_target="tpu_custom_call" | custom-call | tf_op jit(solution)/shard_map/widen/pallas_call | solution.py:426
  121.3 8.9 %widen.6 = bf16[576,1024]{1,0:T(8,128)(2,1)} custom-call(s32[9]{0:T(128)} %get-tuple-element.45.table_ref, bf16[8,96,512]{2,1,0:T(8,128)(2,1)} %bitcast.39, bf16[8,512,2048]{2,1,0:T(8,128)(2,1)} %gate_ref.7, bf16[8,512,2048]{2,1,0:T(8,128)(2,1)} %up_ref.7), custom_call_target="tpu_custom_call" | custom-call | tf_op jit(solution)/shard_map/widen/pallas_call | solution.py:426
  130.9 2.4 %collective-permute-start.22 = (f32[2,128]{1,0:T(2,128)S(1)}, f32[2,128]{1,0:T(2,128)S(1)}, u32[]{:S(2)}, u32[]{:S(2)}) collective-permute-start(f32[2,128]{1,0:T(2,128)S(1)} %fusion.20), channel_id=1, source_target_pairs={{0,4},{1,5},{2,6},{3,7},{4,0},{5,1},{6,2},{7,3},{8,12},{9,13},{10,... | collective-permute-start | bytes 3080 | tf_op jit(solution)/shard_map/ppermute | solution.py:188
  133.9 1.1 copy-done.1
  135.5 1.0 collective-permute-start.27
  136.5 13.6 %collective-permute-done.18 = bf16[288,1024]{1,0:T(8,128)(2,1)S(1)} collective-permute-done((bf16[288,1024]{1,0:T(8,128)(2,1)S(1)}, bf16[288,1024]{1,0:T(8,128)(2,1)S(1)}, u32[]{:S(2)}, u32[]{:S(2)}) %collective-permute-start.18) | collective-permute-done | bytes 589856 | tf_op jit(solution)/shard_map/ppermute | solution.py:188
  150.4 1.4 collective-permute-start.19
  151.7 11.0 %collective-permute-done.27 = bf16[288,1024]{1,0:T(8,128)(2,1)S(1)} collective-permute-done((bf16[288,1024]{1,0:T(8,128)(2,1)S(1)}, bf16[288,1024]{1,0:T(8,128)(2,1)S(1)}, u32[]{:S(2)}, u32[]{:S(2)}) %collective-permute-start.27) | collective-permute-done | bytes 589856 | tf_op jit(solution)/shard_map/ppermute | solution.py:188
  163.4 5.7 %collective-permute-done.19 = bf16[144,1024]{1,0:T(8,128)(2,1)S(1)} collective-permute-done((bf16[144,1024]{1,0:T(8,128)(2,1)S(1)}, bf16[144,1024]{1,0:T(8,128)(2,1)S(1)}, u32[]{:S(2)}, u32[]{:S(2)}) %collective-permute-start.19) | collective-permute-done | bytes 294944 | tf_op jit(solution)/shard_map/ppermute | solution.py:188
  169.2 5.1 %collective-permute-done.28 = bf16[144,1024]{1,0:T(8,128)(2,1)S(1)} collective-permute-done((bf16[144,1024]{1,0:T(8,128)(2,1)S(1)}, bf16[144,1024]{1,0:T(8,128)(2,1)S(1)}, u32[]{:S(2)}, u32[]{:S(2)}) %collective-permute-start.28) | collective-permute-done | bytes 294944 | tf_op jit(solution)/shard_map/ppermute | solution.py:188
  174.6 2.2 collective-permute-start.29
  176.8 1.7 collective-permute-start.23
  178.5 4.6 %collective-permute-done.29 = bf16[144,512]{1,0:T(8,128)(2,1)S(1)} collective-permute-done((bf16[144,512]{1,0:T(8,128)(2,1)S(1)}, bf16[144,512]{1,0:T(8,128)(2,1)S(1)}, u32[]{:S(2)}, u32[]{:S(2)}) %collective-permute-start.29) | collective-permute-done | bytes 147488 | tf_op jit(solution)/shard_map/ppermute | solution.py:188
  183.1 11.5 %collective-permute-start.30 = (bf16[288,512]{1,0:T(8,128)(2,1)S(1)}, bf16[288,512]{1,0:T(8,128)(2,1)S(1)}, u32[]{:S(2)}, u32[]{:S(2)}) collective-permute-start(bf16[288,512]{1,0:T(8,128)(2,1)S(1)} %pad_maximum_fusion.4), channel_id=1, source_target_pairs={{0,2},{1,3},{2,0},{3,1},{4,6},{5,7},{6,4},{7,5},{8,10},{9,11},{10,... | collective-permute-start | bytes 884744 | tf_op jit(solution)/shard_map/ppermute | solution.py:188
  194.6 2.1 collective-permute-start.24
  196.8 5.6 %collective-permute-done.30 = bf16[288,512]{1,0:T(8,128)(2,1)S(1)} collective-permute-done((bf16[288,512]{1,0:T(8,128)(2,1)S(1)}, bf16[288,512]{1,0:T(8,128)(2,1)S(1)}, u32[]{:S(2)}, u32[]{:S(2)}) %collective-permute-start.30) | collective-permute-done | bytes 294944 | tf_op jit(solution)/shard_map/ppermute | solution.py:188
  202.7 3.6 %collective-permute-done.24 = bf16[288,512]{1,0:T(8,128)(2,1)S(1)} collective-permute-done((bf16[288,512]{1,0:T(8,128)(2,1)S(1)}, bf16[288,512]{1,0:T(8,128)(2,1)S(1)}, u32[]{:S(2)}, u32[]{:S(2)}) %collective-permute-start.24) | collective-permute-done | bytes 294944 | tf_op jit(solution)/shard_map/ppermute | solution.py:188
  206.8 1.0 copy.27.scale_ref
  208.4 0.8 fusion.pick_ref
  209.2 1.0 broadcast_in_dim.147.init_ref
  210.3 10.1 %narrow.2.init_ref = f32[256,512]{1,0:T(8,128)} custom-call(s32[10]{0:T(128)} %get-tuple-element.49.table_ref, bf16[576,512]{1,0:T(8,128)(2,1)} %copy-done.3, bf16[576,512]{1,0:T(8,128)(2,1)} %copy-done.8, bf16[8,2048,512]{2,1,0:T(8,128)(2,1)} %far_w_ref.3, bf16[8,2048,512]{2,1,0:T(8,128)(2,1)} %far_w_ref.3, bf16[8,96,256]{2,1,0:T(8,128)(2,1)} %fusion.pick_ref, ...), custom_call_target="tpu_custom_call" | custom-call | tf_op jit(solution)/shard_map/narrow/pallas_call | solution.py:473
  220.4 0.8 copy-done.9
  221.2 10.1 %narrow.3 = f32[256,512]{1,0:T(8,128)} custom-call(s32[10]{0:T(128)} %get-tuple-element.50.table_ref, bf16[576,512]{1,0:T(8,128)(2,1)} %copy-done.4, bf16[576,512]{1,0:T(8,128)(2,1)} %copy-done.9, bf16[8,2048,512]{2,1,0:T(8,128)(2,1)} %far_w_ref.3, bf16[8,2048,512]{2,1,0:T(8,128)(2,1)} %far_w_ref.3, bf16[8,96,256]{2,1,0:T(8,128)(2,1)} %fusion.pick_ref, ...), custom_call_target="tpu_custom_call" | custom-call | tf_op jit(solution)/shard_map/narrow/pallas_call | solution.py:473
  231.4 1.1 convert_element_type.141
  233.6 2.5 %collective-permute-start.34 = (bf16[64,512]{1,0:T(8,128)(2,1)S(1)}, bf16[64,512]{1,0:T(8,128)(2,1)S(1)}, u32[]{:S(2)}, u32[]{:S(2)}) collective-permute-start(bf16[64,512]{1,0:T(8,128)(2,1)S(1)} %get-tuple-element.29), channel_id=1, source_target_pairs={{0,24},{8,16},{16,8},{24,0},{1,25},{9,17},{17,9},{25,1},{2,26},{10... | collective-permute-start | bytes 196616 | tf_op jit(solution)/shard_map/ppermute | solution.py:188
  236.0 1.0 collective-permute-done.32
  237.0 1.0 collective-permute-done.33
  238.0 0.7 collective-permute-done.34
  (149 shorter events, 17.7 us)
Async XLA Ops:
  1.0 6.1 %copy-start.5 = (bf16[64,2048]{1,0:T(8,128)(2,1)}, bf16[64,2048]{1,0:T(8,128)(2,1)S(1)}, u32[]{:S(2)}) copy-start(bf16[64,2048]{1,0:T(8,128)(2,1)S(1)} %constant_dynamic-slice_fusion.12.q_ref) | copy-start | bytes 786436
  1.0 15.0 %collective-permute-start.3 = (bf16[64,2048]{1,0:T(8,128)(2,1)S(1)}, bf16[64,2048]{1,0:T(8,128)(2,1)S(1)}, u32[]{:S(2)}, u32[]{:S(2)}) collective-permute-start(bf16[64,2048]{1,0:T(8,128)(2,1)S(1)} %constant_dynamic-slice_fusion.12.q_ref), channel_id=1, source_target_pairs={{0,16},{8,24},{16,0},{24,8},{1,17},{9,25},{17,1},{25,9},{2,18},{10... | collective-permute-start | bytes 786440 | tf_op jit(solution)/shard_map/ppermute | solution.py:188
  4.0 19.8 %collective-permute-start.5 = (bf16[64,2048]{1,0:T(8,128)(2,1)S(1)}, bf16[64,2048]{1,0:T(8,128)(2,1)S(1)}, u32[]{:S(2)}, u32[]{:S(2)}) collective-permute-start(bf16[64,2048]{1,0:T(8,128)(2,1)S(1)} %constant_dynamic-slice_fusion.12.q_ref), channel_id=1, source_target_pairs={{0,24},{8,16},{16,8},{24,0},{1,25},{9,17},{17,9},{25,1},{2,26},{10... | collective-permute-start | bytes 786440 | tf_op jit(solution)/shard_map/ppermute | solution.py:188
  5.5 25.5 %collective-permute-start.1 = (bf16[64,2048]{1,0:T(8,128)(2,1)S(1)}, bf16[64,2048]{1,0:T(8,128)(2,1)S(1)}, u32[]{:S(2)}, u32[]{:S(2)}) collective-permute-start(bf16[64,2048]{1,0:T(8,128)(2,1)S(1)} %constant_dynamic-slice_fusion.12.q_ref), channel_id=1, source_target_pairs={{0,8},{8,0},{16,24},{24,16},{1,9},{9,1},{17,25},{25,17},{2,10},{10... | collective-permute-start | bytes 786440 | tf_op jit(solution)/shard_map/ppermute | solution.py:188
  6.9 0.8 copy-start.24
  6.9 0.9 copy-start.25
  6.9 1.2 copy-start.31
  6.9 1.2 copy-start.32
  7.1 8.9 %collective-permute-start = (bf16[512,1024]{1,0:T(8,128)(2,1)S(1)}, bf16[512,1024]{1,0:T(8,128)(2,1)S(1)}, u32[]{:S(2)}, u32[]{:S(2)}) collective-permute-start(bf16[512,1024]{1,0:T(8,128)(2,1)S(1)} %pad_maximum_fusion), channel_id=1, source_target_pairs={{0,1},{1,0},{2,3},{3,2},{4,5},{5,4},{6,7},{7,6},{8,9},{9,8},{10,11... | collective-permute-start | bytes 3145736 | tf_op jit(solution)/shard_map/ppermute | solution.py:188
  16.0 1.1 copy-start
  22.1 21.5 %collective-permute-start.4 = (bf16[64,2176]{1,0:T(8,128)(2,1)}, bf16[64,2176]{1,0:T(8,128)(2,1)S(1)}, u32[]{:S(2)}, u32[]{:S(2)}) collective-permute-start(bf16[64,2176]{1,0:T(8,128)(2,1)} %attend.6), channel_id=1, source_target_pairs={{0,16},{8,24},{16,0},{24,8},{1,17},{9,25},{17,1},{25,9},{2,18},{10... | collective-permute-start | bytes 835592 | tf_op jit(solution)/shard_map/ppermute | solution.py:188
  23.8 0.7 copy-start.17
  29.6 14.0 %collective-permute-start.6 = (bf16[64,2176]{1,0:T(8,128)(2,1)}, bf16[64,2176]{1,0:T(8,128)(2,1)S(1)}, u32[]{:S(2)}, u32[]{:S(2)}) collective-permute-start(bf16[64,2176]{1,0:T(8,128)(2,1)} %attend.7), channel_id=1, source_target_pairs={{0,24},{8,16},{16,8},{24,0},{1,25},{9,17},{17,9},{25,1},{2,26},{10... | collective-permute-start | bytes 835592 | tf_op jit(solution)/shard_map/ppermute | solution.py:188
  31.0 0.7 copy-start.16
  36.8 7.2 %collective-permute-start.2 = (bf16[64,2176]{1,0:T(8,128)(2,1)}, bf16[64,2176]{1,0:T(8,128)(2,1)S(1)}, u32[]{:S(2)}, u32[]{:S(2)}) collective-permute-start(bf16[64,2176]{1,0:T(8,128)(2,1)} %attend.5), channel_id=1, source_target_pairs={{0,8},{8,0},{16,24},{24,16},{1,9},{9,1},{17,25},{25,17},{2,10},{10... | collective-permute-start | bytes 835592 | tf_op jit(solution)/shard_map/ppermute | solution.py:188
  43.6 0.8 copy-start.11
  44.0 0.7 copy-start.12
  46.9 5.0 %collective-permute-start.7 = (bf16[64,640]{1,0:T(8,128)(2,1)}, bf16[64,640]{1,0:T(8,128)(2,1)S(1)}, u32[]{:S(2)}, u32[]{:S(2)}) collective-permute-start(bf16[64,640]{1,0:T(8,128)(2,1)} %get-tuple-element.10), channel_id=1, source_target_pairs={{0,2},{1,3},{2,0},{3,1},{4,6},{5,7},{6,4},{7,5},{8,10},{9,11},{10,... | collective-permute-start | bytes 245768 | tf_op jit(solution)/shard_map/ppermute | solution.py:188
  48.5 7.3 %collective-permute-start.8 = (bf16[64,640]{1,0:T(8,128)(2,1)}, bf16[64,640]{1,0:T(8,128)(2,1)S(1)}, u32[]{:S(2)}, u32[]{:S(2)}) collective-permute-start(bf16[64,640]{1,0:T(8,128)(2,1)} %get-tuple-element.11), channel_id=1, source_target_pairs={{0,4},{1,5},{2,6},{3,7},{4,0},{5,1},{6,2},{7,3},{8,12},{9,13},{10,... | collective-permute-start | bytes 245768 | tf_op jit(solution)/shard_map/ppermute | solution.py:188
  51.1 6.5 %collective-permute-start.9 = (bf16[64,640]{1,0:T(8,128)(2,1)}, bf16[64,640]{1,0:T(8,128)(2,1)S(1)}, u32[]{:S(2)}, u32[]{:S(2)}) collective-permute-start(bf16[64,640]{1,0:T(8,128)(2,1)} %get-tuple-element.12), channel_id=1, source_target_pairs={{0,6},{1,7},{2,4},{3,5},{4,2},{5,3},{6,0},{7,1},{8,14},{9,15},{10,... | collective-permute-start | bytes 245768 | tf_op jit(solution)/shard_map/ppermute | solution.py:188
  51.9 5.7 %copy-start.20 = (bf16[64,640]{1,0:T(8,128)(2,1)}, bf16[64,640]{1,0:T(8,128)(2,1)S(1)}, u32[]{:S(2)}) copy-start(bf16[64,640]{1,0:T(8,128)(2,1)S(1)} %collective-permute-done.7.refs_1_) | copy-start | bytes 245764
  55.8 1.8 copy-start.21
  61.6 4.5 %collective-permute-start.10 = (bf16[64,512]{1,0:T(8,128)(2,1)}, bf16[64,512]{1,0:T(8,128)(2,1)S(1)}, u32[]{:S(2)}, u32[]{:S(2)}) collective-permute-start(bf16[64,512]{1,0:T(8,128)(2,1)} %merge.1.refs_0_), channel_id=1, source_target_pairs={{0,2},{1,3},{2,0},{3,1},{4,6},{5,7},{6,4},{7,5},{8,10},{9,11},{10,... | collective-permute-start | bytes 196616 | tf_op jit(solution)/shard_map/ppermute | solution.py:188
  61.6 5.4 %collective-permute-start.11 = (bf16[64,512]{1,0:T(8,128)(2,1)}, bf16[64,512]{1,0:T(8,128)(2,1)S(1)}, u32[]{:S(2)}, u32[]{:S(2)}) collective-permute-start(bf16[64,512]{1,0:T(8,128)(2,1)} %merge.1.refs_0_), channel_id=1, source_target_pairs={{0,4},{1,5},{2,6},{3,7},{4,0},{5,1},{6,2},{7,3},{8,12},{9,13},{10,... | collective-permute-start | bytes 196616 | tf_op jit(solution)/shard_map/ppermute | solution.py:188
  63.4 6.4 %collective-permute-start.12 = (bf16[64,512]{1,0:T(8,128)(2,1)}, bf16[64,512]{1,0:T(8,128)(2,1)S(1)}, u32[]{:S(2)}, u32[]{:S(2)}) collective-permute-start(bf16[64,512]{1,0:T(8,128)(2,1)} %merge.1.refs_0_), channel_id=1, source_target_pairs={{0,6},{1,7},{2,4},{3,5},{4,2},{5,3},{6,0},{7,1},{8,14},{9,15},{10,... | collective-permute-start | bytes 196616 | tf_op jit(solution)/shard_map/ppermute | solution.py:188
  66.1 17.3 %copy-start.27 = (s32[8]{0:T(128)}, s32[8]{0:T(128)S(1)}, u32[]{:S(2)}) copy-start(s32[8]{0:T(128)S(1)} %select_reduce_fusion.3) | copy-start | bytes 100
  66.2 6.8 %copy-start.13 = (bf16[64,512]{1,0:T(8,128)(2,1)}, bf16[64,512]{1,0:T(8,128)(2,1)S(1)}, u32[]{:S(2)}) copy-start(bf16[64,512]{1,0:T(8,128)(2,1)S(1)} %collective-permute-done.10.refs_1_) | copy-start | bytes 196612
  67.0 6.0 %copy-start.14 = (bf16[64,512]{1,0:T(8,128)(2,1)}, bf16[64,512]{1,0:T(8,128)(2,1)S(1)}, u32[]{:S(2)}) copy-start(bf16[64,512]{1,0:T(8,128)(2,1)S(1)} %collective-permute-done.11.refs_2_) | copy-start | bytes 196612
  69.8 3.2 %copy-start.15 = (bf16[64,512]{1,0:T(8,128)(2,1)}, bf16[64,512]{1,0:T(8,128)(2,1)S(1)}, u32[]{:S(2)}) copy-start(bf16[64,512]{1,0:T(8,128)(2,1)S(1)} %collective-permute-done.12.refs_3_) | copy-start | bytes 196612
  70.7 1.6 collective-permute-start.13
  73.0 15.4 %copy-start.29 = (f32[512]{0:T(512)S(1)}, f32[512]{0:T(512)}, u32[]{:S(2)}) copy-start(f32[512]{0:T(512)} %param.26) | copy-start | bytes 6148
  80.0 4.5 %collective-permute-start.14 = (bf16[64,512]{1,0:T(8,128)(2,1)}, bf16[64,512]{1,0:T(8,128)(2,1)S(1)}, u32[]{:S(2)}, u32[]{:S(2)}) collective-permute-start(bf16[64,512]{1,0:T(8,128)(2,1)} %project.1), channel_id=1, source_target_pairs={{0,8},{8,0},{16,24},{24,16},{1,9},{9,1},{17,25},{25,17},{2,10},{10... | collective-permute-start | bytes 196616 | tf_op jit(solution)/shard_map/ppermute | solution.py:188
  81.5 4.5 %collective-permute-start.15 = (bf16[64,512]{1,0:T(8,128)(2,1)}, bf16[64,512]{1,0:T(8,128)(2,1)S(1)}, u32[]{:S(2)}, u32[]{:S(2)}) collective-permute-start(bf16[64,512]{1,0:T(8,128)(2,1)} %project.1), channel_id=1, source_target_pairs={{0,16},{8,24},{16,0},{24,8},{1,17},{9,25},{17,1},{25,9},{2,18},{10... | collective-permute-start | bytes 196616 | tf_op jit(solution)/shard_map/ppermute | solution.py:188
  83.0 5.4 %collective-permute-start.16 = (bf16[64,512]{1,0:T(8,128)(2,1)}, bf16[64,512]{1,0:T(8,128)(2,1)S(1)}, u32[]{:S(2)}, u32[]{:S(2)}) collective-permute-start(bf16[64,512]{1,0:T(8,128)(2,1)} %project.1), channel_id=1, source_target_pairs={{0,24},{8,16},{16,8},{24,0},{1,25},{9,17},{17,9},{25,1},{2,26},{10... | collective-permute-start | bytes 196616 | tf_op jit(solution)/shard_map/ppermute | solution.py:188
  99.3 34.0 %collective-permute-start.17 = (bf16[576,1024]{1,0:T(8,128)(2,1)}, bf16[576,1024]{1,0:T(8,128)(2,1)S(1)}, u32[]{:S(2)}, u32[]{:S(2)}) collective-permute-start(bf16[576,1024]{1,0:T(8,128)(2,1)} %widen.5), channel_id=1, source_target_pairs={{0,1},{1,0},{2,3},{3,2},{4,5},{5,4},{6,7},{7,6},{8,9},{9,8},{10,11... | collective-permute-start | bytes 3538952 | tf_op jit(solution)/shard_map/ppermute | solution.py:188
  99.3 9.4 %copy-start.6 = (bf16[64,512]{1,0:T(8,128)(2,1)S(1)}, bf16[64,512]{1,0:T(8,128)(2,1)}, u32[]{:S(2)}) copy-start(bf16[64,512]{1,0:T(8,128)(2,1)} %project.1) | copy-start | bytes 196612
  108.1 25.7 %collective-permute-start.26 = (bf16[576,1024]{1,0:T(8,128)(2,1)}, bf16[576,1024]{1,0:T(8,128)(2,1)S(1)}, u32[]{:S(2)}, u32[]{:S(2)}) collective-permute-start(bf16[576,1024]{1,0:T(8,128)(2,1)} %widen.7), channel_id=1, source_target_pairs={{0,1},{1,0},{2,3},{3,2},{4,5},{5,4},{6,7},{7,6},{8,9},{9,8},{10,11... | collective-permute-start | bytes 3538952 | tf_op jit(solution)/shard_map/ppermute | solution.py:188
  108.8 12.5 %copy-start.23 = (f32[256]{0:T(256)}, f32[256]{0:T(256)S(1)}, u32[]{:S(2)}) copy-start(f32[256]{0:T(256)S(1)} %fusion.2) | copy-start | bytes 3076
  108.8 2.5 %collective-permute-start.20 = (f32[2,128]{1,0:T(2,128)S(1)}, f32[2,128]{1,0:T(2,128)S(1)}, u32[]{:S(2)}, u32[]{:S(2)}) collective-permute-start(f32[2,128]{1,0:T(2,128)S(1)} %bitcast.42), channel_id=1, source_target_pairs={{0,1},{1,0},{2,3},{3,2},{4,5},{5,4},{6,7},{7,6},{8,9},{9,8},{10,11... | collective-permute-start | bytes 3080 | tf_op jit(solution)/shard_map/ppermute | solution.py:188
  111.3 9.9 %copy-start.26 = (f32[2,128]{1,0:T(2,128)}, f32[2,128]{1,0:T(2,128)S(1)}, u32[]{:S(2)}) copy-start(f32[2,128]{1,0:T(2,128)S(1)} %collective-permute-done.20) | copy-start | bytes 3076
  111.9 18.3 %collective-permute-start.21 = (f32[2,128]{1,0:T(2,128)}, f32[2,128]{1,0:T(2,128)}, u32[]{:S(2)}, u32[]{:S(2)}) collective-permute-start(f32[2,128]{1,0:T(2,128)} %bitcast_add_fusion), channel_id=1, source_target_pairs={{0,2},{1,3},{2,0},{3,1},{4,6},{5,7},{6,4},{7,5},{8,10},{9,11},{10,... | collective-permute-start | bytes 3080 | tf_op jit(solution)/shard_map/ppermute | solution.py:188
  121.3 12.0 %copy-start.2 = (bf16[576,1024]{1,0:T(8,128)(2,1)S(1)}, bf16[576,1024]{1,0:T(8,128)(2,1)}, u32[]{:S(2)}) copy-start(bf16[576,1024]{1,0:T(8,128)(2,1)} %widen.4) | copy-start | bytes 3538948
  130.9 5.6 %collective-permute-start.22 = (f32[2,128]{1,0:T(2,128)S(1)}, f32[2,128]{1,0:T(2,128)S(1)}, u32[]{:S(2)}, u32[]{:S(2)}) collective-permute-start(f32[2,128]{1,0:T(2,128)S(1)} %fusion.20), channel_id=1, source_target_pairs={{0,4},{1,5},{2,6},{3,7},{4,0},{5,1},{6,2},{7,3},{8,12},{9,13},{10,... | collective-permute-start | bytes 3080 | tf_op jit(solution)/shard_map/ppermute | solution.py:188
  133.7 1.3 copy-start.1
  133.8 16.3 %collective-permute-start.18 = (bf16[288,1024]{1,0:T(8,128)(2,1)S(1)}, bf16[288,1024]{1,0:T(8,128)(2,1)S(1)}, u32[]{:S(2)}, u32[]{:S(2)}) collective-permute-start(bf16[288,1024]{1,0:T(8,128)(2,1)S(1)} %constant_dynamic-slice_fusion.7), channel_id=1, source_target_pairs={{0,2},{1,3},{2,0},{3,1},{4,6},{5,7},{6,4},{7,5},{8,10},{9,11},{10,... | collective-permute-start | bytes 1769480 | tf_op jit(solution)/shard_map/ppermute | solution.py:188
  135.5 27.2 %collective-permute-start.27 = (bf16[288,1024]{1,0:T(8,128)(2,1)S(1)}, bf16[288,1024]{1,0:T(8,128)(2,1)S(1)}, u32[]{:S(2)}, u32[]{:S(2)}) collective-permute-start(bf16[288,1024]{1,0:T(8,128)(2,1)S(1)} %constant_dynamic-slice_fusion.1), channel_id=1, source_target_pairs={{0,2},{1,3},{2,0},{3,1},{4,6},{5,7},{6,4},{7,5},{8,10},{9,11},{10,... | collective-permute-start | bytes 1769480 | tf_op jit(solution)/shard_map/ppermute | solution.py:188
  150.3 12.9 %copy-start.19 = (pred[144,256]{1,0:T(8,128)(4,1)S(1)}, pred[144,256]{1,0:T(8,128)(4,1)}, u32[]{:S(2)}) copy-start(pred[144,256]{1,0:T(8,128)(4,1)} %compare_reduce_fusion) | copy-start | bytes 110596
  150.4 18.7 %collective-permute-start.19 = (bf16[144,1024]{1,0:T(8,128)(2,1)S(1)}, bf16[144,1024]{1,0:T(8,128)(2,1)S(1)}, u32[]{:S(2)}, u32[]{:S(2)}) collective-permute-start(bf16[144,1024]{1,0:T(8,128)(2,1)S(1)} %constant_dynamic-slice_fusion.6), channel_id=1, source_target_pairs={{0,6},{1,7},{2,4},{3,5},{4,2},{5,3},{6,0},{7,1},{8,14},{9,15},{10,... | collective-permute-start | bytes 884744 | tf_op jit(solution)/shard_map/ppermute | solution.py:188
  163.0 11.2 %collective-permute-start.28 = (bf16[144,1024]{1,0:T(8,128)(2,1)S(1)}, bf16[144,1024]{1,0:T(8,128)(2,1)S(1)}, u32[]{:S(2)}, u32[]{:S(2)}) collective-permute-start(bf16[144,1024]{1,0:T(8,128)(2,1)S(1)} %constant_dynamic-slice_fusion), channel_id=1, source_target_pairs={{0,6},{1,7},{2,4},{3,5},{4,2},{5,3},{6,0},{7,1},{8,14},{9,15},{10,... | collective-permute-start | bytes 884744 | tf_op jit(solution)/shard_map/ppermute | solution.py:188
  174.6 8.5 %collective-permute-start.29 = (bf16[144,512]{1,0:T(8,128)(2,1)S(1)}, bf16[144,512]{1,0:T(8,128)(2,1)S(1)}, u32[]{:S(2)}, u32[]{:S(2)}) collective-permute-start(bf16[144,512]{1,0:T(8,128)(2,1)S(1)} %get-tuple-element.43), channel_id=1, source_target_pairs={{0,6},{1,7},{2,4},{3,5},{4,2},{5,3},{6,0},{7,1},{8,14},{9,15},{10,... | collective-permute-start | bytes 442376 | tf_op jit(solution)/shard_map/ppermute | solution.py:188
  176.8 17.8 %collective-permute-start.23 = (bf16[144,512]{1,0:T(8,128)(2,1)S(1)}, bf16[144,512]{1,0:T(8,128)(2,1)S(1)}, u32[]{:S(2)}, u32[]{:S(2)}) collective-permute-start(bf16[144,512]{1,0:T(8,128)(2,1)S(1)} %get-tuple-element.44), channel_id=1, source_target_pairs={{0,6},{1,7},{2,4},{3,5},{4,2},{5,3},{6,0},{7,1},{8,14},{9,15},{10,... | collective-permute-start | bytes 442376 | tf_op jit(solution)/shard_map/ppermute | solution.py:188
  183.1 19.3 %collective-permute-start.30 = (bf16[288,512]{1,0:T(8,128)(2,1)S(1)}, bf16[288,512]{1,0:T(8,128)(2,1)S(1)}, u32[]{:S(2)}, u32[]{:S(2)}) collective-permute-start(bf16[288,512]{1,0:T(8,128)(2,1)S(1)} %pad_maximum_fusion.4), channel_id=1, source_target_pairs={{0,2},{1,3},{2,0},{3,1},{4,6},{5,7},{6,4},{7,5},{8,10},{9,11},{10,... | collective-permute-start | bytes 884744 | tf_op jit(solution)/shard_map/ppermute | solution.py:188
  194.6 11.6 %collective-permute-start.24 = (bf16[288,512]{1,0:T(8,128)(2,1)S(1)}, bf16[288,512]{1,0:T(8,128)(2,1)S(1)}, u32[]{:S(2)}, u32[]{:S(2)}) collective-permute-start(bf16[288,512]{1,0:T(8,128)(2,1)S(1)} %pad_maximum_fusion.3), channel_id=1, source_target_pairs={{0,2},{1,3},{2,0},{3,1},{4,6},{5,7},{6,4},{7,5},{8,10},{9,11},{10,... | collective-permute-start | bytes 884744 | tf_op jit(solution)/shard_map/ppermute | solution.py:188
  202.6 3.8 %copy-start.3 = (bf16[576,512]{1,0:T(8,128)(2,1)}, bf16[576,512]{1,0:T(8,128)(2,1)S(1)}, u32[]{:S(2)}) copy-start(bf16[576,512]{1,0:T(8,128)(2,1)S(1)} %pad_maximum_fusion.2.own_ref) | copy-start | bytes 1769476
  202.6 5.1 %copy-start.28 = (s32[8]{0:T(128)S(1)}, s32[8]{0:T(128)}, u32[]{:S(2)}) copy-start(s32[8]{0:T(128)} %copy-done.27) | copy-start | bytes 100
  202.6 6.6 %collective-permute-start.31 = (bf16[576,512]{1,0:T(8,128)(2,1)S(1)}, bf16[576,512]{1,0:T(8,128)(2,1)S(1)}, u32[]{:S(2)}, u32[]{:S(2)}) collective-permute-start(bf16[576,512]{1,0:T(8,128)(2,1)S(1)} %pad_maximum_fusion.2.own_ref), channel_id=1, source_target_pairs={{0,1},{1,0},{2,3},{3,2},{4,5},{5,4},{6,7},{7,6},{8,9},{9,8},{10,11... | collective-permute-start | bytes 1769480 | tf_op jit(solution)/shard_map/ppermute | solution.py:188
  206.5 13.9 %copy-start.4 = (bf16[576,512]{1,0:T(8,128)(2,1)}, bf16[576,512]{1,0:T(8,128)(2,1)S(1)}, u32[]{:S(2)}) copy-start(bf16[576,512]{1,0:T(8,128)(2,1)S(1)} %pad_maximum_fusion.1.own_ref) | copy-start | bytes 1769476
  206.5 13.9 %collective-permute-start.25 = (bf16[576,512]{1,0:T(8,128)(2,1)S(1)}, bf16[576,512]{1,0:T(8,128)(2,1)S(1)}, u32[]{:S(2)}, u32[]{:S(2)}) collective-permute-start(bf16[576,512]{1,0:T(8,128)(2,1)S(1)} %pad_maximum_fusion.1.own_ref), channel_id=1, source_target_pairs={{0,1},{1,0},{2,3},{3,2},{4,5},{5,4},{6,7},{7,6},{8,9},{9,8},{10,11... | collective-permute-start | bytes 1769480 | tf_op jit(solution)/shard_map/ppermute | solution.py:188
  209.2 1.0 copy-start.8
  220.4 0.9 copy-start.9
  231.4 7.4 %copy-start.7 = (bf16[64,512]{1,0:T(8,128)(2,1)S(1)}, bf16[64,512]{1,0:T(8,128)(2,1)}, u32[]{:S(2)}) copy-start(bf16[64,512]{1,0:T(8,128)(2,1)} %project.1) | copy-start | bytes 196612
  232.5 4.6 %collective-permute-start.32 = (bf16[64,512]{1,0:T(8,128)(2,1)S(1)}, bf16[64,512]{1,0:T(8,128)(2,1)S(1)}, u32[]{:S(2)}, u32[]{:S(2)}) collective-permute-start(bf16[64,512]{1,0:T(8,128)(2,1)S(1)} %get-tuple-element.28), channel_id=1, source_target_pairs={{0,8},{8,0},{16,24},{24,16},{1,9},{9,1},{17,25},{25,17},{2,10},{10... | collective-permute-start | bytes 196616 | tf_op jit(solution)/shard_map/ppermute | solution.py:188
  233.1 5.0 %collective-permute-start.33 = (bf16[64,512]{1,0:T(8,128)(2,1)S(1)}, bf16[64,512]{1,0:T(8,128)(2,1)S(1)}, u32[]{:S(2)}, u32[]{:S(2)}) collective-permute-start(bf16[64,512]{1,0:T(8,128)(2,1)S(1)} %get-tuple-element.30), channel_id=1, source_target_pairs={{0,16},{8,24},{16,0},{24,8},{1,17},{9,25},{17,1},{25,9},{2,18},{10... | collective-permute-start | bytes 196616 | tf_op jit(solution)/shard_map/ppermute | solution.py:188
  233.6 5.2 %collective-permute-start.34 = (bf16[64,512]{1,0:T(8,128)(2,1)S(1)}, bf16[64,512]{1,0:T(8,128)(2,1)S(1)}, u32[]{:S(2)}, u32[]{:S(2)}) collective-permute-start(bf16[64,512]{1,0:T(8,128)(2,1)S(1)} %get-tuple-element.29), channel_id=1, source_target_pairs={{0,24},{8,16},{16,8},{24,0},{1,25},{9,17},{17,9},{25,1},{2,26},{10... | collective-permute-start | bytes 196616 | tf_op jit(solution)/shard_map/ppermute | solution.py:188
  (4 other events, 2.7 us)

commit v2 on v1

--- a/solution.py
+++ b/solution.py
@@ -12,6 +12,7 @@
 GROUPS = 3
 LANES = 128
 ROWS = 8
+PER_STEP = 2
 CHUNKS = 2
 
 
@@ -189,47 +190,54 @@
 
 
 def attend_kernel(core_ref, q_ref, k_own_ref, v_own_ref, k_far_ref, v_far_ref, out_ref):
-    head = pl.program_id(0)
-    per_kv = q_ref.shape[1] // HD
+    step = pl.program_id(0)
+    count = k_far_ref.shape[1] // HD
+    per_kv = q_ref.shape[1] // HD // count
     rows = q_ref.shape[0]
     scaling = 1.0 / math.sqrt(HD)
-    q = jnp.concatenate([q_ref[:, j * HD : (j + 1) * HD] for j in range(per_kv)], axis=0)
+    factor = scaling * math.log2(math.e)
     contract = (((1,), (1,)), ((), ()))
-    near = lax.dot_general(q, k_own_ref[0], contract, preferred_element_type=jnp.float32)
-    far = lax.dot_general(q, k_far_ref[...], contract, preferred_element_type=jnp.float32)
-    top = jnp.maximum(
-        jnp.max(near, axis=1, keepdims=True), jnp.max(far, axis=1, keepdims=True)
-    )
-    factor = scaling * math.log2(math.e)
-    near = jnp.exp2((near - top) * factor)
-    far = jnp.exp2((far - top) * factor)
-    total = jnp.sum(near, axis=1, keepdims=True) + jnp.sum(far, axis=1, keepdims=True)
-    acc = jnp.dot(
-        near.astype(jnp.bfloat16), v_own_ref[0], preferred_element_type=jnp.float32
-    ) + jnp.dot(far.astype(jnp.bfloat16), v_far_ref[...], preferred_element_type=jnp.float32)
-    acc = acc / total
-    lse = top * scaling + jnp.log(total)
     lanes = lax.broadcasted_iota(jnp.int32, (rows, LANES), 1)
-    heads = pl.num_programs(0) * per_kv
+    heads = pl.num_programs(0) * count * per_kv
     stats = jnp.zeros((rows, LANES), jnp.float32)
-    for j in range(per_kv):
-        part = lse[j * rows : (j + 1) * rows]
-        high = part.astype(jnp.bfloat16).astype(jnp.float32)
-        middle = (part - high).astype(jnp.bfloat16).astype(jnp.float32)
-        low = part - high - middle
-        place = head * per_kv + j
-        stats = jnp.where(lanes == place, high, stats)
-        stats = jnp.where(lanes == heads + place, middle, stats)
-        stats = jnp.where(lanes == 2 * heads + place, low, stats)
-        where = pl.multiple_of((head * per_kv + j) * HD, HD)
-        out_ref[:, pl.ds(where, HD)] = acc[j * rows : (j + 1) * rows].astype(jnp.bfloat16)
+    for c in range(count):
+        cols = slice(c * HD, (c + 1) * HD)
+        q = jnp.concatenate(
+            [q_ref[:, j * HD : (j + 1) * HD] for j in range(c * per_kv, (c + 1) * per_kv)], axis=0
+        )
+        near = lax.dot_general(q, k_own_ref[0, :, cols], contract, preferred_element_type=jnp.float32)
+        far = lax.dot_general(q, k_far_ref[:, cols], contract, preferred_element_type=jnp.float32)
+        top = jnp.maximum(
+            jnp.max(near, axis=1, keepdims=True), jnp.max(far, axis=1, keepdims=True)
+        )
+        near = jnp.exp2((near - top) * factor)
+        far = jnp.exp2((far - top) * factor)
+        total = jnp.sum(near, axis=1, keepdims=True) + jnp.sum(far, axis=1, keepdims=True)
+        acc = jnp.dot(
+            near.astype(jnp.bfloat16), v_own_ref[0, :, cols], preferred_element_type=jnp.float32
+        ) + jnp.dot(
+            far.astype(jnp.bfloat16), v_far_ref[:, cols], preferred_element_type=jnp.float32
+        )
+        acc = acc / total
+        lse = top * scaling + jnp.log(total)
+        for j in range(per_kv):
+            part = lse[j * rows : (j + 1) * rows]
+            high = part.astype(jnp.bfloat16).astype(jnp.float32)
+            middle = (part - high).astype(jnp.bfloat16).astype(jnp.float32)
+            low = part - high - middle
+            place = (step * count + c) * per_kv + j
+            stats = jnp.where(lanes == place, high, stats)
+            stats = jnp.where(lanes == heads + place, middle, stats)
+            stats = jnp.where(lanes == 2 * heads + place, low, stats)
+            where = pl.multiple_of(place * HD, HD)
+            out_ref[:, pl.ds(where, HD)] = acc[j * rows : (j + 1) * rows].astype(jnp.bfloat16)
     width = out_ref.shape[1] - LANES
 
-    @pl.when(head == 0)
+    @pl.when(step == 0)
     def _():
         out_ref[:, width:] = stats.astype(jnp.bfloat16)
 
-    @pl.when(head > 0)
+    @pl.when(step > 0)
     def _():
         out_ref[:, width:] = (out_ref[:, width:].astype(jnp.float32) + stats).astype(jnp.bfloat16)
 
@@ -238,18 +246,20 @@
     rows, width = q.shape
     slab = keys.shape[1]
     heads = far.shape[1] // 2 // HD
-    span = width // heads
+    steps = heads // PER_STEP
+    span = width // steps
+    depth = PER_STEP * HD
     return pl.pallas_call(
         attend_kernel,
         grid_spec=pltpu.PrefetchScalarGridSpec(
             num_scalar_prefetch=1,
-            grid=(heads,),
+            grid=(steps,),
             in_specs=[
                 pl.BlockSpec((rows, span), lambda h, s: (0, h)),
-                pl.BlockSpec((1, slab, HD), lambda h, s: (0, 0, s[0] * heads + h)),
-                pl.BlockSpec((1, slab, HD), lambda h, s: (0, 0, s[0] * heads + h)),
-                pl.BlockSpec((slab, HD), lambda h, s: (0, h)),
-                pl.BlockSpec((slab, HD), lambda h, s: (0, heads + h)),
+                pl.BlockSpec((1, slab, depth), lambda h, s: (0, 0, s[0] * steps + h)),
+                pl.BlockSpec((1, slab, depth), lambda h, s: (0, 0, s[0] * steps + h)),
+                pl.BlockSpec((slab, depth), lambda h, s: (0, h)),
+                pl.BlockSpec((slab, depth), lambda h, s: (0, steps + h)),
             ],
             out_specs=pl.BlockSpec((rows, width + LANES), lambda h, s: (0, 0)),
         ),
@@ -357,25 +367,12 @@
     )(place, mask, queries, suffix_keys, suffix_values, *pieces)
 
 
-def project_kernel(order_ref, stream_ref, weight_ref, *refs):
-    pieces, out_ref, acc_ref = refs[:-2], refs[-2], refs[-1]
-    step = pl.program_id(0)
-
-    @pl.when(step == 0)
-    def _():
-        acc_ref[...] = stream_ref[...].astype(jnp.float32)
-
-    for k, piece in enumerate(pieces):
-
-        @pl.when(step == k)
-        def _(piece=piece):
-            acc_ref[...] += jnp.dot(
-                piece[...], weight_ref[...], preferred_element_type=jnp.float32
-            )
-
-    @pl.when(step == len(pieces) - 1)
-    def _():
-        out_ref[...] = acc_ref[...].astype(jnp.bfloat16)
+def project_kernel(order_ref, stream_ref, *refs):
+    count = (len(refs) - 1) // 2
+    total = stream_ref[...].astype(jnp.float32)
+    for weight, piece in zip(refs[:count], refs[count : 2 * count]):
+        total = total + jnp.dot(piece[...], weight[...], preferred_element_type=jnp.float32)
+    refs[-1][...] = total.astype(jnp.bfloat16)
 
 
 def project(order, stream, weight, pieces):
@@ -385,36 +382,40 @@
         project_kernel,
         grid_spec=pltpu.PrefetchScalarGridSpec(
             num_scalar_prefetch=1,
-            grid=(len(pieces),),
-            in_specs=[
-                pl.BlockSpec((rows, width), lambda i, s: (0, 0)),
-                pl.BlockSpec((span, width), lambda i, s: (s[i], 0)),
+            grid=(1,),
+            in_specs=[pl.BlockSpec((rows, width), lambda i, s: (0, 0))]
+            + [
+                pl.BlockSpec((span, width), lambda i, s, k=k: (s[k], 0))
+                for k in range(len(pieces))
             ]
             + [pl.BlockSpec((rows, span), lambda i, s: (0, 0))] * len(pieces),
             out_specs=pl.BlockSpec((rows, width), lambda i, s: (0, 0)),
-            scratch_shapes=[pltpu.VMEM((rows, width), jnp.float32)],
         ),
         out_shape=jax.ShapeDtypeStruct((rows, width), jnp.bfloat16),
         name="project",
-    )(order, stream, weight, *pieces)
+    )(order, stream, *[weight] * len(pieces), *pieces)
 
 
 def widen_kernel(table_ref, rows_ref, gate_ref, up_ref, out_ref, acc_ref):
-    expert = pl.program_id(0)
-    capacity = rows_ref.shape[1]
+    step = pl.program_id(0)
+    count, capacity = rows_ref.shape[:2]
     width = gate_ref.shape[2]
-    here = pl.ds(pl.multiple_of(table_ref[1 + expert], ROWS), capacity)
-
-    @pl.when(expert == 0)
+    filled = out_ref.shape[0] - pl.num_programs(0) * count * ROWS
+
+    @pl.when(step == 0)
     def _():
-        acc_ref[...] = jnp.zeros(acc_ref.shape, jnp.float32)
-
-    acc_ref[here, :width] = jnp.dot(
-        rows_ref[0], gate_ref[0], preferred_element_type=jnp.float32
-    )
-    acc_ref[here, width:] = jnp.dot(rows_ref[0], up_ref[0], preferred_element_type=jnp.float32)
-
-    @pl.when(expert == pl.num_programs(0) - 1)
+        acc_ref[filled:, :] = jnp.zeros((acc_ref.shape[0] - filled, 2 * width), jnp.float32)
+
+    for k in range(count):
+        here = pl.ds(pl.multiple_of(table_ref[1 + step * count + k], ROWS), capacity)
+        acc_ref[here, :width] = jnp.dot(
+            rows_ref[k], gate_ref[k], preferred_element_type=jnp.float32
+        )
+        acc_ref[here, width:] = jnp.dot(
+            rows_ref[k], up_ref[k], preferred_element_type=jnp.float32
+        )
+
+    @pl.when(step == pl.num_programs(0) - 1)
     def _():
         out_ref[...] = acc_ref[: out_ref.shape[0], :].astype(jnp.bfloat16)
 
@@ -422,14 +423,14 @@
 def widen(table, rows_in, w_gate, w_up, parts, slots):
     experts, capacity, depth = rows_in.shape
     width = w_gate.shape[2] // parts
-    weight = pl.BlockSpec((1, depth, width), lambda e, s: (e, 0, s[0]))
+    weight = pl.BlockSpec((PER_STEP, depth, width), lambda e, s: (e, 0, s[0]))
     return pl.pallas_call(
         widen_kernel,
         grid_spec=pltpu.PrefetchScalarGridSpec(
             num_scalar_prefetch=1,
-            grid=(experts,),
+            grid=(experts // PER_STEP,),
             in_specs=[
-                pl.BlockSpec((1, capacity, depth), lambda e, s: (e, 0, 0)),
+                pl.BlockSpec((PER_STEP, capacity, depth), lambda e, s: (e, 0, 0)),
                 weight,
                 weight,
             ],
@@ -442,11 +443,11 @@
 
 
 def narrow_kernel(table_ref, own_ref, far_ref, near_w_ref, far_w_ref, pick_ref, scale_ref, init_ref, out_ref, own_f, far_f):
-    expert = pl.program_id(0)
+    step = pl.program_id(0)
     slots = own_ref.shape[0]
-    capacity = pick_ref.shape[1]
-
-    @pl.when(expert == 0)
+    count, capacity = pick_ref.shape[:2]
+
+    @pl.when(step == 0)
     def _():
         own_f[:slots, :] = own_ref[...].astype(jnp.float32)
         far_f[:slots, :] = far_ref[...].astype(jnp.float32)
@@ -454,16 +455,17 @@
         far_f[slots:, :] = jnp.zeros((capacity, far_f.shape[1]), jnp.float32)
         out_ref[...] = init_ref[...]
 
-    here = pl.ds(pl.multiple_of(table_ref[2 + expert], ROWS), capacity)
-    rows = jnp.dot(
-        own_f[here, :].astype(jnp.bfloat16), near_w_ref[0], preferred_element_type=jnp.float32
-    ) + jnp.dot(
-        far_f[here, :].astype(jnp.bfloat16), far_w_ref[0], preferred_element_type=jnp.float32
-    )
-    rows = (rows * scale_ref[0]).astype(jnp.bfloat16)
-    out_ref[...] += lax.dot_general(
-        pick_ref[0], rows, (((0,), (0,)), ((), ())), preferred_element_type=jnp.float32
-    )
+    for k in range(count):
+        here = pl.ds(pl.multiple_of(table_ref[2 + step * count + k], ROWS), capacity)
+        rows = jnp.dot(
+            own_f[here, :].astype(jnp.bfloat16), near_w_ref[k], preferred_element_type=jnp.float32
+        ) + jnp.dot(
+            far_f[here, :].astype(jnp.bfloat16), far_w_ref[k], preferred_element_type=jnp.float32
+        )
+        rows = (rows * scale_ref[k]).astype(jnp.bfloat16)
+        out_ref[...] += lax.dot_general(
+            pick_ref[k], rows, (((0,), (0,)), ((), ())), preferred_element_type=jnp.float32
+        )
 
 
 def narrow(table, own, far, w_down, pick, scale, init):
@@ -474,14 +476,14 @@
         narrow_kernel,
         grid_spec=pltpu.PrefetchScalarGridSpec(
             num_scalar_prefetch=1,
-            grid=(experts,),
+            grid=(experts // PER_STEP,),
             in_specs=[
                 pl.BlockSpec((slots, width), lambda e, s: (0, 0)),
                 pl.BlockSpec((slots, width), lambda e, s: (0, 0)),
-                pl.BlockSpec((1, width, cols), lambda e, s: (e, s[0], 0)),
-                pl.BlockSpec((1, width, cols), lambda e, s: (e, s[1], 0)),
-                pl.BlockSpec((1, capacity, tokens), lambda e, s: (e, 0, 0)),
-                pl.BlockSpec((1, capacity, 1), lambda e, s: (e, 0, 0)),
+                pl.BlockSpec((PER_STEP, width, cols), lambda e, s: (e, s[0], 0)),
+                pl.BlockSpec((PER_STEP, width, cols), lambda e, s: (e, s[1], 0)),
+                pl.BlockSpec((PER_STEP, capacity, tokens), lambda e, s: (e, 0, 0)),
+                pl.BlockSpec((PER_STEP, capacity, 1), lambda e, s: (e, 0, 0)),
                 pl.BlockSpec((tokens, cols), lambda e, s: (0, 0)),
             ],
             out_specs=pl.BlockSpec((tokens, cols), lambda e, s: (0, 0)),
@@ -614,9 +616,6 @@
     ).astype(jnp.float32)
     scaled = (all_resid * norm_gain[None, :]).astype(jnp.bfloat16)
     squares = jnp.sum(all_resid * all_resid, axis=1).reshape(-1, LANES)
-    for bit in (1, 2, 4):
-        squares = squares + flip(squares, "gy", n_gy, bit)
-    rstd = 1.0 / jnp.sqrt(squares.reshape(-1) / D + EPSILON)
     rows_in = (
         jnp.dot(
             row_pick.reshape(experts * capacity, tokens),
@@ -627,43 +626,56 @@
         .reshape(experts, capacity, -1)
     )
 
-    half_id = (z_index ^ (z_index >> 1)) & 1
-    low_id = z_index >> 1
-    quarter = half_id * 2 + low_id
-    row_ids = quarter * (slots // 4) + jnp.arange(slots // 4, dtype=i32)
+    near_id = (z_index ^ (z_index >> 1)) & 1
+    wrap_id = z_index >> 1
+    routes_z = [((near_id, 2), (wrap_id, 6)), ((wrap_id, 6), (near_id, 2))]
     slot_of = jnp.where(hits > 0, starts[None, :] + position, -1)
-    owner_mask = jnp.any(row_ids[:, None, None] == slot_of.T[None, :, :], axis=1)
-    row_rstd = jnp.sum(jnp.where(owner_mask, rstd[None, :], 0.0), axis=1, keepdims=True)
+
+    def quarter_rstd(quarter):
+        row_ids = quarter * (slots // 4) + jnp.arange(slots // 4, dtype=i32)
+        owner_mask = jnp.any(row_ids[:, None, None] == slot_of.T[None, :, :], axis=1)
+        return jnp.sum(jnp.where(owner_mask, rstd[None, :], 0.0), axis=1, keepdims=True)
 
     f32 = jnp.float32
     parts = 2 * CHUNKS
     rounded = lambda a, b: (a.astype(f32) + b.astype(f32)).astype(jnp.bfloat16)
-    sums = []
+    halves = []
     for chunk in range(CHUNKS):
-        outs = []
-        for side in (1 - core, core):
-            table = jnp.concatenate([as_vector(2 * chunk + side), starts])
-            outs.append(widen(table, rows_in, w_gate, w_up, parts, slots))
-        sums.append((outs[1], flip(outs[0], "gy", n_gy, 1)))
+        (half_id, half_bit), _ = routes_z[chunk % 2]
+        tables = [
+            jnp.concatenate([as_vector(2 * chunk + side), starts]) for side in (1 - core, core)
+        ]
+        away = widen(tables[0], rows_in, w_gate, w_up, parts, slots)
+        rows_in, away = lax.optimization_barrier((rows_in, away))
+        seen = flip(away, "gy", n_gy, 1)
+        keep = widen(tables[1], rows_in, w_gate, w_up, parts, slots)
+        part = rounded(keep, seen)
+        send = take_block(part, 1 - half_id, slots // 2, 0)
+        keep = take_block(part, half_id, slots // 2, 0)
+        rows_in, send, keep, squares = lax.optimization_barrier((rows_in, send, keep, squares))
+        halves.append((keep, flip(send, "gy", n_gy, half_bit)))
+    for bit in (1, 2, 4):
+        squares = squares + flip(squares, "gy", n_gy, bit)
+    rstd = 1.0 / jnp.sqrt(squares.reshape(-1) / D + EPSILON)
     hidden = []
-    for keep, seen in sums:
+    for chunk, (keep, seen) in enumerate(halves):
+        (half_id, _), (low_id, low_bit) = routes_z[chunk % 2]
         part = rounded(keep, seen)
-        seen = flip(take_block(part, 1 - half_id, slots // 2, 0), "gy", n_gy, 2)
-        part = rounded(take_block(part, half_id, slots // 2, 0), seen)
-        seen = flip(take_block(part, 1 - low_id, slots // 4, 0), "gy", n_gy, 6)
+        seen = flip(take_block(part, 1 - low_id, slots // 4, 0), "gy", n_gy, low_bit)
         part = take_block(part, low_id, slots // 4, 0).astype(f32) + seen.astype(f32)
         width = part.shape[1] // 2
+        row_rstd = quarter_rstd(half_id * 2 + low_id)
         gate = part[:, :width] * row_rstd
         up = part[:, width:] * row_rstd
         hidden.append((jax.nn.silu(gate) * up).astype(jnp.bfloat16))
     total = jnp.zeros((tokens, w_down.shape[2]), f32)
     for chunk, part in enumerate(hidden):
-        seen = flip(part, "gy", n_gy, 6)
-        first = low_id == 0
-        part = jnp.concatenate([jnp.where(first, part, seen), jnp.where(first, seen, part)], axis=0)
-        seen = flip(part, "gy", n_gy, 2)
-        first = half_id == 0
-        part = jnp.concatenate([jnp.where(first, part, seen), jnp.where(first, seen, part)], axis=0)
+        for index, bit in routes_z[chunk % 2][::-1]:
+            seen = flip(part, "gy", n_gy, bit)
+            first = index == 0
+            part = jnp.concatenate(
+                [jnp.where(first, part, seen), jnp.where(first, seen, part)], axis=0
+            )
         seen = flip(part, "gy", n_gy, 1)
         table = jnp.concatenate([as_vector(2 * chunk + core, 2 * chunk + 1 - core), starts])
         total = narrow(table, part, seen, w_down, row_pick, row_weight, total)

time: 241 us -> 217 us (0.900)
  Pallas kernels: 88.3 us -> 71.2 us
  starting transfers between devices: 48.1 us -> 39.5 us
  waiting for transfers between devices: 75 us -> 78.2 us
    ppermute x35, starting transfers between devices: 48.1 us -> 39.5 us  [flip(): return lax.ppermute(value, axis, [(i, i ^ bit) for i in range(size)])]
    pallas_call x4, Pallas kernels: 35.2 us -> 27.6 us  [widen(): pl.pallas_call(widen_kernel, grid_spec=pltpu.PrefetchScalarGridSpec(num_s...]
    pallas_call x2, Pallas kernels: 20.2 us -> 16.3 us  [narrow(): pl.pallas_call(narrow_kernel, grid_spec=pltpu.PrefetchScalarGridSpec(num_...]
    ppermute x35, waiting for transfers between devices: 75 us -> 78.2 us  [flip(): return lax.ppermute(value, axis, [(i, i ^ bit) for i in range(size)])]
    pallas_call x4, Pallas kernels: 20.2 us -> 17.2 us  [attend(): pl.pallas_call(attend_kernel, grid_spec=pltpu.PrefetchScalarGridSpec(num_...]
    pallas_call x1, Pallas kernels: 6.98 us -> 4.4 us  [project(): pl.pallas_call(project_kernel, grid_spec=pltpu.PrefetchScalarGridSpec(num...]
    unnamed x66 -> x52, local copies, waits for them, and re-layouts: 6.31 us -> 5.11 us
  transfers between devices with their start and end apart: 35 -> 35, of which waited for: 21 -> 21; matrix products, arithmetic and copies ran while one was open for 6% -> 6% of each run, Pallas kernels for 24% -> 18%
where the time goes in v2:
time: 217 us; the launch traced here: 216 us
  waiting for transfers between devices  78.2 us (36%)
  Pallas kernels  71.2 us (33%)
  starting transfers between devices  39.5 us (18%)
  other arithmetic  12.8 us (6%)
  local copies, waits for them, and re-layouts  11.8 us (5%)
  matrix products  2.28 us (1%)
    ppermute x35, waiting for transfers between devices, flip(): return lax.ppermute(value, axis, [(i, i ^ bit) for i in range(size)])  78.2 us
    ppermute x35, starting transfers between devices, flip(): return lax.ppermute(value, axis, [(i, i ^ bit) for i in range(size)])  39.5 us
    pallas_call x4, Pallas kernels, widen(): pl.pallas_call(widen_kernel, grid_spec=pltpu.PrefetchScalarGridSpec(num_s...  27.6 us
    pallas_call x4, Pallas kernels, attend(): pl.pallas_call(attend_kernel, grid_spec=pltpu.PrefetchScalarGridSpec(num_...  17.2 us
    pallas_call x2, Pallas kernels, narrow(): pl.pallas_call(narrow_kernel, grid_spec=pltpu.PrefetchScalarGridSpec(num_...  16.3 us
    unnamed x52, local copies, waits for them, and re-layouts  5.11 us
    pallas_call x1, Pallas kernels, project(): pl.pallas_call(project_kernel, grid_spec=pltpu.PrefetchScalarGridSpec(num...  4.4 us
  transfers between devices with their start and end apart: 35, of which 21 were waited for; matrix products, arithmetic and copies ran while one was open for 6% of the time, Pallas kernels for 18%

profile of v2, /device:TPU:0, one launch (start us, length us, event | category | flops | bytes accessed | tf_op | source)
XLA Modules:
  0.0 216.2 jit_solution(9102498554758763770)
XLA Ops:
  0.0 1.0 constant_dynamic-slice_fusion.14.q_ref
  1.0 3.0 %collective-permute-start.1 = (bf16[64,2048]{1,0:T(8,128)(2,1)S(1)}, bf16[64,2048]{1,0:T(8,128)(2,1)S(1)}, u32[]{:S(2)}, u32[]{:S(2)}) collective-permute-start(bf16[64,2048]{1,0:T(8,128)(2,1)S(1)} %constant_dynamic-slice_fusion.14.q_ref), channel_id=1, source_target_pairs={{0,8},{8,0},{16,24},{24,16},{1,9},{9,1},{17,25},{25,17},{2,10},{10... | collective-permute-start | bytes 786440 | tf_op jit(solution)/shard_map/ppermute | solution.py:189
  4.0 1.5 collective-permute-start.3
  5.6 1.3 dynamic-slice_bitcast_fusion
  8.5 2.7 %collective-permute-done.1.q_ref = bf16[64,2048]{1,0:T(8,128)(2,1)S(1)} collective-permute-done((bf16[64,2048]{1,0:T(8,128)(2,1)S(1)}, bf16[64,2048]{1,0:T(8,128)(2,1)S(1)}, u32[]{:S(2)}, u32[]{:S(2)}) %collective-permute-start.1) | collective-permute-done | bytes 262176 | tf_op jit(solution)/shard_map/ppermute | solution.py:189
  12.2 4.3 %attend.5 = bf16[64,2176]{1,0:T(8,128)(2,1)} custom-call(s32[1]{0:T(128)} %bitcast.12.core_ref, bf16[64,2048]{1,0:T(8,128)(2,1)} %copy-done.16, bf16[1,512,1024]{2,1,0:T(8,128)(2,1)} %k_own_ref.7, bf16[1,512,1024]{2,1,0:T(8,128)(2,1)} %v_own_ref.7, bf16[512,1024]{1,0:T(8,128)(2,1)} %copy-done, bf16[512,1024]{1,0:T(8,128)(2,1)} %copy-done), custom_call_target="tpu_custom_call" | custom-call | tf_op jit(solution)/shard_map/attend/pallas_call | solution.py:252
  16.5 2.0 collective-permute-start.2
  19.2 4.3 %attend.6 = bf16[64,2176]{1,0:T(8,128)(2,1)} custom-call(s32[1]{0:T(128)} %bitcast.12.core_ref, bf16[64,2048]{1,0:T(8,128)(2,1)} %copy-done.15, bf16[1,512,1024]{2,1,0:T(8,128)(2,1)} %k_own_ref.7, bf16[1,512,1024]{2,1,0:T(8,128)(2,1)} %v_own_ref.7, bf16[512,1024]{1,0:T(8,128)(2,1)} %copy-done, bf16[512,1024]{1,0:T(8,128)(2,1)} %copy-done), custom_call_target="tpu_custom_call" | custom-call | tf_op jit(solution)/shard_map/attend/pallas_call | solution.py:252
  23.6 1.5 collective-permute-start.4
  25.8 4.3 %attend.7 = bf16[64,2176]{1,0:T(8,128)(2,1)} custom-call(s32[1]{0:T(128)} %bitcast.12.core_ref, bf16[64,2048]{1,0:T(8,128)(2,1)} %copy-done.14, bf16[1,512,1024]{2,1,0:T(8,128)(2,1)} %k_own_ref.7, bf16[1,512,1024]{2,1,0:T(8,128)(2,1)} %v_own_ref.7, bf16[512,1024]{1,0:T(8,128)(2,1)} %copy-done, bf16[512,1024]{1,0:T(8,128)(2,1)} %copy-done), custom_call_target="tpu_custom_call" | custom-call | tf_op jit(solution)/shard_map/attend/pallas_call | solution.py:252
  30.1 0.7 copy.25.pick_ref
  31.5 4.3 %attend.4.a_ref = bf16[64,2176]{1,0:T(8,128)(2,1)} custom-call(s32[1]{0:T(128)} %bitcast.12.core_ref, bf16[64,2048]{1,0:T(8,128)(2,1)} %copy-done.4, bf16[1,512,1024]{2,1,0:T(8,128)(2,1)} %k_own_ref.7, bf16[1,512,1024]{2,1,0:T(8,128)(2,1)} %v_own_ref.7, bf16[512,1024]{1,0:T(8,128)(2,1)} %copy-done, bf16[512,1024]{1,0:T(8,128)(2,1)} %copy-done), custom_call_target="tpu_custom_call" | custom-call | tf_op jit(solution)/shard_map/attend/pallas_call | solution.py:252
  35.8 1.9 collective-permute-done.6.d_ref
  38.5 2.2 %choose.1 = (bf16[64,640]{1,0:T(8,128)(2,1)}, bf16[64,640]{1,0:T(8,128)(2,1)}, bf16[64,640]{1,0:T(8,128)(2,1)}, bf16[64,640]{1,0:T(8,128)(2,1)}) custom-call(s32[1]{0:T(128)} %bitcast.8.z_ref, s32[64,1]{1,0:T(8,128)} %copy.25.pick_ref, bf16[64,2176]{1,0:T(8,128)(2,1)} %attend.4.a_ref, bf16[64,2176]{1,0:T(8,128)(2,1)} %copy-done.8, ...), custom_call_target="tpu_custom_call" | custom-call | tf_op jit(solution)/shard_map/choose/pallas_call | solution.py:293
  40.6 1.6 collective-permute-start.7
  42.2 2.6 %collective-permute-start.8 = (bf16[64,640]{1,0:T(8,128)(2,1)}, bf16[64,640]{1,0:T(8,128)(2,1)S(1)}, u32[]{:S(2)}, u32[]{:S(2)}) collective-permute-start(bf16[64,640]{1,0:T(8,128)(2,1)} %get-tuple-element.22), channel_id=1, source_target_pairs={{0,4},{1,5},{2,6},{3,7},{4,0},{5,1},{6,2},{7,3},{8,12},{9,13},{10,... | collective-permute-start | bytes 245768 | tf_op jit(solution)/shard_map/ppermute | solution.py:189
  45.6 3.3 %collective-permute-done.8.refs_2_ = bf16[64,640]{1,0:T(8,128)(2,1)S(1)} collective-permute-done((bf16[64,640]{1,0:T(8,128)(2,1)}, bf16[64,640]{1,0:T(8,128)(2,1)S(1)}, u32[]{:S(2)}, u32[]{:S(2)}) %collective-permute-start.8) | collective-permute-done | bytes 81952 | tf_op jit(solution)/shard_map/ppermute | solution.py:189
  48.9 2.4 %collective-permute-done.9.refs_3_ = bf16[64,640]{1,0:T(8,128)(2,1)S(1)} collective-permute-done((bf16[64,640]{1,0:T(8,128)(2,1)}, bf16[64,640]{1,0:T(8,128)(2,1)S(1)}, u32[]{:S(2)}, u32[]{:S(2)}) %collective-permute-start.9) | collective-permute-done | bytes 81952 | tf_op jit(solution)/shard_map/ppermute | solution.py:189
  51.9 3.4 %merge.1.refs_8_ = bf16[64,512]{1,0:T(8,128)(2,1)} custom-call(s32[2]{0:T(128)} %pad_add_fusion.1.place_ref, f32[64,64]{1,0:T(8,128)} %fusion.10.mask_ref, bf16[64,4096]{1,0:T(8,128)(2,1)} %q_ref.1, bf16[64,1024]{1,0:T(8,128)(2,1)} %k_ref.1, bf16[64,1024]{1,0:T(8,128)(2,1)} %v_ref.1, bf16[64,640]{1,0:T(8,128)(2,1)} %get-tuple-element.20.refs_0_, ...), custom_call_target="tpu_custom_call" | custom-call | tf_op jit(solution)/shard_map/merge/pallas_call | solution.py:351
  55.3 1.5 collective-permute-start.11
  56.9 2.8 %collective-permute-start.12 = (bf16[64,512]{1,0:T(8,128)(2,1)}, bf16[64,512]{1,0:T(8,128)(2,1)S(1)}, u32[]{:S(2)}, u32[]{:S(2)}) collective-permute-start(bf16[64,512]{1,0:T(8,128)(2,1)} %merge.1.refs_8_), channel_id=1, source_target_pairs={{0,6},{1,7},{2,4},{3,5},{4,2},{5,3},{6,0},{7,1},{8,14},{9,15},{10,... | collective-permute-start | bytes 196616 | tf_op jit(solution)/shard_map/ppermute | solution.py:189
  59.8 0.9 collective-permute-done.11.refs_10_
  60.7 2.4 %collective-permute-done.12.refs_11_ = bf16[64,512]{1,0:T(8,128)(2,1)S(1)} collective-permute-done((bf16[64,512]{1,0:T(8,128)(2,1)}, bf16[64,512]{1,0:T(8,128)(2,1)S(1)}, u32[]{:S(2)}, u32[]{:S(2)}) %collective-permute-start.12) | collective-permute-done | bytes 65568 | tf_op jit(solution)/shard_map/ppermute | solution.py:189
  63.2 0.9 pad_maximum_fusion.5
  65.6 0.7 fusion.18
  66.4 4.4 %project.1 = bf16[64,512]{1,0:T(8,128)(2,1)} custom-call(s32[8]{0:T(128)} %stack.60.order_ref, bf16[64,512]{1,0:T(8,128)(2,1)} %stream_ref.1, bf16[4096,512]{1,0:T(8,128)(2,1)} %refs_7_.1, bf16[4096,512]{1,0:T(8,128)(2,1)} %refs_7_.1, bf16[4096,512]{1,0:T(8,128)(2,1)} %refs_7_.1, bf16[4096,512]{1,0:T(8,128)(2,1)} %refs_7_.1, bf16[4096,512]{1,0:T(8,128)(2,1)} %refs_7_.1, ...), custom_call_target="tpu_custom_call" | custom-call | tf_op jit(solution)/shard_map/project/pallas_call | solution.py:381
  70.8 1.2 collective-permute-start.16
  71.9 0.8 collective-permute-start.15
  72.8 1.5 collective-permute-start.14
  74.9 1.6 collective-permute-done.16
  76.5 0.9 collective-permute-done.15
  77.4 2.1 convolution_convert_fusion
  79.5 6.9 %widen.4 = bf16[576,1024]{1,0:T(8,128)(2,1)} custom-call(s32[9]{0:T(128)} %get-tuple-element.78.table_ref, bf16[8,96,512]{2,1,0:T(8,128)(2,1)} %bitcast.33, bf16[8,512,2048]{2,1,0:T(8,128)(2,1)} %gate_ref.7, bf16[8,512,2048]{2,1,0:T(8,128)(2,1)} %up_ref.7), custom_call_target="tpu_custom_call" | custom-call | tf_op jit(solution)/shard_map/widen/pallas_call | solution.py:427
  86.4 7.0 %widen.5 = bf16[576,1024]{1,0:T(8,128)(2,1)} custom-call(s32[9]{0:T(128)} %get-tuple-element.76.table_ref, bf16[8,96,512]{2,1,0:T(8,128)(2,1)} %bitcast.34, bf16[8,512,2048]{2,1,0:T(8,128)(2,1)} %gate_ref.7, bf16[8,512,2048]{2,1,0:T(8,128)(2,1)} %up_ref.7), custom_call_target="tpu_custom_call" | custom-call | tf_op jit(solution)/shard_map/widen/pallas_call | solution.py:427
  93.5 1.7 add_convert_fusion.1
  95.4 6.9 %widen.6 = bf16[576,1024]{1,0:T(8,128)(2,1)} custom-call(s32[9]{0:T(128)} %get-tuple-element.77.table_ref, bf16[8,96,512]{2,1,0:T(8,128)(2,1)} %bitcast.35, bf16[8,512,2048]{2,1,0:T(8,128)(2,1)} %gate_ref.7, bf16[8,512,2048]{2,1,0:T(8,128)(2,1)} %up_ref.7), custom_call_target="tpu_custom_call" | custom-call | tf_op jit(solution)/shard_map/widen/pallas_call | solution.py:427
  102.7 0.8 collective-permute-start.27
  103.5 6.9 %widen.7 = bf16[576,1024]{1,0:T(8,128)(2,1)} custom-call(s32[9]{0:T(128)} %get-tuple-element.75.table_ref, bf16[8,96,512]{2,1,0:T(8,128)(2,1)} %bitcast.36, bf16[8,512,2048]{2,1,0:T(8,128)(2,1)} %gate_ref.7, bf16[8,512,2048]{2,1,0:T(8,128)(2,1)} %up_ref.7), custom_call_target="tpu_custom_call" | custom-call | tf_op jit(solution)/shard_map/widen/pallas_call | solution.py:427
  110.4 7.6 %collective-permute-done.27 = bf16[288,1024]{1,0:T(8,128)(2,1)S(1)} collective-permute-done((bf16[288,1024]{1,0:T(8,128)(2,1)S(1)}, bf16[288,1024]{1,0:T(8,128)(2,1)S(1)}, u32[]{:S(2)}, u32[]{:S(2)}) %collective-permute-start.27) | collective-permute-done | bytes 589856 | tf_op jit(solution)/shard_map/ppermute | solution.py:189
  118.2 2.9 %collective-permute-start.28 = (bf16[144,1024]{1,0:T(8,128)(2,1)S(1)}, bf16[144,1024]{1,0:T(8,128)(2,1)S(1)}, u32[]{:S(2)}, u32[]{:S(2)}) collective-permute-start(bf16[144,1024]{1,0:T(8,128)(2,1)S(1)} %constant_dynamic-slice_fusion), channel_id=1, source_target_pairs={{0,6},{1,7},{2,4},{3,5},{4,2},{5,3},{6,0},{7,1},{8,14},{9,15},{10,... | collective-permute-start | bytes 884744 | tf_op jit(solution)/shard_map/ppermute | solution.py:189
  121.8 1.1 collective-permute-start.19
  122.9 1.2 compare_reduce_fusion
  124.2 15.3 %collective-permute-done.22 = f32[2,128]{1,0:T(2,128)S(1)} collective-permute-done((f32[2,128]{1,0:T(2,128)S(1)}, f32[2,128]{1,0:T(2,128)S(1)}, u32[]{:S(2)}, u32[]{:S(2)}) %collective-permute-start.22) | collective-permute-done | bytes 1056 | tf_op jit(solution)/shard_map/ppermute | solution.py:189
  139.4 2.0 collective-permute-start.23
  141.5 16.7 %collective-permute-done.23 = f32[2,128]{1,0:T(2,128)S(1)} collective-permute-done((f32[2,128]{1,0:T(2,128)S(1)}, f32[2,128]{1,0:T(2,128)S(1)}, u32[]{:S(2)}, u32[]{:S(2)}) %collective-permute-start.23) | collective-permute-done | bytes 1056 | tf_op jit(solution)/shard_map/ppermute | solution.py:189
  159.4 2.6 %collective-permute-start.29 = (bf16[144,512]{1,0:T(8,128)(2,1)S(1)}, bf16[144,512]{1,0:T(8,128)(2,1)S(1)}, u32[]{:S(2)}, u32[]{:S(2)}) collective-permute-start(bf16[144,512]{1,0:T(8,128)(2,1)S(1)} %fusion.4), channel_id=1, source_target_pairs={{0,6},{1,7},{2,4},{3,5},{4,2},{5,3},{6,0},{7,1},{8,14},{9,15},{10,... | collective-permute-start | bytes 442376 | tf_op jit(solution)/shard_map/ppermute | solution.py:189
  162.1 5.2 %collective-permute-done.20 = bf16[144,1024]{1,0:T(8,128)(2,1)S(1)} collective-permute-done((bf16[144,1024]{1,0:T(8,128)(2,1)S(1)}, bf16[144,1024]{1,0:T(8,128)(2,1)S(1)}, u32[]{:S(2)}, u32[]{:S(2)}) %collective-permute-start.20) | collective-permute-done | bytes 294944 | tf_op jit(solution)/shard_map/ppermute | solution.py:189
  167.6 1.8 collective-permute-start.24
  169.3 3.4 %collective-permute-done.29 = bf16[144,512]{1,0:T(8,128)(2,1)S(1)} collective-permute-done((bf16[144,512]{1,0:T(8,128)(2,1)S(1)}, bf16[144,512]{1,0:T(8,128)(2,1)S(1)}, u32[]{:S(2)}, u32[]{:S(2)}) %collective-permute-start.29) | collective-permute-done | bytes 147488 | tf_op jit(solution)/shard_map/ppermute | solution.py:189
  173.0 2.1 collective-permute-done.24
  175.4 2.9 %collective-permute-start.25 = (bf16[288,512]{1,0:T(8,128)(2,1)S(1)}, bf16[288,512]{1,0:T(8,128)(2,1)S(1)}, u32[]{:S(2)}, u32[]{:S(2)}) collective-permute-start(bf16[288,512]{1,0:T(8,128)(2,1)S(1)} %pad_maximum_fusion.3), channel_id=1, source_target_pairs={{0,6},{1,7},{2,4},{3,5},{4,2},{5,3},{6,0},{7,1},{8,14},{9,15},{10,... | collective-permute-start | bytes 884744 | tf_op jit(solution)/shard_map/ppermute | solution.py:189
  178.2 4.6 %collective-permute-done.30 = bf16[288,512]{1,0:T(8,128)(2,1)S(1)} collective-permute-done((bf16[288,512]{1,0:T(8,128)(2,1)S(1)}, bf16[288,512]{1,0:T(8,128)(2,1)S(1)}, u32[]{:S(2)}, u32[]{:S(2)}) %collective-permute-start.30) | collective-permute-done | bytes 294944 | tf_op jit(solution)/shard_map/ppermute | solution.py:189
  183.1 3.1 %collective-permute-done.25 = bf16[288,512]{1,0:T(8,128)(2,1)S(1)} collective-permute-done((bf16[288,512]{1,0:T(8,128)(2,1)S(1)}, bf16[288,512]{1,0:T(8,128)(2,1)S(1)}, u32[]{:S(2)}, u32[]{:S(2)}) %collective-permute-start.25) | collective-permute-done | bytes 294944 | tf_op jit(solution)/shard_map/ppermute | solution.py:189
  186.7 1.0 copy.27.scale_ref
  188.3 0.9 fusion.pick_ref
  189.1 0.9 broadcast_in_dim.155.init_ref
  190.1 8.2 %narrow.2.init_ref = f32[256,512]{1,0:T(8,128)} custom-call(s32[10]{0:T(128)} %get-tuple-element.73.table_ref, bf16[576,512]{1,0:T(8,128)(2,1)} %copy-done.2, bf16[576,512]{1,0:T(8,128)(2,1)} %copy-done.6, bf16[8,2048,512]{2,1,0:T(8,128)(2,1)} %far_w_ref.3, bf16[8,2048,512]{2,1,0:T(8,128)(2,1)} %far_w_ref.3, bf16[8,96,256]{2,1,0:T(8,128)(2,1)} %fusion.pick_ref, ...), custom_call_target="tpu_custom_call" | custom-call | tf_op jit(solution)/shard_map/narrow/pallas_call | solution.py:475
  198.3 0.8 copy-done.7
  199.2 8.2 %narrow.3 = f32[256,512]{1,0:T(8,128)} custom-call(s32[10]{0:T(128)} %get-tuple-element.74.table_ref, bf16[576,512]{1,0:T(8,128)(2,1)} %copy-done.3, bf16[576,512]{1,0:T(8,128)(2,1)} %copy-done.7, bf16[8,2048,512]{2,1,0:T(8,128)(2,1)} %far_w_ref.3, bf16[8,2048,512]{2,1,0:T(8,128)(2,1)} %far_w_ref.3, bf16[8,96,256]{2,1,0:T(8,128)(2,1)} %fusion.pick_ref, ...), custom_call_target="tpu_custom_call" | custom-call | tf_op jit(solution)/shard_map/narrow/pallas_call | solution.py:475
  207.3 1.1 convert_element_type.141
  208.4 1.4 collective-permute-start.34
  209.8 1.5 collective-permute-start.33
  212.0 2.0 collective-permute-done.34
  214.0 1.3 collective-permute-done.33
  (136 shorter events, 15.9 us)
Async XLA Ops:
  1.0 6.1 %copy-start.4 = (bf16[64,2048]{1,0:T(8,128)(2,1)}, bf16[64,2048]{1,0:T(8,128)(2,1)S(1)}, u32[]{:S(2)}) copy-start(bf16[64,2048]{1,0:T(8,128)(2,1)S(1)} %constant_dynamic-slice_fusion.14.q_ref) | copy-start | bytes 786436
  1.0 10.2 %collective-permute-start.1 = (bf16[64,2048]{1,0:T(8,128)(2,1)S(1)}, bf16[64,2048]{1,0:T(8,128)(2,1)S(1)}, u32[]{:S(2)}, u32[]{:S(2)}) collective-permute-start(bf16[64,2048]{1,0:T(8,128)(2,1)S(1)} %constant_dynamic-slice_fusion.14.q_ref), channel_id=1, source_target_pairs={{0,8},{8,0},{16,24},{24,16},{1,9},{9,1},{17,25},{25,17},{2,10},{10... | collective-permute-start | bytes 786440 | tf_op jit(solution)/shard_map/ppermute | solution.py:189
  4.0 14.5 %collective-permute-start.3 = (bf16[64,2048]{1,0:T(8,128)(2,1)S(1)}, bf16[64,2048]{1,0:T(8,128)(2,1)S(1)}, u32[]{:S(2)}, u32[]{:S(2)}) collective-permute-start(bf16[64,2048]{1,0:T(8,128)(2,1)S(1)} %constant_dynamic-slice_fusion.14.q_ref), channel_id=1, source_target_pairs={{0,16},{8,24},{16,0},{24,8},{1,17},{9,25},{17,1},{25,9},{2,18},{10... | collective-permute-start | bytes 786440 | tf_op jit(solution)/shard_map/ppermute | solution.py:189
  5.5 19.6 %collective-permute-start.5 = (bf16[64,2048]{1,0:T(8,128)(2,1)S(1)}, bf16[64,2048]{1,0:T(8,128)(2,1)S(1)}, u32[]{:S(2)}, u32[]{:S(2)}) collective-permute-start(bf16[64,2048]{1,0:T(8,128)(2,1)S(1)} %constant_dynamic-slice_fusion.14.q_ref), channel_id=1, source_target_pairs={{0,24},{8,16},{16,8},{24,0},{1,25},{9,17},{17,9},{25,1},{2,26},{10... | collective-permute-start | bytes 786440 | tf_op jit(solution)/shard_map/ppermute | solution.py:189
  6.8 0.7 copy-start.20
  6.8 0.8 copy-start.21
  6.8 0.8 copy-start.23
  6.9 1.2 copy-start.24
  6.9 1.2 copy-start.25
  7.0 4.1 %collective-permute-start = (bf16[512,1024]{1,0:T(8,128)(2,1)S(1)}, bf16[512,1024]{1,0:T(8,128)(2,1)S(1)}, u32[]{:S(2)}, u32[]{:S(2)}) collective-permute-start(bf16[512,1024]{1,0:T(8,128)(2,1)S(1)} %pad_maximum_fusion), channel_id=1, source_target_pairs={{0,1},{1,0},{2,3},{3,2},{4,5},{5,4},{6,7},{7,6},{8,9},{9,8},{10,11... | collective-permute-start | bytes 3145736 | tf_op jit(solution)/shard_map/ppermute | solution.py:189
  11.2 0.7 copy-start.16
  11.2 1.1 copy-start
  16.5 19.3 %collective-permute-start.2 = (bf16[64,2176]{1,0:T(8,128)(2,1)}, bf16[64,2176]{1,0:T(8,128)(2,1)S(1)}, u32[]{:S(2)}, u32[]{:S(2)}) collective-permute-start(bf16[64,2176]{1,0:T(8,128)(2,1)} %attend.5), channel_id=1, source_target_pairs={{0,8},{8,0},{16,24},{24,16},{1,9},{9,1},{17,25},{25,17},{2,10},{10... | collective-permute-start | bytes 835592 | tf_op jit(solution)/shard_map/ppermute | solution.py:189
  18.6 0.7 copy-start.15
  23.6 12.3 %collective-permute-start.4 = (bf16[64,2176]{1,0:T(8,128)(2,1)}, bf16[64,2176]{1,0:T(8,128)(2,1)S(1)}, u32[]{:S(2)}, u32[]{:S(2)}) collective-permute-start(bf16[64,2176]{1,0:T(8,128)(2,1)} %attend.6), channel_id=1, source_target_pairs={{0,16},{8,24},{16,0},{24,8},{1,17},{9,25},{17,1},{25,9},{2,18},{10... | collective-permute-start | bytes 835592 | tf_op jit(solution)/shard_map/ppermute | solution.py:189
  25.1 0.7 copy-start.14
  30.1 7.7 %collective-permute-start.6 = (bf16[64,2176]{1,0:T(8,128)(2,1)}, bf16[64,2176]{1,0:T(8,128)(2,1)S(1)}, u32[]{:S(2)}, u32[]{:S(2)}) collective-permute-start(bf16[64,2176]{1,0:T(8,128)(2,1)} %attend.7), channel_id=1, source_target_pairs={{0,24},{8,16},{16,8},{24,0},{1,25},{9,17},{17,9},{25,1},{2,26},{10... | collective-permute-start | bytes 835592 | tf_op jit(solution)/shard_map/ppermute | solution.py:189
  35.8 2.0 copy-start.8
  35.8 1.9 copy-start.9
  37.8 0.7 copy-start.10
  40.6 4.9 %collective-permute-start.7 = (bf16[64,640]{1,0:T(8,128)(2,1)}, bf16[64,640]{1,0:T(8,128)(2,1)S(1)}, u32[]{:S(2)}, u32[]{:S(2)}) collective-permute-start(bf16[64,640]{1,0:T(8,128)(2,1)} %get-tuple-element.21), channel_id=1, source_target_pairs={{0,2},{1,3},{2,0},{3,1},{4,6},{5,7},{6,4},{7,5},{8,10},{9,11},{10,... | collective-permute-start | bytes 245768 | tf_op jit(solution)/shard_map/ppermute | solution.py:189
  42.2 6.6 %collective-permute-start.8 = (bf16[64,640]{1,0:T(8,128)(2,1)}, bf16[64,640]{1,0:T(8,128)(2,1)S(1)}, u32[]{:S(2)}, u32[]{:S(2)}) collective-permute-start(bf16[64,640]{1,0:T(8,128)(2,1)} %get-tuple-element.22), channel_id=1, source_target_pairs={{0,4},{1,5},{2,6},{3,7},{4,0},{5,1},{6,2},{7,3},{8,12},{9,13},{10,... | collective-permute-start | bytes 245768 | tf_op jit(solution)/shard_map/ppermute | solution.py:189
  44.8 6.4 %collective-permute-start.9 = (bf16[64,640]{1,0:T(8,128)(2,1)}, bf16[64,640]{1,0:T(8,128)(2,1)S(1)}, u32[]{:S(2)}, u32[]{:S(2)}) collective-permute-start(bf16[64,640]{1,0:T(8,128)(2,1)} %get-tuple-element.23), channel_id=1, source_target_pairs={{0,6},{1,7},{2,4},{3,5},{4,2},{5,3},{6,0},{7,1},{8,14},{9,15},{10,... | collective-permute-start | bytes 245768 | tf_op jit(solution)/shard_map/ppermute | solution.py:189
  45.6 5.7 %copy-start.17 = (bf16[64,640]{1,0:T(8,128)(2,1)}, bf16[64,640]{1,0:T(8,128)(2,1)S(1)}, u32[]{:S(2)}) copy-start(bf16[64,640]{1,0:T(8,128)(2,1)S(1)} %collective-permute-done.7.refs_1_) | copy-start | bytes 245764
  48.9 2.4 %copy-start.18 = (bf16[64,640]{1,0:T(8,128)(2,1)}, bf16[64,640]{1,0:T(8,128)(2,1)S(1)}, u32[]{:S(2)}) copy-start(bf16[64,640]{1,0:T(8,128)(2,1)S(1)} %collective-permute-done.8.refs_2_) | copy-start | bytes 245764
  51.3 0.6 copy-start.19
  55.3 4.5 %collective-permute-start.10 = (bf16[64,512]{1,0:T(8,128)(2,1)}, bf16[64,512]{1,0:T(8,128)(2,1)S(1)}, u32[]{:S(2)}, u32[]{:S(2)}) collective-permute-start(bf16[64,512]{1,0:T(8,128)(2,1)} %merge.1.refs_8_), channel_id=1, source_target_pairs={{0,2},{1,3},{2,0},{3,1},{4,6},{5,7},{6,4},{7,5},{8,10},{9,11},{10,... | collective-permute-start | bytes 196616 | tf_op jit(solution)/shard_map/ppermute | solution.py:189
  55.3 5.4 %collective-permute-start.11 = (bf16[64,512]{1,0:T(8,128)(2,1)}, bf16[64,512]{1,0:T(8,128)(2,1)S(1)}, u32[]{:S(2)}, u32[]{:S(2)}) collective-permute-start(bf16[64,512]{1,0:T(8,128)(2,1)} %merge.1.refs_8_), channel_id=1, source_target_pairs={{0,4},{1,5},{2,6},{3,7},{4,0},{5,1},{6,2},{7,3},{8,12},{9,13},{10,... | collective-permute-start | bytes 196616 | tf_op jit(solution)/shard_map/ppermute | solution.py:189
  56.9 6.3 %collective-permute-start.12 = (bf16[64,512]{1,0:T(8,128)(2,1)}, bf16[64,512]{1,0:T(8,128)(2,1)S(1)}, u32[]{:S(2)}, u32[]{:S(2)}) collective-permute-start(bf16[64,512]{1,0:T(8,128)(2,1)} %merge.1.refs_8_), channel_id=1, source_target_pairs={{0,6},{1,7},{2,4},{3,5},{4,2},{5,3},{6,0},{7,1},{8,14},{9,15},{10,... | collective-permute-start | bytes 196616 | tf_op jit(solution)/shard_map/ppermute | solution.py:189
  59.8 6.5 %copy-start.11 = (bf16[64,512]{1,0:T(8,128)(2,1)}, bf16[64,512]{1,0:T(8,128)(2,1)S(1)}, u32[]{:S(2)}) copy-start(bf16[64,512]{1,0:T(8,128)(2,1)S(1)} %collective-permute-done.10.refs_9_) | copy-start | bytes 196612
  60.7 5.6 %copy-start.12 = (bf16[64,512]{1,0:T(8,128)(2,1)}, bf16[64,512]{1,0:T(8,128)(2,1)S(1)}, u32[]{:S(2)}) copy-start(bf16[64,512]{1,0:T(8,128)(2,1)S(1)} %collective-permute-done.11.refs_10_) | copy-start | bytes 196612
  63.1 3.2 %copy-start.13 = (bf16[64,512]{1,0:T(8,128)(2,1)}, bf16[64,512]{1,0:T(8,128)(2,1)S(1)}, u32[]{:S(2)}) copy-start(bf16[64,512]{1,0:T(8,128)(2,1)S(1)} %collective-permute-done.12.refs_11_) | copy-start | bytes 196612
  64.0 1.6 collective-permute-start.13
  66.4 11.1 %copy-start.22 = (f32[512]{0:T(512)S(1)}, f32[512]{0:T(512)}, u32[]{:S(2)}) copy-start(f32[512]{0:T(512)} %param.26) | copy-start | bytes 6148
  70.8 5.7 %collective-permute-start.16 = (bf16[64,512]{1,0:T(8,128)(2,1)}, bf16[64,512]{1,0:T(8,128)(2,1)S(1)}, u32[]{:S(2)}, u32[]{:S(2)}) collective-permute-start(bf16[64,512]{1,0:T(8,128)(2,1)} %project.1), channel_id=1, source_target_pairs={{0,24},{8,16},{16,8},{24,0},{1,25},{9,17},{17,9},{25,1},{2,26},{10... | collective-permute-start | bytes 196616 | tf_op jit(solution)/shard_map/ppermute | solution.py:189
  71.9 5.5 %collective-permute-start.15 = (bf16[64,512]{1,0:T(8,128)(2,1)}, bf16[64,512]{1,0:T(8,128)(2,1)S(1)}, u32[]{:S(2)}, u32[]{:S(2)}) collective-permute-start(bf16[64,512]{1,0:T(8,128)(2,1)} %project.1), channel_id=1, source_target_pairs={{0,16},{8,24},{16,0},{24,8},{1,17},{9,25},{17,1},{25,9},{2,18},{10... | collective-permute-start | bytes 196616 | tf_op jit(solution)/shard_map/ppermute | solution.py:189
  72.8 4.6 %collective-permute-start.14 = (bf16[64,512]{1,0:T(8,128)(2,1)}, bf16[64,512]{1,0:T(8,128)(2,1)S(1)}, u32[]{:S(2)}, u32[]{:S(2)}) collective-permute-start(bf16[64,512]{1,0:T(8,128)(2,1)} %project.1), channel_id=1, source_target_pairs={{0,8},{8,0},{16,24},{24,16},{1,9},{9,1},{17,25},{25,17},{2,10},{10... | collective-permute-start | bytes 196616 | tf_op jit(solution)/shard_map/ppermute | solution.py:189
  86.4 7.1 %collective-permute-start.17 = (bf16[576,1024]{1,0:T(8,128)(2,1)}, bf16[576,1024]{1,0:T(8,128)(2,1)S(1)}, u32[]{:S(2)}, u32[]{:S(2)}) collective-permute-start(bf16[576,1024]{1,0:T(8,128)(2,1)} %widen.4), channel_id=1, source_target_pairs={{0,1},{1,0},{2,3},{3,2},{4,5},{5,4},{6,7},{7,6},{8,9},{9,8},{10,11... | collective-permute-start | bytes 3538952 | tf_op jit(solution)/shard_map/ppermute | solution.py:189
  86.4 7.0 %copy-start.5 = (bf16[64,512]{1,0:T(8,128)(2,1)S(1)}, bf16[64,512]{1,0:T(8,128)(2,1)}, u32[]{:S(2)}) copy-start(bf16[64,512]{1,0:T(8,128)(2,1)} %project.1) | copy-start | bytes 196612
  102.2 18.9 %collective-permute-start.18 = (bf16[576,1024]{1,0:T(8,128)(2,1)}, bf16[576,1024]{1,0:T(8,128)(2,1)S(1)}, u32[]{:S(2)}, u32[]{:S(2)}) collective-permute-start(bf16[576,1024]{1,0:T(8,128)(2,1)} %widen.6), channel_id=1, source_target_pairs={{0,1},{1,0},{2,3},{3,2},{4,5},{5,4},{6,7},{7,6},{8,9},{9,8},{10,11... | collective-permute-start | bytes 3538952 | tf_op jit(solution)/shard_map/ppermute | solution.py:189
  102.7 15.2 %collective-permute-start.27 = (bf16[288,1024]{1,0:T(8,128)(2,1)S(1)}, bf16[288,1024]{1,0:T(8,128)(2,1)S(1)}, u32[]{:S(2)}, u32[]{:S(2)}) collective-permute-start(bf16[288,1024]{1,0:T(8,128)(2,1)S(1)} %get-tuple-element.34), channel_id=1, source_target_pairs={{0,2},{1,3},{2,0},{3,1},{4,6},{5,7},{6,4},{7,5},{8,10},{9,11},{10,... | collective-permute-start | bytes 1769480 | tf_op jit(solution)/shard_map/ppermute | solution.py:189
  110.4 10.7 %copy-start.1 = (bf16[576,1024]{1,0:T(8,128)(2,1)S(1)}, bf16[576,1024]{1,0:T(8,128)(2,1)}, u32[]{:S(2)}) copy-start(bf16[576,1024]{1,0:T(8,128)(2,1)} %widen.7) | copy-start | bytes 3538948
  118.2 23.2 %collective-permute-start.28 = (bf16[144,1024]{1,0:T(8,128)(2,1)S(1)}, bf16[144,1024]{1,0:T(8,128)(2,1)S(1)}, u32[]{:S(2)}, u32[]{:S(2)}) collective-permute-start(bf16[144,1024]{1,0:T(8,128)(2,1)S(1)} %constant_dynamic-slice_fusion), channel_id=1, source_target_pairs={{0,6},{1,7},{2,4},{3,5},{4,2},{5,3},{6,0},{7,1},{8,14},{9,15},{10,... | collective-permute-start | bytes 884744 | tf_op jit(solution)/shard_map/ppermute | solution.py:189
  121.7 1.2 collective-permute-start.21
  121.8 36.5 %collective-permute-start.19 = (bf16[288,1024]{1,0:T(8,128)(2,1)S(1)}, bf16[288,1024]{1,0:T(8,128)(2,1)S(1)}, u32[]{:S(2)}, u32[]{:S(2)}) collective-permute-start(bf16[288,1024]{1,0:T(8,128)(2,1)S(1)} %get-tuple-element.31), channel_id=1, source_target_pairs={{0,6},{1,7},{2,4},{3,5},{4,2},{5,3},{6,0},{7,1},{8,14},{9,15},{10,... | collective-permute-start | bytes 1769480 | tf_op jit(solution)/shard_map/ppermute | solution.py:189
  122.9 16.5 %collective-permute-start.22 = (f32[2,128]{1,0:T(2,128)S(1)}, f32[2,128]{1,0:T(2,128)S(1)}, u32[]{:S(2)}, u32[]{:S(2)}) collective-permute-start(f32[2,128]{1,0:T(2,128)S(1)} %add.220), channel_id=1, source_target_pairs={{0,2},{1,3},{2,0},{3,1},{4,6},{5,7},{6,4},{7,5},{8,10},{9,11},{10,... | collective-permute-start | bytes 3080 | tf_op jit(solution)/shard_map/ppermute | solution.py:189
  139.4 18.8 %collective-permute-start.23 = (f32[2,128]{1,0:T(2,128)S(1)}, f32[2,128]{1,0:T(2,128)S(1)}, u32[]{:S(2)}, u32[]{:S(2)}) collective-permute-start(f32[2,128]{1,0:T(2,128)S(1)} %add.221), channel_id=1, source_target_pairs={{0,4},{1,5},{2,6},{3,7},{4,0},{5,1},{6,2},{7,3},{8,12},{9,13},{10,... | collective-permute-start | bytes 3080 | tf_op jit(solution)/shard_map/ppermute | solution.py:189
  158.5 8.8 %collective-permute-start.20 = (bf16[144,1024]{1,0:T(8,128)(2,1)S(1)}, bf16[144,1024]{1,0:T(8,128)(2,1)S(1)}, u32[]{:S(2)}, u32[]{:S(2)}) collective-permute-start(bf16[144,1024]{1,0:T(8,128)(2,1)S(1)} %constant_dynamic-slice_fusion.5), channel_id=1, source_target_pairs={{0,2},{1,3},{2,0},{3,1},{4,6},{5,7},{6,4},{7,5},{8,10},{9,11},{10,... | collective-permute-start | bytes 884744 | tf_op jit(solution)/shard_map/ppermute | solution.py:189
  159.4 13.3 %collective-permute-start.29 = (bf16[144,512]{1,0:T(8,128)(2,1)S(1)}, bf16[144,512]{1,0:T(8,128)(2,1)S(1)}, u32[]{:S(2)}, u32[]{:S(2)}) collective-permute-start(bf16[144,512]{1,0:T(8,128)(2,1)S(1)} %fusion.4), channel_id=1, source_target_pairs={{0,6},{1,7},{2,4},{3,5},{4,2},{5,3},{6,0},{7,1},{8,14},{9,15},{10,... | collective-permute-start | bytes 442376 | tf_op jit(solution)/shard_map/ppermute | solution.py:189
  167.6 7.6 %collective-permute-start.24 = (bf16[144,512]{1,0:T(8,128)(2,1)S(1)}, bf16[144,512]{1,0:T(8,128)(2,1)S(1)}, u32[]{:S(2)}, u32[]{:S(2)}) collective-permute-start(bf16[144,512]{1,0:T(8,128)(2,1)S(1)} %fusion.6), channel_id=1, source_target_pairs={{0,2},{1,3},{2,0},{3,1},{4,6},{5,7},{6,4},{7,5},{8,10},{9,11},{10,... | collective-permute-start | bytes 442376 | tf_op jit(solution)/shard_map/ppermute | solution.py:189
  173.0 9.9 %collective-permute-start.30 = (bf16[288,512]{1,0:T(8,128)(2,1)S(1)}, bf16[288,512]{1,0:T(8,128)(2,1)S(1)}, u32[]{:S(2)}, u32[]{:S(2)}) collective-permute-start(bf16[288,512]{1,0:T(8,128)(2,1)S(1)} %pad_maximum_fusion.4), channel_id=1, source_target_pairs={{0,2},{1,3},{2,0},{3,1},{4,6},{5,7},{6,4},{7,5},{8,10},{9,11},{10,... | collective-permute-start | bytes 884744 | tf_op jit(solution)/shard_map/ppermute | solution.py:189
  175.4 10.9 %collective-permute-start.25 = (bf16[288,512]{1,0:T(8,128)(2,1)S(1)}, bf16[288,512]{1,0:T(8,128)(2,1)S(1)}, u32[]{:S(2)}, u32[]{:S(2)}) collective-permute-start(bf16[288,512]{1,0:T(8,128)(2,1)S(1)} %pad_maximum_fusion.3), channel_id=1, source_target_pairs={{0,6},{1,7},{2,4},{3,5},{4,2},{5,3},{6,0},{7,1},{8,14},{9,15},{10,... | collective-permute-start | bytes 884744 | tf_op jit(solution)/shard_map/ppermute | solution.py:189
  183.0 3.4 %copy-start.2 = (bf16[576,512]{1,0:T(8,128)(2,1)}, bf16[576,512]{1,0:T(8,128)(2,1)S(1)}, u32[]{:S(2)}) copy-start(bf16[576,512]{1,0:T(8,128)(2,1)S(1)} %pad_maximum_fusion.2.own_ref) | copy-start | bytes 1769476
  183.0 6.1 %collective-permute-start.31 = (bf16[576,512]{1,0:T(8,128)(2,1)S(1)}, bf16[576,512]{1,0:T(8,128)(2,1)S(1)}, u32[]{:S(2)}, u32[]{:S(2)}) collective-permute-start(bf16[576,512]{1,0:T(8,128)(2,1)S(1)} %pad_maximum_fusion.2.own_ref), channel_id=1, source_target_pairs={{0,1},{1,0},{2,3},{3,2},{4,5},{5,4},{6,7},{7,6},{8,9},{9,8},{10,11... | collective-permute-start | bytes 1769480 | tf_op jit(solution)/shard_map/ppermute | solution.py:189
  186.4 11.9 %copy-start.3 = (bf16[576,512]{1,0:T(8,128)(2,1)}, bf16[576,512]{1,0:T(8,128)(2,1)S(1)}, u32[]{:S(2)}) copy-start(bf16[576,512]{1,0:T(8,128)(2,1)S(1)} %pad_maximum_fusion.1.own_ref) | copy-start | bytes 1769476
  186.4 11.9 %collective-permute-start.26 = (bf16[576,512]{1,0:T(8,128)(2,1)S(1)}, bf16[576,512]{1,0:T(8,128)(2,1)S(1)}, u32[]{:S(2)}, u32[]{:S(2)}) collective-permute-start(bf16[576,512]{1,0:T(8,128)(2,1)S(1)} %pad_maximum_fusion.1.own_ref), channel_id=1, source_target_pairs={{0,1},{1,0},{2,3},{3,2},{4,5},{5,4},{6,7},{7,6},{8,9},{9,8},{10,11... | collective-permute-start | bytes 1769480 | tf_op jit(solution)/shard_map/ppermute | solution.py:189
  189.1 1.0 copy-start.6
  198.3 0.8 copy-start.7
  208.4 5.6 %collective-permute-start.34 = (bf16[64,512]{1,0:T(8,128)(2,1)S(1)}, bf16[64,512]{1,0:T(8,128)(2,1)S(1)}, u32[]{:S(2)}, u32[]{:S(2)}) collective-permute-start(bf16[64,512]{1,0:T(8,128)(2,1)S(1)} %get-tuple-element.59), channel_id=1, source_target_pairs={{0,24},{8,16},{16,8},{24,0},{1,25},{9,17},{17,9},{25,1},{2,26},{10... | collective-permute-start | bytes 196616 | tf_op jit(solution)/shard_map/ppermute | solution.py:189
  209.8 5.5 %collective-permute-start.33 = (bf16[64,512]{1,0:T(8,128)(2,1)S(1)}, bf16[64,512]{1,0:T(8,128)(2,1)S(1)}, u32[]{:S(2)}, u32[]{:S(2)}) collective-permute-start(bf16[64,512]{1,0:T(8,128)(2,1)S(1)} %get-tuple-element.60), channel_id=1, source_target_pairs={{0,16},{8,24},{16,0},{24,8},{1,17},{9,25},{17,1},{25,9},{2,18},{10... | collective-permute-start | bytes 196616 | tf_op jit(solution)/shard_map/ppermute | solution.py:189
  211.3 4.3 %collective-permute-start.32 = (bf16[64,512]{1,0:T(8,128)(2,1)S(1)}, bf16[64,512]{1,0:T(8,128)(2,1)S(1)}, u32[]{:S(2)}, u32[]{:S(2)}) collective-permute-start(bf16[64,512]{1,0:T(8,128)(2,1)S(1)} %get-tuple-element.58), channel_id=1, source_target_pairs={{0,8},{8,0},{16,24},{24,16},{1,9},{9,1},{17,25},{25,17},{2,10},{10... | collective-permute-start | bytes 196616 | tf_op jit(solution)/shard_map/ppermute | solution.py:189

commit v3 on v2

--- a/solution.py
+++ b/solution.py
@@ -646,16 +646,18 @@
             jnp.concatenate([as_vector(2 * chunk + side), starts]) for side in (1 - core, core)
         ]
         away = widen(tables[0], rows_in, w_gate, w_up, parts, slots)
-        rows_in, away = lax.optimization_barrier((rows_in, away))
+        if chunk == 0:
+            squares = squares + flip(squares, "gy", n_gy, 1)
+        rows_in, away, squares = lax.optimization_barrier((rows_in, away, squares))
         seen = flip(away, "gy", n_gy, 1)
         keep = widen(tables[1], rows_in, w_gate, w_up, parts, slots)
+        if chunk == 0:
+            squares = squares + sum(flip(squares, "gy", n_gy, bit) for bit in (2, 4, 6))
         part = rounded(keep, seen)
         send = take_block(part, 1 - half_id, slots // 2, 0)
         keep = take_block(part, half_id, slots // 2, 0)
         rows_in, send, keep, squares = lax.optimization_barrier((rows_in, send, keep, squares))
         halves.append((keep, flip(send, "gy", n_gy, half_bit)))
-    for bit in (1, 2, 4):
-        squares = squares + flip(squares, "gy", n_gy, bit)
     rstd = 1.0 / jnp.sqrt(squares.reshape(-1) / D + EPSILON)
     hidden = []
     for chunk, (keep, seen) in enumerate(halves):
@@ -669,6 +671,9 @@
         up = part[:, width:] * row_rstd
         hidden.append((jax.nn.silu(gate) * up).astype(jnp.bfloat16))
     total = jnp.zeros((tokens, w_down.shape[2]), f32)
+    hidden[0], row_pick, row_weight, total = lax.optimization_barrier(
+        (hidden[0], row_pick, row_weight, total)
+    )
     for chunk, part in enumerate(hidden):
         for index, bit in routes_z[chunk % 2][::-1]:
             seen = flip(part, "gy", n_gy, bit)

time: 217 us -> 223 us (1.028)
  starting transfers between devices: 39.5 us -> 59.2 us
  waiting for transfers between devices: 78.2 us -> 63.8 us
    ppermute x35 -> x36, starting transfers between devices: 39.5 us -> 59.2 us  [flip(): return lax.ppermute(value, axis, [(i, i ^ bit) for i in range(size)])]
    ppermute x35 -> x36, waiting for transfers between devices: 78.2 us -> 63.8 us  [flip(): return lax.ppermute(value, axis, [(i, i ^ bit) for i in range(size)])]
  transfers between devices with their start and end apart: 35 -> 36, of which waited for: 21 -> 20; matrix products, arithmetic and copies ran while one was open for 6% -> 7% of each run, Pallas kernels for 18% -> 21%
where the time goes in v3:
time: 223 us; the launch traced here: 222 us
  Pallas kernels  71.1 us (32%)
  waiting for transfers between devices  63.8 us (29%)
  starting transfers between devices  59.2 us (27%)
  other arithmetic  13.4 us (6%)
  local copies, waits for them, and re-layouts  11.8 us (5%)
  matrix products  2.3 us (1%)
    ppermute x36, waiting for transfers between devices, flip(): return lax.ppermute(value, axis, [(i, i ^ bit) for i in range(size)])  63.8 us
    ppermute x36, starting transfers between devices, flip(): return lax.ppermute(value, axis, [(i, i ^ bit) for i in range(size)])  59.2 us
    pallas_call x4, Pallas kernels, widen(): pl.pallas_call(widen_kernel, grid_spec=pltpu.PrefetchScalarGridSpec(num_s...  27.4 us
    pallas_call x4, Pallas kernels, attend(): pl.pallas_call(attend_kernel, grid_spec=pltpu.PrefetchScalarGridSpec(num_...  17.2 us
    pallas_call x2, Pallas kernels, narrow(): pl.pallas_call(narrow_kernel, grid_spec=pltpu.PrefetchScalarGridSpec(num_...  16.4 us
    unnamed x52, local copies, waits for them, and re-layouts  5.18 us
  transfers between devices with their start and end apart: 36, of which 20 were waited for; matrix products, arithmetic and copies ran while one was open for 7% of the time, Pallas kernels for 21%

profile of v3, /device:TPU:0, one launch (start us, length us, event | category | flops | bytes accessed | tf_op | source)
XLA Modules:
  0.0 222.1 jit_solution(4404528883459637081)
XLA Ops:
  0.0 1.0 constant_dynamic-slice_fusion.14.q_ref
  1.0 3.0 %collective-permute-start.1 = (bf16[64,2048]{1,0:T(8,128)(2,1)S(1)}, bf16[64,2048]{1,0:T(8,128)(2,1)S(1)}, u32[]{:S(2)}, u32[]{:S(2)}) collective-permute-start(bf16[64,2048]{1,0:T(8,128)(2,1)S(1)} %constant_dynamic-slice_fusion.14.q_ref), channel_id=1, source_target_pairs={{0,8},{8,0},{16,24},{24,16},{1,9},{9,1},{17,25},{25,17},{2,10},{10... | collective-permute-start | bytes 786440 | tf_op jit(solution)/shard_map/ppermute | solution.py:189
  4.0 1.5 collective-permute-start.3
  5.6 1.3 dynamic-slice_bitcast_fusion
  8.5 2.7 %collective-permute-done.1.q_ref = bf16[64,2048]{1,0:T(8,128)(2,1)S(1)} collective-permute-done((bf16[64,2048]{1,0:T(8,128)(2,1)S(1)}, bf16[64,2048]{1,0:T(8,128)(2,1)S(1)}, u32[]{:S(2)}, u32[]{:S(2)}) %collective-permute-start.1) | collective-permute-done | bytes 262176 | tf_op jit(solution)/shard_map/ppermute | solution.py:189
  12.3 4.3 %attend.5 = bf16[64,2176]{1,0:T(8,128)(2,1)} custom-call(s32[1]{0:T(128)} %bitcast.12.core_ref, bf16[64,2048]{1,0:T(8,128)(2,1)} %copy-done.16, bf16[1,512,1024]{2,1,0:T(8,128)(2,1)} %k_own_ref.7, bf16[1,512,1024]{2,1,0:T(8,128)(2,1)} %v_own_ref.7, bf16[512,1024]{1,0:T(8,128)(2,1)} %copy-done, bf16[512,1024]{1,0:T(8,128)(2,1)} %copy-done), custom_call_target="tpu_custom_call" | custom-call | tf_op jit(solution)/shard_map/attend/pallas_call | solution.py:252
  16.6 2.0 collective-permute-start.2
  19.3 4.3 %attend.6 = bf16[64,2176]{1,0:T(8,128)(2,1)} custom-call(s32[1]{0:T(128)} %bitcast.12.core_ref, bf16[64,2048]{1,0:T(8,128)(2,1)} %copy-done.15, bf16[1,512,1024]{2,1,0:T(8,128)(2,1)} %k_own_ref.7, bf16[1,512,1024]{2,1,0:T(8,128)(2,1)} %v_own_ref.7, bf16[512,1024]{1,0:T(8,128)(2,1)} %copy-done, bf16[512,1024]{1,0:T(8,128)(2,1)} %copy-done), custom_call_target="tpu_custom_call" | custom-call | tf_op jit(solution)/shard_map/attend/pallas_call | solution.py:252
  23.6 1.5 collective-permute-start.4
  25.8 4.3 %attend.7 = bf16[64,2176]{1,0:T(8,128)(2,1)} custom-call(s32[1]{0:T(128)} %bitcast.12.core_ref, bf16[64,2048]{1,0:T(8,128)(2,1)} %copy-done.14, bf16[1,512,1024]{2,1,0:T(8,128)(2,1)} %k_own_ref.7, bf16[1,512,1024]{2,1,0:T(8,128)(2,1)} %v_own_ref.7, bf16[512,1024]{1,0:T(8,128)(2,1)} %copy-done, bf16[512,1024]{1,0:T(8,128)(2,1)} %copy-done), custom_call_target="tpu_custom_call" | custom-call | tf_op jit(solution)/shard_map/attend/pallas_call | solution.py:252
  31.6 4.3 %attend.4.a_ref = bf16[64,2176]{1,0:T(8,128)(2,1)} custom-call(s32[1]{0:T(128)} %bitcast.12.core_ref, bf16[64,2048]{1,0:T(8,128)(2,1)} %copy-done.4, bf16[1,512,1024]{2,1,0:T(8,128)(2,1)} %k_own_ref.7, bf16[1,512,1024]{2,1,0:T(8,128)(2,1)} %v_own_ref.7, bf16[512,1024]{1,0:T(8,128)(2,1)} %copy-done, bf16[512,1024]{1,0:T(8,128)(2,1)} %copy-done), custom_call_target="tpu_custom_call" | custom-call | tf_op jit(solution)/shard_map/attend/pallas_call | solution.py:252
  35.9 1.9 collective-permute-done.6.d_ref
  38.6 2.2 choose.1
  40.7 1.6 collective-permute-start.7
  42.3 2.6 %collective-permute-start.8 = (bf16[64,640]{1,0:T(8,128)(2,1)}, bf16[64,640]{1,0:T(8,128)(2,1)S(1)}, u32[]{:S(2)}, u32[]{:S(2)}) collective-permute-start(bf16[64,640]{1,0:T(8,128)(2,1)} %get-tuple-element.28), channel_id=1, source_target_pairs={{0,4},{1,5},{2,6},{3,7},{4,0},{5,1},{6,2},{7,3},{8,12},{9,13},{10,... | collective-permute-start | bytes 245768 | tf_op jit(solution)/shard_map/ppermute | solution.py:189
  45.8 3.2 %collective-permute-done.8.refs_2_ = bf16[64,640]{1,0:T(8,128)(2,1)S(1)} collective-permute-done((bf16[64,640]{1,0:T(8,128)(2,1)}, bf16[64,640]{1,0:T(8,128)(2,1)S(1)}, u32[]{:S(2)}, u32[]{:S(2)}) %collective-permute-start.8) | collective-permute-done | bytes 81952 | tf_op jit(solution)/shard_map/ppermute | solution.py:189
  49.0 2.4 %collective-permute-done.9.refs_3_ = bf16[64,640]{1,0:T(8,128)(2,1)S(1)} collective-permute-done((bf16[64,640]{1,0:T(8,128)(2,1)}, bf16[64,640]{1,0:T(8,128)(2,1)S(1)}, u32[]{:S(2)}, u32[]{:S(2)}) %collective-permute-start.9) | collective-permute-done | bytes 81952 | tf_op jit(solution)/shard_map/ppermute | solution.py:189
  52.0 3.4 %merge.1.refs_8_ = bf16[64,512]{1,0:T(8,128)(2,1)} custom-call(s32[2]{0:T(128)} %pad_add_fusion.1.place_ref, f32[64,64]{1,0:T(8,128)} %fusion.10.mask_ref, bf16[64,4096]{1,0:T(8,128)(2,1)} %q_ref.1, bf16[64,1024]{1,0:T(8,128)(2,1)} %k_ref.1, bf16[64,1024]{1,0:T(8,128)(2,1)} %v_ref.1, bf16[64,640]{1,0:T(8,128)(2,1)} %get-tuple-element.26.refs_0_, ...), custom_call_target="tpu_custom_call" | custom-call | tf_op jit(solution)/shard_map/merge/pallas_call | solution.py:351
  55.4 1.5 collective-permute-start.11
  57.0 2.8 %collective-permute-start.12 = (bf16[64,512]{1,0:T(8,128)(2,1)}, bf16[64,512]{1,0:T(8,128)(2,1)S(1)}, u32[]{:S(2)}, u32[]{:S(2)}) collective-permute-start(bf16[64,512]{1,0:T(8,128)(2,1)} %merge.1.refs_8_), channel_id=1, source_target_pairs={{0,6},{1,7},{2,4},{3,5},{4,2},{5,3},{6,0},{7,1},{8,14},{9,15},{10,... | collective-permute-start | bytes 196616 | tf_op jit(solution)/shard_map/ppermute | solution.py:189
  59.9 0.9 collective-permute-done.11.refs_10_
  60.8 2.4 %collective-permute-done.12.refs_11_ = bf16[64,512]{1,0:T(8,128)(2,1)S(1)} collective-permute-done((bf16[64,512]{1,0:T(8,128)(2,1)}, bf16[64,512]{1,0:T(8,128)(2,1)S(1)}, u32[]{:S(2)}, u32[]{:S(2)}) %collective-permute-start.12) | collective-permute-done | bytes 65568 | tf_op jit(solution)/shard_map/ppermute | solution.py:189
  63.2 0.9 pad_maximum_fusion.5
  66.5 4.4 %project.1 = bf16[64,512]{1,0:T(8,128)(2,1)} custom-call(s32[8]{0:T(128)} %stack.60.order_ref, bf16[64,512]{1,0:T(8,128)(2,1)} %stream_ref.1, bf16[4096,512]{1,0:T(8,128)(2,1)} %refs_7_.1, bf16[4096,512]{1,0:T(8,128)(2,1)} %refs_7_.1, bf16[4096,512]{1,0:T(8,128)(2,1)} %refs_7_.1, bf16[4096,512]{1,0:T(8,128)(2,1)} %refs_7_.1, bf16[4096,512]{1,0:T(8,128)(2,1)} %refs_7_.1, ...), custom_call_target="tpu_custom_call" | custom-call | tf_op jit(solution)/shard_map/project/pallas_call | solution.py:381
  70.9 1.2 collective-permute-start.16
  72.0 0.8 collective-permute-start.15
  72.9 1.5 collective-permute-start.14
  75.0 1.6 collective-permute-done.16
  76.6 0.9 collective-permute-done.15
  77.5 1.0 fusion.2
  78.6 2.1 convolution_convert_fusion
  80.7 6.9 %widen.4 = bf16[576,1024]{1,0:T(8,128)(2,1)} custom-call(s32[9]{0:T(128)} %get-tuple-element.90.table_ref, bf16[8,96,512]{2,1,0:T(8,128)(2,1)} %bitcast.34, bf16[8,512,2048]{2,1,0:T(8,128)(2,1)} %gate_ref.7, bf16[8,512,2048]{2,1,0:T(8,128)(2,1)} %up_ref.7), custom_call_target="tpu_custom_call" | custom-call | tf_op jit(solution)/shard_map/widen/pallas_call | solution.py:427
  88.1 2.8 %collective-permute-start.21 = (f32[2,128]{1,0:T(2,128)S(1)}, f32[2,128]{1,0:T(2,128)S(1)}, u32[]{:S(2)}, u32[]{:S(2)}) collective-permute-start(f32[2,128]{1,0:T(2,128)S(1)} %bitcast_add_fusion), channel_id=1, source_target_pairs={{0,6},{1,7},{2,4},{3,5},{4,2},{5,3},{6,0},{7,1},{8,14},{9,15},{10,... | collective-permute-start | bytes 3080 | tf_op jit(solution)/shard_map/ppermute | solution.py:189
  91.0 1.5 collective-permute-start.20
  92.5 6.9 %widen.5 = bf16[576,1024]{1,0:T(8,128)(2,1)} custom-call(s32[9]{0:T(128)} %get-tuple-element.88.table_ref, bf16[8,96,512]{2,1,0:T(8,128)(2,1)} %bitcast.35, bf16[8,512,2048]{2,1,0:T(8,128)(2,1)} %gate_ref.7, bf16[8,512,2048]{2,1,0:T(8,128)(2,1)} %up_ref.7), custom_call_target="tpu_custom_call" | custom-call | tf_op jit(solution)/shard_map/widen/pallas_call | solution.py:427
  99.4 1.7 add_convert_fusion.1
  101.2 6.9 %widen.6 = bf16[576,1024]{1,0:T(8,128)(2,1)} custom-call(s32[9]{0:T(128)} %get-tuple-element.89.table_ref, bf16[8,96,512]{2,1,0:T(8,128)(2,1)} %bitcast.36, bf16[8,512,2048]{2,1,0:T(8,128)(2,1)} %gate_ref.7, bf16[8,512,2048]{2,1,0:T(8,128)(2,1)} %up_ref.7), custom_call_target="tpu_custom_call" | custom-call | tf_op jit(solution)/shard_map/widen/pallas_call | solution.py:427
  108.6 1.0 compare_reduce_fusion
  109.6 0.8 fusion.pick_ref
  110.4 6.9 %widen.7 = bf16[576,1024]{1,0:T(8,128)(2,1)} custom-call(s32[9]{0:T(128)} %get-tuple-element.87.table_ref, bf16[8,96,512]{2,1,0:T(8,128)(2,1)} %bitcast.37, bf16[8,512,2048]{2,1,0:T(8,128)(2,1)} %gate_ref.7, bf16[8,512,2048]{2,1,0:T(8,128)(2,1)} %up_ref.7), custom_call_target="tpu_custom_call" | custom-call | tf_op jit(solution)/shard_map/widen/pallas_call | solution.py:427
  117.3 6.5 %collective-permute-done.28 = bf16[288,1024]{1,0:T(8,128)(2,1)S(1)} collective-permute-done((bf16[288,1024]{1,0:T(8,128)(2,1)S(1)}, bf16[288,1024]{1,0:T(8,128)(2,1)S(1)}, u32[]{:S(2)}, u32[]{:S(2)}) %collective-permute-start.28) | collective-permute-done | bytes 589856 | tf_op jit(solution)/shard_map/ppermute | solution.py:189
  124.1 2.9 %collective-permute-start.29 = (bf16[144,1024]{1,0:T(8,128)(2,1)S(1)}, bf16[144,1024]{1,0:T(8,128)(2,1)S(1)}, u32[]{:S(2)}, u32[]{:S(2)}) collective-permute-start(bf16[144,1024]{1,0:T(8,128)(2,1)S(1)} %constant_dynamic-slice_fusion.4), channel_id=1, source_target_pairs={{0,6},{1,7},{2,4},{3,5},{4,2},{5,3},{6,0},{7,1},{8,14},{9,15},{10,... | collective-permute-start | bytes 884744 | tf_op jit(solution)/shard_map/ppermute | solution.py:189
  127.6 1.1 collective-permute-start.23
  128.8 7.1 %collective-permute-done.29 = bf16[144,1024]{1,0:T(8,128)(2,1)S(1)} collective-permute-done((bf16[144,1024]{1,0:T(8,128)(2,1)S(1)}, bf16[144,1024]{1,0:T(8,128)(2,1)S(1)}, u32[]{:S(2)}, u32[]{:S(2)}) %collective-permute-start.29) | collective-permute-done | bytes 294944 | tf_op jit(solution)/shard_map/ppermute | solution.py:189
  136.0 11.3 %collective-permute-done.23 = bf16[288,1024]{1,0:T(8,128)(2,1)S(1)} collective-permute-done((bf16[288,1024]{1,0:T(8,128)(2,1)S(1)}, bf16[288,1024]{1,0:T(8,128)(2,1)S(1)}, u32[]{:S(2)}, u32[]{:S(2)}) %collective-permute-start.23) | collective-permute-done | bytes 589856 | tf_op jit(solution)/shard_map/ppermute | solution.py:189
  147.5 17.9 %collective-permute-start.24 = (bf16[144,1024]{1,0:T(8,128)(2,1)S(1)}, bf16[144,1024]{1,0:T(8,128)(2,1)S(1)}, u32[]{:S(2)}, u32[]{:S(2)}) collective-permute-start(bf16[144,1024]{1,0:T(8,128)(2,1)S(1)} %constant_dynamic-slice_fusion.5), channel_id=1, source_target_pairs={{0,2},{1,3},{2,0},{3,1},{4,6},{5,7},{6,4},{7,5},{8,10},{9,11},{10,... | collective-permute-start | bytes 884744 | tf_op jit(solution)/shard_map/ppermute | solution.py:189
  165.7 2.7 %collective-permute-start.30 = (bf16[144,512]{1,0:T(8,128)(2,1)S(1)}, bf16[144,512]{1,0:T(8,128)(2,1)S(1)}, u32[]{:S(2)}, u32[]{:S(2)}) collective-permute-start(bf16[144,512]{1,0:T(8,128)(2,1)S(1)} %fusion.4), channel_id=1, source_target_pairs={{0,6},{1,7},{2,4},{3,5},{4,2},{5,3},{6,0},{7,1},{8,14},{9,15},{10,... | collective-permute-start | bytes 442376 | tf_op jit(solution)/shard_map/ppermute | solution.py:189
  168.4 4.4 %collective-permute-done.24 = bf16[144,1024]{1,0:T(8,128)(2,1)S(1)} collective-permute-done((bf16[144,1024]{1,0:T(8,128)(2,1)S(1)}, bf16[144,1024]{1,0:T(8,128)(2,1)S(1)}, u32[]{:S(2)}, u32[]{:S(2)}) %collective-permute-start.24) | collective-permute-done | bytes 294944 | tf_op jit(solution)/shard_map/ppermute | solution.py:189
  173.1 2.5 %collective-permute-start.25 = (bf16[144,512]{1,0:T(8,128)(2,1)S(1)}, bf16[144,512]{1,0:T(8,128)(2,1)S(1)}, u32[]{:S(2)}, u32[]{:S(2)}) collective-permute-start(bf16[144,512]{1,0:T(8,128)(2,1)S(1)} %fusion.6), channel_id=1, source_target_pairs={{0,2},{1,3},{2,0},{3,1},{4,6},{5,7},{6,4},{7,5},{8,10},{9,11},{10,... | collective-permute-start | bytes 442376 | tf_op jit(solution)/shard_map/ppermute | solution.py:189
  175.6 3.5 %collective-permute-done.30 = bf16[144,512]{1,0:T(8,128)(2,1)S(1)} collective-permute-done((bf16[144,512]{1,0:T(8,128)(2,1)S(1)}, bf16[144,512]{1,0:T(8,128)(2,1)S(1)}, u32[]{:S(2)}, u32[]{:S(2)}) %collective-permute-start.30) | collective-permute-done | bytes 147488 | tf_op jit(solution)/shard_map/ppermute | solution.py:189
  179.2 1.7 collective-permute-done.25
  181.2 2.3 %collective-permute-start.26 = (bf16[288,512]{1,0:T(8,128)(2,1)S(1)}, bf16[288,512]{1,0:T(8,128)(2,1)S(1)}, u32[]{:S(2)}, u32[]{:S(2)}) collective-permute-start(bf16[288,512]{1,0:T(8,128)(2,1)S(1)} %pad_maximum_fusion.3), channel_id=1, source_target_pairs={{0,6},{1,7},{2,4},{3,5},{4,2},{5,3},{6,0},{7,1},{8,14},{9,15},{10,... | collective-permute-start | bytes 884744 | tf_op jit(solution)/shard_map/ppermute | solution.py:189
  183.5 4.5 %collective-permute-done.31 = bf16[288,512]{1,0:T(8,128)(2,1)S(1)} collective-permute-done((bf16[288,512]{1,0:T(8,128)(2,1)S(1)}, bf16[288,512]{1,0:T(8,128)(2,1)S(1)}, u32[]{:S(2)}, u32[]{:S(2)}) %collective-permute-start.31) | collective-permute-done | bytes 294944 | tf_op jit(solution)/shard_map/ppermute | solution.py:189
  188.2 4.9 %collective-permute-done.26 = bf16[288,512]{1,0:T(8,128)(2,1)S(1)} collective-permute-done((bf16[288,512]{1,0:T(8,128)(2,1)S(1)}, bf16[288,512]{1,0:T(8,128)(2,1)S(1)}, u32[]{:S(2)}, u32[]{:S(2)}) %collective-permute-start.26) | collective-permute-done | bytes 294944 | tf_op jit(solution)/shard_map/ppermute | solution.py:189
  194.0 1.0 copy.27.scale_ref
  195.0 0.9 broadcast_in_dim.155.init_ref
  196.0 8.2 %narrow.2.init_ref = f32[256,512]{1,0:T(8,128)} custom-call(s32[10]{0:T(128)} %get-tuple-element.85.table_ref, bf16[576,512]{1,0:T(8,128)(2,1)} %copy-done.2, bf16[576,512]{1,0:T(8,128)(2,1)} %copy-done.6, bf16[8,2048,512]{2,1,0:T(8,128)(2,1)} %far_w_ref.3, bf16[8,2048,512]{2,1,0:T(8,128)(2,1)} %far_w_ref.3, bf16[8,96,256]{2,1,0:T(8,128)(2,1)} %fusion.pick_ref, ...), custom_call_target="tpu_custom_call" | custom-call | tf_op jit(solution)/shard_map/narrow/pallas_call | solution.py:475
  204.2 0.8 copy-done.7
  205.0 8.2 %narrow.3 = f32[256,512]{1,0:T(8,128)} custom-call(s32[10]{0:T(128)} %get-tuple-element.86.table_ref, bf16[576,512]{1,0:T(8,128)(2,1)} %copy-done.3, bf16[576,512]{1,0:T(8,128)(2,1)} %copy-done.7, bf16[8,2048,512]{2,1,0:T(8,128)(2,1)} %far_w_ref.3, bf16[8,2048,512]{2,1,0:T(8,128)(2,1)} %far_w_ref.3, bf16[8,96,256]{2,1,0:T(8,128)(2,1)} %fusion.pick_ref, ...), custom_call_target="tpu_custom_call" | custom-call | tf_op jit(solution)/shard_map/narrow/pallas_call | solution.py:475
  213.2 1.1 convert_element_type.141
  214.3 1.3 collective-permute-start.35
  215.6 1.5 collective-permute-start.34
  217.9 2.0 collective-permute-done.35
  219.9 1.3 collective-permute-done.34
  (138 shorter events, 17.1 us)
Async XLA Ops:
  1.0 6.1 %copy-start.4 = (bf16[64,2048]{1,0:T(8,128)(2,1)}, bf16[64,2048]{1,0:T(8,128)(2,1)S(1)}, u32[]{:S(2)}) copy-start(bf16[64,2048]{1,0:T(8,128)(2,1)S(1)} %constant_dynamic-slice_fusion.14.q_ref) | copy-start | bytes 786436
  1.0 10.2 %collective-permute-start.1 = (bf16[64,2048]{1,0:T(8,128)(2,1)S(1)}, bf16[64,2048]{1,0:T(8,128)(2,1)S(1)}, u32[]{:S(2)}, u32[]{:S(2)}) collective-permute-start(bf16[64,2048]{1,0:T(8,128)(2,1)S(1)} %constant_dynamic-slice_fusion.14.q_ref), channel_id=1, source_target_pairs={{0,8},{8,0},{16,24},{24,16},{1,9},{9,1},{17,25},{25,17},{2,10},{10... | collective-permute-start | bytes 786440 | tf_op jit(solution)/shard_map/ppermute | solution.py:189
  4.0 14.6 %collective-permute-start.3 = (bf16[64,2048]{1,0:T(8,128)(2,1)S(1)}, bf16[64,2048]{1,0:T(8,128)(2,1)S(1)}, u32[]{:S(2)}, u32[]{:S(2)}) collective-permute-start(bf16[64,2048]{1,0:T(8,128)(2,1)S(1)} %constant_dynamic-slice_fusion.14.q_ref), channel_id=1, source_target_pairs={{0,16},{8,24},{16,0},{24,8},{1,17},{9,25},{17,1},{25,9},{2,18},{10... | collective-permute-start | bytes 786440 | tf_op jit(solution)/shard_map/ppermute | solution.py:189
  5.5 19.6 %collective-permute-start.5 = (bf16[64,2048]{1,0:T(8,128)(2,1)S(1)}, bf16[64,2048]{1,0:T(8,128)(2,1)S(1)}, u32[]{:S(2)}, u32[]{:S(2)}) collective-permute-start(bf16[64,2048]{1,0:T(8,128)(2,1)S(1)} %constant_dynamic-slice_fusion.14.q_ref), channel_id=1, source_target_pairs={{0,24},{8,16},{16,8},{24,0},{1,25},{9,17},{17,9},{25,1},{2,26},{10... | collective-permute-start | bytes 786440 | tf_op jit(solution)/shard_map/ppermute | solution.py:189
  6.8 0.7 copy-start.20
  6.8 0.8 copy-start.21
  6.8 0.8 copy-start.23
  6.9 1.2 copy-start.24
  6.9 1.2 copy-start.25
  7.0 4.1 %collective-permute-start = (bf16[512,1024]{1,0:T(8,128)(2,1)S(1)}, bf16[512,1024]{1,0:T(8,128)(2,1)S(1)}, u32[]{:S(2)}, u32[]{:S(2)}) collective-permute-start(bf16[512,1024]{1,0:T(8,128)(2,1)S(1)} %pad_maximum_fusion), channel_id=1, source_target_pairs={{0,1},{1,0},{2,3},{3,2},{4,5},{5,4},{6,7},{7,6},{8,9},{9,8},{10,11... | collective-permute-start | bytes 3145736 | tf_op jit(solution)/shard_map/ppermute | solution.py:189
  11.2 0.7 copy-start.16
  11.2 1.1 copy-start
  16.6 19.3 %collective-permute-start.2 = (bf16[64,2176]{1,0:T(8,128)(2,1)}, bf16[64,2176]{1,0:T(8,128)(2,1)S(1)}, u32[]{:S(2)}, u32[]{:S(2)}) collective-permute-start(bf16[64,2176]{1,0:T(8,128)(2,1)} %attend.5), channel_id=1, source_target_pairs={{0,8},{8,0},{16,24},{24,16},{1,9},{9,1},{17,25},{25,17},{2,10},{10... | collective-permute-start | bytes 835592 | tf_op jit(solution)/shard_map/ppermute | solution.py:189
  18.6 0.7 copy-start.15
  23.6 12.3 %collective-permute-start.4 = (bf16[64,2176]{1,0:T(8,128)(2,1)}, bf16[64,2176]{1,0:T(8,128)(2,1)S(1)}, u32[]{:S(2)}, u32[]{:S(2)}) collective-permute-start(bf16[64,2176]{1,0:T(8,128)(2,1)} %attend.6), channel_id=1, source_target_pairs={{0,16},{8,24},{16,0},{24,8},{1,17},{9,25},{17,1},{25,9},{2,18},{10... | collective-permute-start | bytes 835592 | tf_op jit(solution)/shard_map/ppermute | solution.py:189
  25.1 0.7 copy-start.14
  30.1 7.7 %collective-permute-start.6 = (bf16[64,2176]{1,0:T(8,128)(2,1)}, bf16[64,2176]{1,0:T(8,128)(2,1)S(1)}, u32[]{:S(2)}, u32[]{:S(2)}) collective-permute-start(bf16[64,2176]{1,0:T(8,128)(2,1)} %attend.7), channel_id=1, source_target_pairs={{0,24},{8,16},{16,8},{24,0},{1,25},{9,17},{17,9},{25,1},{2,26},{10... | collective-permute-start | bytes 835592 | tf_op jit(solution)/shard_map/ppermute | solution.py:189
  35.9 2.0 copy-start.8
  35.9 2.0 copy-start.9
  37.8 0.7 copy-start.10
  40.7 5.0 %collective-permute-start.7 = (bf16[64,640]{1,0:T(8,128)(2,1)}, bf16[64,640]{1,0:T(8,128)(2,1)S(1)}, u32[]{:S(2)}, u32[]{:S(2)}) collective-permute-start(bf16[64,640]{1,0:T(8,128)(2,1)} %get-tuple-element.27), channel_id=1, source_target_pairs={{0,2},{1,3},{2,0},{3,1},{4,6},{5,7},{6,4},{7,5},{8,10},{9,11},{10,... | collective-permute-start | bytes 245768 | tf_op jit(solution)/shard_map/ppermute | solution.py:189
  42.3 6.7 %collective-permute-start.8 = (bf16[64,640]{1,0:T(8,128)(2,1)}, bf16[64,640]{1,0:T(8,128)(2,1)S(1)}, u32[]{:S(2)}, u32[]{:S(2)}) collective-permute-start(bf16[64,640]{1,0:T(8,128)(2,1)} %get-tuple-element.28), channel_id=1, source_target_pairs={{0,4},{1,5},{2,6},{3,7},{4,0},{5,1},{6,2},{7,3},{8,12},{9,13},{10,... | collective-permute-start | bytes 245768 | tf_op jit(solution)/shard_map/ppermute | solution.py:189
  44.9 6.4 %collective-permute-start.9 = (bf16[64,640]{1,0:T(8,128)(2,1)}, bf16[64,640]{1,0:T(8,128)(2,1)S(1)}, u32[]{:S(2)}, u32[]{:S(2)}) collective-permute-start(bf16[64,640]{1,0:T(8,128)(2,1)} %get-tuple-element.29), channel_id=1, source_target_pairs={{0,6},{1,7},{2,4},{3,5},{4,2},{5,3},{6,0},{7,1},{8,14},{9,15},{10,... | collective-permute-start | bytes 245768 | tf_op jit(solution)/shard_map/ppermute | solution.py:189
  45.8 5.6 %copy-start.17 = (bf16[64,640]{1,0:T(8,128)(2,1)}, bf16[64,640]{1,0:T(8,128)(2,1)S(1)}, u32[]{:S(2)}) copy-start(bf16[64,640]{1,0:T(8,128)(2,1)S(1)} %collective-permute-done.7.refs_1_) | copy-start | bytes 245764
  49.0 2.4 %copy-start.18 = (bf16[64,640]{1,0:T(8,128)(2,1)}, bf16[64,640]{1,0:T(8,128)(2,1)S(1)}, u32[]{:S(2)}) copy-start(bf16[64,640]{1,0:T(8,128)(2,1)S(1)} %collective-permute-done.8.refs_2_) | copy-start | bytes 245764
  51.4 0.6 copy-start.19
  55.4 4.5 %collective-permute-start.10 = (bf16[64,512]{1,0:T(8,128)(2,1)}, bf16[64,512]{1,0:T(8,128)(2,1)S(1)}, u32[]{:S(2)}, u32[]{:S(2)}) collective-permute-start(bf16[64,512]{1,0:T(8,128)(2,1)} %merge.1.refs_8_), channel_id=1, source_target_pairs={{0,2},{1,3},{2,0},{3,1},{4,6},{5,7},{6,4},{7,5},{8,10},{9,11},{10,... | collective-permute-start | bytes 196616 | tf_op jit(solution)/shard_map/ppermute | solution.py:189
  55.4 5.4 %collective-permute-start.11 = (bf16[64,512]{1,0:T(8,128)(2,1)}, bf16[64,512]{1,0:T(8,128)(2,1)S(1)}, u32[]{:S(2)}, u32[]{:S(2)}) collective-permute-start(bf16[64,512]{1,0:T(8,128)(2,1)} %merge.1.refs_8_), channel_id=1, source_target_pairs={{0,4},{1,5},{2,6},{3,7},{4,0},{5,1},{6,2},{7,3},{8,12},{9,13},{10,... | collective-permute-start | bytes 196616 | tf_op jit(solution)/shard_map/ppermute | solution.py:189
  57.0 6.3 %collective-permute-start.12 = (bf16[64,512]{1,0:T(8,128)(2,1)}, bf16[64,512]{1,0:T(8,128)(2,1)S(1)}, u32[]{:S(2)}, u32[]{:S(2)}) collective-permute-start(bf16[64,512]{1,0:T(8,128)(2,1)} %merge.1.refs_8_), channel_id=1, source_target_pairs={{0,6},{1,7},{2,4},{3,5},{4,2},{5,3},{6,0},{7,1},{8,14},{9,15},{10,... | collective-permute-start | bytes 196616 | tf_op jit(solution)/shard_map/ppermute | solution.py:189
  59.9 6.5 %copy-start.11 = (bf16[64,512]{1,0:T(8,128)(2,1)}, bf16[64,512]{1,0:T(8,128)(2,1)S(1)}, u32[]{:S(2)}) copy-start(bf16[64,512]{1,0:T(8,128)(2,1)S(1)} %collective-permute-done.10.refs_9_) | copy-start | bytes 196612
  60.8 5.6 %copy-start.12 = (bf16[64,512]{1,0:T(8,128)(2,1)}, bf16[64,512]{1,0:T(8,128)(2,1)S(1)}, u32[]{:S(2)}) copy-start(bf16[64,512]{1,0:T(8,128)(2,1)S(1)} %collective-permute-done.11.refs_10_) | copy-start | bytes 196612
  63.2 3.2 %copy-start.13 = (bf16[64,512]{1,0:T(8,128)(2,1)}, bf16[64,512]{1,0:T(8,128)(2,1)S(1)}, u32[]{:S(2)}) copy-start(bf16[64,512]{1,0:T(8,128)(2,1)S(1)} %collective-permute-done.12.refs_11_) | copy-start | bytes 196612
  64.1 1.6 collective-permute-start.13
  66.5 12.1 %copy-start.22 = (f32[512]{0:T(512)S(1)}, f32[512]{0:T(512)}, u32[]{:S(2)}) copy-start(f32[512]{0:T(512)} %param.26) | copy-start | bytes 6148
  70.9 5.8 %collective-permute-start.16 = (bf16[64,512]{1,0:T(8,128)(2,1)}, bf16[64,512]{1,0:T(8,128)(2,1)S(1)}, u32[]{:S(2)}, u32[]{:S(2)}) collective-permute-start(bf16[64,512]{1,0:T(8,128)(2,1)} %project.1), channel_id=1, source_target_pairs={{0,24},{8,16},{16,8},{24,0},{1,25},{9,17},{17,9},{25,1},{2,26},{10... | collective-permute-start | bytes 196616 | tf_op jit(solution)/shard_map/ppermute | solution.py:189
  72.0 5.5 %collective-permute-start.15 = (bf16[64,512]{1,0:T(8,128)(2,1)}, bf16[64,512]{1,0:T(8,128)(2,1)S(1)}, u32[]{:S(2)}, u32[]{:S(2)}) collective-permute-start(bf16[64,512]{1,0:T(8,128)(2,1)} %project.1), channel_id=1, source_target_pairs={{0,16},{8,24},{16,0},{24,8},{1,17},{9,25},{17,1},{25,9},{2,18},{10... | collective-permute-start | bytes 196616 | tf_op jit(solution)/shard_map/ppermute | solution.py:189
  72.9 4.6 %collective-permute-start.14 = (bf16[64,512]{1,0:T(8,128)(2,1)}, bf16[64,512]{1,0:T(8,128)(2,1)S(1)}, u32[]{:S(2)}, u32[]{:S(2)}) collective-permute-start(bf16[64,512]{1,0:T(8,128)(2,1)} %project.1), channel_id=1, source_target_pairs={{0,8},{8,0},{16,24},{24,16},{1,9},{9,1},{17,25},{25,17},{2,10},{10... | collective-permute-start | bytes 196616 | tf_op jit(solution)/shard_map/ppermute | solution.py:189
  78.5 9.1 %collective-permute-start.17 = (f32[2,128]{1,0:T(2,128)S(1)}, f32[2,128]{1,0:T(2,128)S(1)}, u32[]{:S(2)}, u32[]{:S(2)}) collective-permute-start(f32[2,128]{1,0:T(2,128)S(1)} %bitcast.40), channel_id=1, source_target_pairs={{0,1},{1,0},{2,3},{3,2},{4,5},{5,4},{6,7},{7,6},{8,9},{9,8},{10,11... | collective-permute-start | bytes 3080 | tf_op jit(solution)/shard_map/ppermute | solution.py:189
  87.6 11.8 %collective-permute-start.18 = (bf16[576,1024]{1,0:T(8,128)(2,1)}, bf16[576,1024]{1,0:T(8,128)(2,1)S(1)}, u32[]{:S(2)}, u32[]{:S(2)}) collective-permute-start(bf16[576,1024]{1,0:T(8,128)(2,1)} %widen.4), channel_id=1, source_target_pairs={{0,1},{1,0},{2,3},{3,2},{4,5},{5,4},{6,7},{7,6},{8,9},{9,8},{10,11... | collective-permute-start | bytes 3538952 | tf_op jit(solution)/shard_map/ppermute | solution.py:189
  88.1 11.2 %collective-permute-start.21 = (f32[2,128]{1,0:T(2,128)S(1)}, f32[2,128]{1,0:T(2,128)S(1)}, u32[]{:S(2)}, u32[]{:S(2)}) collective-permute-start(f32[2,128]{1,0:T(2,128)S(1)} %bitcast_add_fusion), channel_id=1, source_target_pairs={{0,6},{1,7},{2,4},{3,5},{4,2},{5,3},{6,0},{7,1},{8,14},{9,15},{10,... | collective-permute-start | bytes 3080 | tf_op jit(solution)/shard_map/ppermute | solution.py:189
  91.0 8.4 %collective-permute-start.19 = (f32[2,128]{1,0:T(2,128)S(1)}, f32[2,128]{1,0:T(2,128)S(1)}, u32[]{:S(2)}, u32[]{:S(2)}) collective-permute-start(f32[2,128]{1,0:T(2,128)S(1)} %bitcast_add_fusion), channel_id=1, source_target_pairs={{0,2},{1,3},{2,0},{3,1},{4,6},{5,7},{6,4},{7,5},{8,10},{9,11},{10,... | collective-permute-start | bytes 3080 | tf_op jit(solution)/shard_map/ppermute | solution.py:189
  91.0 8.4 %collective-permute-start.20 = (f32[2,128]{1,0:T(2,128)S(1)}, f32[2,128]{1,0:T(2,128)S(1)}, u32[]{:S(2)}, u32[]{:S(2)}) collective-permute-start(f32[2,128]{1,0:T(2,128)S(1)} %bitcast_add_fusion), channel_id=1, source_target_pairs={{0,4},{1,5},{2,6},{3,7},{4,0},{5,1},{6,2},{7,3},{8,12},{9,13},{10,... | collective-permute-start | bytes 3080 | tf_op jit(solution)/shard_map/ppermute | solution.py:189
  108.1 18.9 %collective-permute-start.22 = (bf16[576,1024]{1,0:T(8,128)(2,1)}, bf16[576,1024]{1,0:T(8,128)(2,1)S(1)}, u32[]{:S(2)}, u32[]{:S(2)}) collective-permute-start(bf16[576,1024]{1,0:T(8,128)(2,1)} %widen.6), channel_id=1, source_target_pairs={{0,1},{1,0},{2,3},{3,2},{4,5},{5,4},{6,7},{7,6},{8,9},{9,8},{10,11... | collective-permute-start | bytes 3538952 | tf_op jit(solution)/shard_map/ppermute | solution.py:189
  108.1 15.7 %collective-permute-start.28 = (bf16[288,1024]{1,0:T(8,128)(2,1)S(1)}, bf16[288,1024]{1,0:T(8,128)(2,1)S(1)}, u32[]{:S(2)}, u32[]{:S(2)}) collective-permute-start(bf16[288,1024]{1,0:T(8,128)(2,1)S(1)} %get-tuple-element.42), channel_id=1, source_target_pairs={{0,2},{1,3},{2,0},{3,1},{4,6},{5,7},{6,4},{7,5},{8,10},{9,11},{10,... | collective-permute-start | bytes 1769480 | tf_op jit(solution)/shard_map/ppermute | solution.py:189
  117.3 9.7 %copy-start.1 = (bf16[576,1024]{1,0:T(8,128)(2,1)S(1)}, bf16[576,1024]{1,0:T(8,128)(2,1)}, u32[]{:S(2)}) copy-start(bf16[576,1024]{1,0:T(8,128)(2,1)} %widen.7) | copy-start | bytes 3538948
  124.1 11.8 %collective-permute-start.29 = (bf16[144,1024]{1,0:T(8,128)(2,1)S(1)}, bf16[144,1024]{1,0:T(8,128)(2,1)S(1)}, u32[]{:S(2)}, u32[]{:S(2)}) collective-permute-start(bf16[144,1024]{1,0:T(8,128)(2,1)S(1)} %constant_dynamic-slice_fusion.4), channel_id=1, source_target_pairs={{0,6},{1,7},{2,4},{3,5},{4,2},{5,3},{6,0},{7,1},{8,14},{9,15},{10,... | collective-permute-start | bytes 884744 | tf_op jit(solution)/shard_map/ppermute | solution.py:189
  127.6 19.7 %collective-permute-start.23 = (bf16[288,1024]{1,0:T(8,128)(2,1)S(1)}, bf16[288,1024]{1,0:T(8,128)(2,1)S(1)}, u32[]{:S(2)}, u32[]{:S(2)}) collective-permute-start(bf16[288,1024]{1,0:T(8,128)(2,1)S(1)} %get-tuple-element.39), channel_id=1, source_target_pairs={{0,6},{1,7},{2,4},{3,5},{4,2},{5,3},{6,0},{7,1},{8,14},{9,15},{10,... | collective-permute-start | bytes 1769480 | tf_op jit(solution)/shard_map/ppermute | solution.py:189
  147.5 25.3 %collective-permute-start.24 = (bf16[144,1024]{1,0:T(8,128)(2,1)S(1)}, bf16[144,1024]{1,0:T(8,128)(2,1)S(1)}, u32[]{:S(2)}, u32[]{:S(2)}) collective-permute-start(bf16[144,1024]{1,0:T(8,128)(2,1)S(1)} %constant_dynamic-slice_fusion.5), channel_id=1, source_target_pairs={{0,2},{1,3},{2,0},{3,1},{4,6},{5,7},{6,4},{7,5},{8,10},{9,11},{10,... | collective-permute-start | bytes 884744 | tf_op jit(solution)/shard_map/ppermute | solution.py:189
  165.7 13.3 %collective-permute-start.30 = (bf16[144,512]{1,0:T(8,128)(2,1)S(1)}, bf16[144,512]{1,0:T(8,128)(2,1)S(1)}, u32[]{:S(2)}, u32[]{:S(2)}) collective-permute-start(bf16[144,512]{1,0:T(8,128)(2,1)S(1)} %fusion.4), channel_id=1, source_target_pairs={{0,6},{1,7},{2,4},{3,5},{4,2},{5,3},{6,0},{7,1},{8,14},{9,15},{10,... | collective-permute-start | bytes 442376 | tf_op jit(solution)/shard_map/ppermute | solution.py:189
  173.1 7.9 %collective-permute-start.25 = (bf16[144,512]{1,0:T(8,128)(2,1)S(1)}, bf16[144,512]{1,0:T(8,128)(2,1)S(1)}, u32[]{:S(2)}, u32[]{:S(2)}) collective-permute-start(bf16[144,512]{1,0:T(8,128)(2,1)S(1)} %fusion.6), channel_id=1, source_target_pairs={{0,2},{1,3},{2,0},{3,1},{4,6},{5,7},{6,4},{7,5},{8,10},{9,11},{10,... | collective-permute-start | bytes 442376 | tf_op jit(solution)/shard_map/ppermute | solution.py:189
  179.1 8.9 %collective-permute-start.31 = (bf16[288,512]{1,0:T(8,128)(2,1)S(1)}, bf16[288,512]{1,0:T(8,128)(2,1)S(1)}, u32[]{:S(2)}, u32[]{:S(2)}) collective-permute-start(bf16[288,512]{1,0:T(8,128)(2,1)S(1)} %pad_maximum_fusion.4), channel_id=1, source_target_pairs={{0,2},{1,3},{2,0},{3,1},{4,6},{5,7},{6,4},{7,5},{8,10},{9,11},{10,... | collective-permute-start | bytes 884744 | tf_op jit(solution)/shard_map/ppermute | solution.py:189
  181.2 11.9 %collective-permute-start.26 = (bf16[288,512]{1,0:T(8,128)(2,1)S(1)}, bf16[288,512]{1,0:T(8,128)(2,1)S(1)}, u32[]{:S(2)}, u32[]{:S(2)}) collective-permute-start(bf16[288,512]{1,0:T(8,128)(2,1)S(1)} %pad_maximum_fusion.3), channel_id=1, source_target_pairs={{0,6},{1,7},{2,4},{3,5},{4,2},{5,3},{6,0},{7,1},{8,14},{9,15},{10,... | collective-permute-start | bytes 884744 | tf_op jit(solution)/shard_map/ppermute | solution.py:189
  188.1 5.1 %copy-start.2 = (bf16[576,512]{1,0:T(8,128)(2,1)}, bf16[576,512]{1,0:T(8,128)(2,1)S(1)}, u32[]{:S(2)}) copy-start(bf16[576,512]{1,0:T(8,128)(2,1)S(1)} %pad_maximum_fusion.2.own_ref) | copy-start | bytes 1769476
  188.1 6.8 %collective-permute-start.32 = (bf16[576,512]{1,0:T(8,128)(2,1)S(1)}, bf16[576,512]{1,0:T(8,128)(2,1)S(1)}, u32[]{:S(2)}, u32[]{:S(2)}) collective-permute-start(bf16[576,512]{1,0:T(8,128)(2,1)S(1)} %pad_maximum_fusion.2.own_ref), channel_id=1, source_target_pairs={{0,1},{1,0},{2,3},{3,2},{4,5},{5,4},{6,7},{7,6},{8,9},{9,8},{10,11... | collective-permute-start | bytes 1769480 | tf_op jit(solution)/shard_map/ppermute | solution.py:189
  193.2 10.9 %copy-start.3 = (bf16[576,512]{1,0:T(8,128)(2,1)}, bf16[576,512]{1,0:T(8,128)(2,1)S(1)}, u32[]{:S(2)}) copy-start(bf16[576,512]{1,0:T(8,128)(2,1)S(1)} %pad_maximum_fusion.1.own_ref) | copy-start | bytes 1769476
  193.2 10.9 %collective-permute-start.27 = (bf16[576,512]{1,0:T(8,128)(2,1)S(1)}, bf16[576,512]{1,0:T(8,128)(2,1)S(1)}, u32[]{:S(2)}, u32[]{:S(2)}) collective-permute-start(bf16[576,512]{1,0:T(8,128)(2,1)S(1)} %pad_maximum_fusion.1.own_ref), channel_id=1, source_target_pairs={{0,1},{1,0},{2,3},{3,2},{4,5},{5,4},{6,7},{7,6},{8,9},{9,8},{10,11... | collective-permute-start | bytes 1769480 | tf_op jit(solution)/shard_map/ppermute | solution.py:189
  195.0 1.0 copy-start.6
  204.2 0.8 copy-start.7
  213.2 8.3 %copy-start.5 = (bf16[64,512]{1,0:T(8,128)(2,1)S(1)}, bf16[64,512]{1,0:T(8,128)(2,1)}, u32[]{:S(2)}) copy-start(bf16[64,512]{1,0:T(8,128)(2,1)} %project.1) | copy-start | bytes 196612
  214.3 5.6 %collective-permute-start.35 = (bf16[64,512]{1,0:T(8,128)(2,1)S(1)}, bf16[64,512]{1,0:T(8,128)(2,1)S(1)}, u32[]{:S(2)}, u32[]{:S(2)}) collective-permute-start(bf16[64,512]{1,0:T(8,128)(2,1)S(1)} %get-tuple-element.71), channel_id=1, source_target_pairs={{0,24},{8,16},{16,8},{24,0},{1,25},{9,17},{17,9},{25,1},{2,26},{10... | collective-permute-start | bytes 196616 | tf_op jit(solution)/shard_map/ppermute | solution.py:189
  215.6 5.5 %collective-permute-start.34 = (bf16[64,512]{1,0:T(8,128)(2,1)S(1)}, bf16[64,512]{1,0:T(8,128)(2,1)S(1)}, u32[]{:S(2)}, u32[]{:S(2)}) collective-permute-start(bf16[64,512]{1,0:T(8,128)(2,1)S(1)} %get-tuple-element.72), channel_id=1, source_target_pairs={{0,16},{8,24},{16,0},{24,8},{1,17},{9,25},{17,1},{25,9},{2,18},{10... | collective-permute-start | bytes 196616 | tf_op jit(solution)/shard_map/ppermute | solution.py:189
  217.2 4.3 %collective-permute-start.33 = (bf16[64,512]{1,0:T(8,128)(2,1)S(1)}, bf16[64,512]{1,0:T(8,128)(2,1)S(1)}, u32[]{:S(2)}, u32[]{:S(2)}) collective-permute-start(bf16[64,512]{1,0:T(8,128)(2,1)S(1)} %get-tuple-element.70), channel_id=1, source_target_pairs={{0,8},{8,0},{16,24},{24,16},{1,9},{9,1},{17,25},{25,17},{2,10},{10... | collective-permute-start | bytes 196616 | tf_op jit(solution)/shard_map/ppermute | solution.py:189

commit v4 on v3

--- a/solution.py
+++ b/solution.py
@@ -626,9 +626,7 @@
         .reshape(experts, capacity, -1)
     )
 
-    near_id = (z_index ^ (z_index >> 1)) & 1
-    wrap_id = z_index >> 1
-    routes_z = [((near_id, 2), (wrap_id, 6)), ((wrap_id, 6), (near_id, 2))]
+    routes_z = [((z_index & 1, 2), (z_index >> 1, 4))] * 2
     slot_of = jnp.where(hits > 0, starts[None, :] + position, -1)
 
     def quarter_rstd(quarter):

time: 223 us -> 221 us (level)
  starting transfers between devices: 59.2 us -> 36.4 us
  waiting for transfers between devices: 63.8 us -> 83 us
    ppermute x36, starting transfers between devices: 59.2 us -> 36.4 us  [flip(): return lax.ppermute(value, axis, [(i, i ^ bit) for i in range(size)])]
    ppermute x36, waiting for transfers between devices: 63.8 us -> 83 us  [flip(): return lax.ppermute(value, axis, [(i, i ^ bit) for i in range(size)])]
    unnamed x52 -> x62, local copies, waits for them, and re-layouts: 5.18 us -> 5.22 us
  transfers between devices with their start and end apart: 36 -> 36, of which waited for: 20 -> 18; matrix products, arithmetic and copies ran while one was open for 7% -> 7% of each run, Pallas kernels for 21% -> 21%
where the time goes in v4:
time: 221 us; the launch traced here: 220 us
  waiting for transfers between devices  83 us (38%)
  Pallas kernels  71.1 us (32%)
  starting transfers between devices  36.4 us (16%)
  other arithmetic  13.7 us (6%)
  local copies, waits for them, and re-layouts  11.9 us (5%)
  matrix products  2.91 us (1%)
    ppermute x36, waiting for transfers between devices, flip(): return lax.ppermute(value, axis, [(i, i ^ bit) for i in range(size)])  83 us
    ppermute x36, starting transfers between devices, flip(): return lax.ppermute(value, axis, [(i, i ^ bit) for i in range(size)])  36.4 us
    pallas_call x4, Pallas kernels, widen(): pl.pallas_call(widen_kernel, grid_spec=pltpu.PrefetchScalarGridSpec(num_s...  27.4 us
    pallas_call x4, Pallas kernels, attend(): pl.pallas_call(attend_kernel, grid_spec=pltpu.PrefetchScalarGridSpec(num_...  17.3 us
    pallas_call x2, Pallas kernels, narrow(): pl.pallas_call(narrow_kernel, grid_spec=pltpu.PrefetchScalarGridSpec(num_...  16.4 us
    unnamed x62, local copies, waits for them, and re-layouts  5.22 us
  transfers between devices with their start and end apart: 36, of which 18 were waited for; matrix products, arithmetic and copies ran while one was open for 7% of the time, Pallas kernels for 21%

profile of v4, /device:TPU:0, one launch (start us, length us, event | category | flops | bytes accessed | tf_op | source)
XLA Modules:
  0.0 219.7 jit_solution(6747615402659501911)
XLA Ops:
  0.0 1.0 constant_dynamic-slice_fusion.14.q_ref
  1.0 3.0 %collective-permute-start.1 = (bf16[64,2048]{1,0:T(8,128)(2,1)S(1)}, bf16[64,2048]{1,0:T(8,128)(2,1)S(1)}, u32[]{:S(2)}, u32[]{:S(2)}) collective-permute-start(bf16[64,2048]{1,0:T(8,128)(2,1)S(1)} %constant_dynamic-slice_fusion.14.q_ref), channel_id=1, source_target_pairs={{0,8},{8,0},{16,24},{24,16},{1,9},{9,1},{17,25},{25,17},{2,10},{10... | collective-permute-start | bytes 786440 | tf_op jit(solution)/shard_map/ppermute | solution.py:189
  4.0 1.5 collective-permute-start.3
  5.6 1.3 dynamic-slice_bitcast_fusion
  8.5 2.7 %collective-permute-done.1.q_ref = bf16[64,2048]{1,0:T(8,128)(2,1)S(1)} collective-permute-done((bf16[64,2048]{1,0:T(8,128)(2,1)S(1)}, bf16[64,2048]{1,0:T(8,128)(2,1)S(1)}, u32[]{:S(2)}, u32[]{:S(2)}) %collective-permute-start.1) | collective-permute-done | bytes 262176 | tf_op jit(solution)/shard_map/ppermute | solution.py:189
  12.2 4.3 %attend.5 = bf16[64,2176]{1,0:T(8,128)(2,1)} custom-call(s32[1]{0:T(128)} %bitcast.12.core_ref, bf16[64,2048]{1,0:T(8,128)(2,1)} %copy-done.16, bf16[1,512,1024]{2,1,0:T(8,128)(2,1)} %k_own_ref.7, bf16[1,512,1024]{2,1,0:T(8,128)(2,1)} %v_own_ref.7, bf16[512,1024]{1,0:T(8,128)(2,1)} %copy-done, bf16[512,1024]{1,0:T(8,128)(2,1)} %copy-done), custom_call_target="tpu_custom_call" | custom-call | tf_op jit(solution)/shard_map/attend/pallas_call | solution.py:252
  16.6 2.0 collective-permute-start.2
  18.6 0.7 copy-done.15
  19.3 4.3 %attend.6 = bf16[64,2176]{1,0:T(8,128)(2,1)} custom-call(s32[1]{0:T(128)} %bitcast.12.core_ref, bf16[64,2048]{1,0:T(8,128)(2,1)} %copy-done.15, bf16[1,512,1024]{2,1,0:T(8,128)(2,1)} %k_own_ref.7, bf16[1,512,1024]{2,1,0:T(8,128)(2,1)} %v_own_ref.7, bf16[512,1024]{1,0:T(8,128)(2,1)} %copy-done, bf16[512,1024]{1,0:T(8,128)(2,1)} %copy-done), custom_call_target="tpu_custom_call" | custom-call | tf_op jit(solution)/shard_map/attend/pallas_call | solution.py:252
  23.6 1.5 collective-permute-start.4
  25.9 4.3 %attend.7 = bf16[64,2176]{1,0:T(8,128)(2,1)} custom-call(s32[1]{0:T(128)} %bitcast.12.core_ref, bf16[64,2048]{1,0:T(8,128)(2,1)} %copy-done.14, bf16[1,512,1024]{2,1,0:T(8,128)(2,1)} %k_own_ref.7, bf16[1,512,1024]{2,1,0:T(8,128)(2,1)} %v_own_ref.7, bf16[512,1024]{1,0:T(8,128)(2,1)} %copy-done, bf16[512,1024]{1,0:T(8,128)(2,1)} %copy-done), custom_call_target="tpu_custom_call" | custom-call | tf_op jit(solution)/shard_map/attend/pallas_call | solution.py:252
  31.6 4.3 %attend.4.a_ref = bf16[64,2176]{1,0:T(8,128)(2,1)} custom-call(s32[1]{0:T(128)} %bitcast.12.core_ref, bf16[64,2048]{1,0:T(8,128)(2,1)} %copy-done.4, bf16[1,512,1024]{2,1,0:T(8,128)(2,1)} %k_own_ref.7, bf16[1,512,1024]{2,1,0:T(8,128)(2,1)} %v_own_ref.7, bf16[512,1024]{1,0:T(8,128)(2,1)} %copy-done, bf16[512,1024]{1,0:T(8,128)(2,1)} %copy-done), custom_call_target="tpu_custom_call" | custom-call | tf_op jit(solution)/shard_map/attend/pallas_call | solution.py:252
  36.0 1.9 collective-permute-done.6.d_ref
  38.6 2.2 %choose.1 = (bf16[64,640]{1,0:T(8,128)(2,1)}, bf16[64,640]{1,0:T(8,128)(2,1)}, bf16[64,640]{1,0:T(8,128)(2,1)}, bf16[64,640]{1,0:T(8,128)(2,1)}) custom-call(s32[1]{0:T(128)} %bitcast.8.z_ref, s32[64,1]{1,0:T(8,128)} %copy.25.pick_ref, bf16[64,2176]{1,0:T(8,128)(2,1)} %attend.4.a_ref, bf16[64,2176]{1,0:T(8,128)(2,1)} %copy-done.8, ...), custom_call_target="tpu_custom_call" | custom-call | tf_op jit(solution)/shard_map/choose/pallas_call | solution.py:293
  40.8 1.6 collective-permute-start.7
  42.4 2.6 %collective-permute-start.8 = (bf16[64,640]{1,0:T(8,128)(2,1)}, bf16[64,640]{1,0:T(8,128)(2,1)S(1)}, u32[]{:S(2)}, u32[]{:S(2)}) collective-permute-start(bf16[64,640]{1,0:T(8,128)(2,1)} %get-tuple-element.28), channel_id=1, source_target_pairs={{0,4},{1,5},{2,6},{3,7},{4,0},{5,1},{6,2},{7,3},{8,12},{9,13},{10,... | collective-permute-start | bytes 245768 | tf_op jit(solution)/shard_map/ppermute | solution.py:189
  45.8 3.2 %collective-permute-done.8.refs_2_ = bf16[64,640]{1,0:T(8,128)(2,1)S(1)} collective-permute-done((bf16[64,640]{1,0:T(8,128)(2,1)}, bf16[64,640]{1,0:T(8,128)(2,1)S(1)}, u32[]{:S(2)}, u32[]{:S(2)}) %collective-permute-start.8) | collective-permute-done | bytes 81952 | tf_op jit(solution)/shard_map/ppermute | solution.py:189
  49.0 2.4 %collective-permute-done.9.refs_3_ = bf16[64,640]{1,0:T(8,128)(2,1)S(1)} collective-permute-done((bf16[64,640]{1,0:T(8,128)(2,1)}, bf16[64,640]{1,0:T(8,128)(2,1)S(1)}, u32[]{:S(2)}, u32[]{:S(2)}) %collective-permute-start.9) | collective-permute-done | bytes 81952 | tf_op jit(solution)/shard_map/ppermute | solution.py:189
  52.0 3.4 %merge.1.refs_8_ = bf16[64,512]{1,0:T(8,128)(2,1)} custom-call(s32[2]{0:T(128)} %pad_add_fusion.1.place_ref, f32[64,64]{1,0:T(8,128)} %fusion.10.mask_ref, bf16[64,4096]{1,0:T(8,128)(2,1)} %q_ref.1, bf16[64,1024]{1,0:T(8,128)(2,1)} %k_ref.1, bf16[64,1024]{1,0:T(8,128)(2,1)} %v_ref.1, bf16[64,640]{1,0:T(8,128)(2,1)} %get-tuple-element.26.refs_0_, ...), custom_call_target="tpu_custom_call" | custom-call | tf_op jit(solution)/shard_map/merge/pallas_call | solution.py:351
  55.5 1.5 collective-permute-start.11
  57.0 2.8 %collective-permute-start.12 = (bf16[64,512]{1,0:T(8,128)(2,1)}, bf16[64,512]{1,0:T(8,128)(2,1)S(1)}, u32[]{:S(2)}, u32[]{:S(2)}) collective-permute-start(bf16[64,512]{1,0:T(8,128)(2,1)} %merge.1.refs_8_), channel_id=1, source_target_pairs={{0,6},{1,7},{2,4},{3,5},{4,2},{5,3},{6,0},{7,1},{8,14},{9,15},{10,... | collective-permute-start | bytes 196616 | tf_op jit(solution)/shard_map/ppermute | solution.py:189
  60.0 0.9 collective-permute-done.11.refs_10_
  60.8 2.4 %collective-permute-done.12.refs_11_ = bf16[64,512]{1,0:T(8,128)(2,1)S(1)} collective-permute-done((bf16[64,512]{1,0:T(8,128)(2,1)}, bf16[64,512]{1,0:T(8,128)(2,1)S(1)}, u32[]{:S(2)}, u32[]{:S(2)}) %collective-permute-start.12) | collective-permute-done | bytes 65568 | tf_op jit(solution)/shard_map/ppermute | solution.py:189
  63.3 0.9 pad_maximum_fusion.5
  64.3 0.8 add_select_fusion
  66.7 4.4 %project.1 = bf16[64,512]{1,0:T(8,128)(2,1)} custom-call(s32[8]{0:T(128)} %stack.60.order_ref, bf16[64,512]{1,0:T(8,128)(2,1)} %stream_ref.1, bf16[4096,512]{1,0:T(8,128)(2,1)} %refs_7_.1, bf16[4096,512]{1,0:T(8,128)(2,1)} %refs_7_.1, bf16[4096,512]{1,0:T(8,128)(2,1)} %refs_7_.1, bf16[4096,512]{1,0:T(8,128)(2,1)} %refs_7_.1, bf16[4096,512]{1,0:T(8,128)(2,1)} %refs_7_.1, ...), custom_call_target="tpu_custom_call" | custom-call | tf_op jit(solution)/shard_map/project/pallas_call | solution.py:381
  71.1 1.2 collective-permute-start.16
  72.3 0.8 collective-permute-start.15
  73.1 1.5 collective-permute-start.14
  75.3 1.8 collective-permute-done.16
  77.0 1.1 collective-permute-done.15
  78.1 1.0 fusion.2
  79.2 2.1 convolution_convert_fusion
  81.3 6.9 %widen.4 = bf16[576,1024]{1,0:T(8,128)(2,1)} custom-call(s32[9]{0:T(128)} %get-tuple-element.88.table_ref, bf16[8,96,512]{2,1,0:T(8,128)(2,1)} %bitcast.34, bf16[8,512,2048]{2,1,0:T(8,128)(2,1)} %gate_ref.7, bf16[8,512,2048]{2,1,0:T(8,128)(2,1)} %up_ref.7), custom_call_target="tpu_custom_call" | custom-call | tf_op jit(solution)/shard_map/widen/pallas_call | solution.py:427
  88.7 2.8 %collective-permute-start.21 = (f32[2,128]{1,0:T(2,128)S(1)}, f32[2,128]{1,0:T(2,128)S(1)}, u32[]{:S(2)}, u32[]{:S(2)}) collective-permute-start(f32[2,128]{1,0:T(2,128)S(1)} %bitcast_add_fusion), channel_id=1, source_target_pairs={{0,6},{1,7},{2,4},{3,5},{4,2},{5,3},{6,0},{7,1},{8,14},{9,15},{10,... | collective-permute-start | bytes 3080 | tf_op jit(solution)/shard_map/ppermute | solution.py:189
  91.6 1.5 collective-permute-start.20
  93.1 6.9 %widen.5 = bf16[576,1024]{1,0:T(8,128)(2,1)} custom-call(s32[9]{0:T(128)} %get-tuple-element.86.table_ref, bf16[8,96,512]{2,1,0:T(8,128)(2,1)} %bitcast.35, bf16[8,512,2048]{2,1,0:T(8,128)(2,1)} %gate_ref.7, bf16[8,512,2048]{2,1,0:T(8,128)(2,1)} %up_ref.7), custom_call_target="tpu_custom_call" | custom-call | tf_op jit(solution)/shard_map/widen/pallas_call | solution.py:427
  100.0 1.7 add_convert_fusion.1
  101.8 6.9 %widen.6 = bf16[576,1024]{1,0:T(8,128)(2,1)} custom-call(s32[9]{0:T(128)} %get-tuple-element.87.table_ref, bf16[8,96,512]{2,1,0:T(8,128)(2,1)} %bitcast.36, bf16[8,512,2048]{2,1,0:T(8,128)(2,1)} %gate_ref.7, bf16[8,512,2048]{2,1,0:T(8,128)(2,1)} %up_ref.7), custom_call_target="tpu_custom_call" | custom-call | tf_op jit(solution)/shard_map/widen/pallas_call | solution.py:427
  110.0 6.9 %widen.7 = bf16[576,1024]{1,0:T(8,128)(2,1)} custom-call(s32[9]{0:T(128)} %get-tuple-element.85.table_ref, bf16[8,96,512]{2,1,0:T(8,128)(2,1)} %bitcast.37, bf16[8,512,2048]{2,1,0:T(8,128)(2,1)} %gate_ref.7, bf16[8,512,2048]{2,1,0:T(8,128)(2,1)} %up_ref.7), custom_call_target="tpu_custom_call" | custom-call | tf_op jit(solution)/shard_map/widen/pallas_call | solution.py:427
  116.8 7.6 %collective-permute-done.28 = bf16[288,1024]{1,0:T(8,128)(2,1)S(1)} collective-permute-done((bf16[288,1024]{1,0:T(8,128)(2,1)S(1)}, bf16[288,1024]{1,0:T(8,128)(2,1)S(1)}, u32[]{:S(2)}, u32[]{:S(2)}) %collective-permute-start.28) | collective-permute-done | bytes 589856 | tf_op jit(solution)/shard_map/ppermute | solution.py:189
  124.7 1.7 collective-permute-start.29
  127.0 1.8 collective-permute-start.23
  128.9 1.1 compare_reduce_fusion
  129.9 0.8 fusion.pick_ref
  130.8 9.9 %collective-permute-done.29 = bf16[144,1024]{1,0:T(8,128)(2,1)S(1)} collective-permute-done((bf16[144,1024]{1,0:T(8,128)(2,1)S(1)}, bf16[144,1024]{1,0:T(8,128)(2,1)S(1)}, u32[]{:S(2)}, u32[]{:S(2)}) %collective-permute-start.29) | collective-permute-done | bytes 294944 | tf_op jit(solution)/shard_map/ppermute | solution.py:189
  140.8 7.2 %collective-permute-done.23 = bf16[288,1024]{1,0:T(8,128)(2,1)S(1)} collective-permute-done((bf16[288,1024]{1,0:T(8,128)(2,1)S(1)}, bf16[288,1024]{1,0:T(8,128)(2,1)S(1)}, u32[]{:S(2)}, u32[]{:S(2)}) %collective-permute-start.23) | collective-permute-done | bytes 589856 | tf_op jit(solution)/shard_map/ppermute | solution.py:189
  148.5 14.5 %collective-permute-done.24 = bf16[144,1024]{1,0:T(8,128)(2,1)S(1)} collective-permute-done((bf16[144,1024]{1,0:T(8,128)(2,1)S(1)}, bf16[144,1024]{1,0:T(8,128)(2,1)S(1)}, u32[]{:S(2)}, u32[]{:S(2)}) %collective-permute-start.24) | collective-permute-done | bytes 294944 | tf_op jit(solution)/shard_map/ppermute | solution.py:189
  163.4 2.9 %collective-permute-start.25 = (bf16[144,512]{1,0:T(8,128)(2,1)S(1)}, bf16[144,512]{1,0:T(8,128)(2,1)S(1)}, u32[]{:S(2)}, u32[]{:S(2)}) collective-permute-start(bf16[144,512]{1,0:T(8,128)(2,1)S(1)} %get-tuple-element.82), channel_id=1, source_target_pairs={{0,4},{1,5},{2,6},{3,7},{4,0},{5,1},{6,2},{7,3},{8,12},{9,13},{10,... | collective-permute-start | bytes 442376 | tf_op jit(solution)/shard_map/ppermute | solution.py:189
  166.3 9.0 %collective-permute-done.30 = bf16[144,512]{1,0:T(8,128)(2,1)S(1)} collective-permute-done((bf16[144,512]{1,0:T(8,128)(2,1)S(1)}, bf16[144,512]{1,0:T(8,128)(2,1)S(1)}, u32[]{:S(2)}, u32[]{:S(2)}) %collective-permute-start.30) | collective-permute-done | bytes 147488 | tf_op jit(solution)/shard_map/ppermute | solution.py:189
  175.4 3.0 %collective-permute-done.25 = bf16[144,512]{1,0:T(8,128)(2,1)S(1)} collective-permute-done((bf16[144,512]{1,0:T(8,128)(2,1)S(1)}, bf16[144,512]{1,0:T(8,128)(2,1)S(1)}, u32[]{:S(2)}, u32[]{:S(2)}) %collective-permute-start.25) | collective-permute-done | bytes 147488 | tf_op jit(solution)/shard_map/ppermute | solution.py:189
  178.5 6.7 %collective-permute-done.31 = bf16[288,512]{1,0:T(8,128)(2,1)S(1)} collective-permute-done((bf16[288,512]{1,0:T(8,128)(2,1)S(1)}, bf16[288,512]{1,0:T(8,128)(2,1)S(1)}, u32[]{:S(2)}, u32[]{:S(2)}) %collective-permute-start.31) | collective-permute-done | bytes 294944 | tf_op jit(solution)/shard_map/ppermute | solution.py:189
  185.5 5.5 %collective-permute-done.26 = bf16[288,512]{1,0:T(8,128)(2,1)S(1)} collective-permute-done((bf16[288,512]{1,0:T(8,128)(2,1)S(1)}, bf16[288,512]{1,0:T(8,128)(2,1)S(1)}, u32[]{:S(2)}, u32[]{:S(2)}) %collective-permute-start.26) | collective-permute-done | bytes 294944 | tf_op jit(solution)/shard_map/ppermute | solution.py:189
  191.9 0.9 copy.27.scale_ref
  192.8 0.9 broadcast_in_dim.155.init_ref
  193.8 8.2 %narrow.2.init_ref = f32[256,512]{1,0:T(8,128)} custom-call(s32[10]{0:T(128)} %get-tuple-element.83.table_ref, bf16[576,512]{1,0:T(8,128)(2,1)} %copy-done.2, bf16[576,512]{1,0:T(8,128)(2,1)} %copy-done.6, bf16[8,2048,512]{2,1,0:T(8,128)(2,1)} %far_w_ref.3, bf16[8,2048,512]{2,1,0:T(8,128)(2,1)} %far_w_ref.3, bf16[8,96,256]{2,1,0:T(8,128)(2,1)} %fusion.pick_ref, ...), custom_call_target="tpu_custom_call" | custom-call | tf_op jit(solution)/shard_map/narrow/pallas_call | solution.py:475
  202.0 0.8 copy-done.7
  202.8 8.2 %narrow.3 = f32[256,512]{1,0:T(8,128)} custom-call(s32[10]{0:T(128)} %get-tuple-element.84.table_ref, bf16[576,512]{1,0:T(8,128)(2,1)} %copy-done.3, bf16[576,512]{1,0:T(8,128)(2,1)} %copy-done.7, bf16[8,2048,512]{2,1,0:T(8,128)(2,1)} %far_w_ref.3, bf16[8,2048,512]{2,1,0:T(8,128)(2,1)} %far_w_ref.3, bf16[8,96,256]{2,1,0:T(8,128)(2,1)} %fusion.pick_ref, ...), custom_call_target="tpu_custom_call" | custom-call | tf_op jit(solution)/shard_map/narrow/pallas_call | solution.py:475
  211.0 1.1 convert_element_type.141
  212.2 1.2 collective-permute-start.35
  213.4 1.2 collective-permute-start.34
  214.7 1.1 collective-permute-start.33
  215.7 2.1 collective-permute-done.35
  217.8 1.2 collective-permute-done.34
  (147 shorter events, 15.3 us)
Async XLA Ops:
  1.0 6.1 %copy-start.4 = (bf16[64,2048]{1,0:T(8,128)(2,1)}, bf16[64,2048]{1,0:T(8,128)(2,1)S(1)}, u32[]{:S(2)}) copy-start(bf16[64,2048]{1,0:T(8,128)(2,1)S(1)} %constant_dynamic-slice_fusion.14.q_ref) | copy-start | bytes 786436
  1.0 10.2 %collective-permute-start.1 = (bf16[64,2048]{1,0:T(8,128)(2,1)S(1)}, bf16[64,2048]{1,0:T(8,128)(2,1)S(1)}, u32[]{:S(2)}, u32[]{:S(2)}) collective-permute-start(bf16[64,2048]{1,0:T(8,128)(2,1)S(1)} %constant_dynamic-slice_fusion.14.q_ref), channel_id=1, source_target_pairs={{0,8},{8,0},{16,24},{24,16},{1,9},{9,1},{17,25},{25,17},{2,10},{10... | collective-permute-start | bytes 786440 | tf_op jit(solution)/shard_map/ppermute | solution.py:189
  4.0 14.6 %collective-permute-start.3 = (bf16[64,2048]{1,0:T(8,128)(2,1)S(1)}, bf16[64,2048]{1,0:T(8,128)(2,1)S(1)}, u32[]{:S(2)}, u32[]{:S(2)}) collective-permute-start(bf16[64,2048]{1,0:T(8,128)(2,1)S(1)} %constant_dynamic-slice_fusion.14.q_ref), channel_id=1, source_target_pairs={{0,16},{8,24},{16,0},{24,8},{1,17},{9,25},{17,1},{25,9},{2,18},{10... | collective-permute-start | bytes 786440 | tf_op jit(solution)/shard_map/ppermute | solution.py:189
  5.5 19.6 %collective-permute-start.5 = (bf16[64,2048]{1,0:T(8,128)(2,1)S(1)}, bf16[64,2048]{1,0:T(8,128)(2,1)S(1)}, u32[]{:S(2)}, u32[]{:S(2)}) collective-permute-start(bf16[64,2048]{1,0:T(8,128)(2,1)S(1)} %constant_dynamic-slice_fusion.14.q_ref), channel_id=1, source_target_pairs={{0,24},{8,16},{16,8},{24,0},{1,25},{9,17},{17,9},{25,1},{2,26},{10... | collective-permute-start | bytes 786440 | tf_op jit(solution)/shard_map/ppermute | solution.py:189
  6.8 0.8 copy-start.22
  6.8 0.8 copy-start.28
  6.9 1.2 copy-start.29
  6.9 1.2 copy-start.30
  7.0 4.1 %collective-permute-start = (bf16[512,1024]{1,0:T(8,128)(2,1)S(1)}, bf16[512,1024]{1,0:T(8,128)(2,1)S(1)}, u32[]{:S(2)}, u32[]{:S(2)}) collective-permute-start(bf16[512,1024]{1,0:T(8,128)(2,1)S(1)} %pad_maximum_fusion), channel_id=1, source_target_pairs={{0,1},{1,0},{2,3},{3,2},{4,5},{5,4},{6,7},{7,6},{8,9},{9,8},{10,11... | collective-permute-start | bytes 3145736 | tf_op jit(solution)/shard_map/ppermute | solution.py:189
  11.2 0.7 copy-start.16
  11.2 1.1 copy-start
  16.6 19.4 %collective-permute-start.2 = (bf16[64,2176]{1,0:T(8,128)(2,1)}, bf16[64,2176]{1,0:T(8,128)(2,1)S(1)}, u32[]{:S(2)}, u32[]{:S(2)}) collective-permute-start(bf16[64,2176]{1,0:T(8,128)(2,1)} %attend.5), channel_id=1, source_target_pairs={{0,8},{8,0},{16,24},{24,16},{1,9},{9,1},{17,25},{25,17},{2,10},{10... | collective-permute-start | bytes 835592 | tf_op jit(solution)/shard_map/ppermute | solution.py:189
  18.6 0.7 copy-start.15
  23.6 12.3 %collective-permute-start.4 = (bf16[64,2176]{1,0:T(8,128)(2,1)}, bf16[64,2176]{1,0:T(8,128)(2,1)S(1)}, u32[]{:S(2)}, u32[]{:S(2)}) collective-permute-start(bf16[64,2176]{1,0:T(8,128)(2,1)} %attend.6), channel_id=1, source_target_pairs={{0,16},{8,24},{16,0},{24,8},{1,17},{9,25},{17,1},{25,9},{2,18},{10... | collective-permute-start | bytes 835592 | tf_op jit(solution)/shard_map/ppermute | solution.py:189
  25.1 0.7 copy-start.14
  30.2 7.7 %collective-permute-start.6 = (bf16[64,2176]{1,0:T(8,128)(2,1)}, bf16[64,2176]{1,0:T(8,128)(2,1)S(1)}, u32[]{:S(2)}, u32[]{:S(2)}) collective-permute-start(bf16[64,2176]{1,0:T(8,128)(2,1)} %attend.7), channel_id=1, source_target_pairs={{0,24},{8,16},{16,8},{24,0},{1,25},{9,17},{17,9},{25,1},{2,26},{10... | collective-permute-start | bytes 835592 | tf_op jit(solution)/shard_map/ppermute | solution.py:189
  35.9 2.0 copy-start.8
  35.9 1.9 copy-start.9
  40.8 5.0 %collective-permute-start.7 = (bf16[64,640]{1,0:T(8,128)(2,1)}, bf16[64,640]{1,0:T(8,128)(2,1)S(1)}, u32[]{:S(2)}, u32[]{:S(2)}) collective-permute-start(bf16[64,640]{1,0:T(8,128)(2,1)} %get-tuple-element.27), channel_id=1, source_target_pairs={{0,2},{1,3},{2,0},{3,1},{4,6},{5,7},{6,4},{7,5},{8,10},{9,11},{10,... | collective-permute-start | bytes 245768 | tf_op jit(solution)/shard_map/ppermute | solution.py:189
  42.4 6.7 %collective-permute-start.8 = (bf16[64,640]{1,0:T(8,128)(2,1)}, bf16[64,640]{1,0:T(8,128)(2,1)S(1)}, u32[]{:S(2)}, u32[]{:S(2)}) collective-permute-start(bf16[64,640]{1,0:T(8,128)(2,1)} %get-tuple-element.28), channel_id=1, source_target_pairs={{0,4},{1,5},{2,6},{3,7},{4,0},{5,1},{6,2},{7,3},{8,12},{9,13},{10,... | collective-permute-start | bytes 245768 | tf_op jit(solution)/shard_map/ppermute | solution.py:189
  45.0 6.4 %collective-permute-start.9 = (bf16[64,640]{1,0:T(8,128)(2,1)}, bf16[64,640]{1,0:T(8,128)(2,1)S(1)}, u32[]{:S(2)}, u32[]{:S(2)}) collective-permute-start(bf16[64,640]{1,0:T(8,128)(2,1)} %get-tuple-element.29), channel_id=1, source_target_pairs={{0,6},{1,7},{2,4},{3,5},{4,2},{5,3},{6,0},{7,1},{8,14},{9,15},{10,... | collective-permute-start | bytes 245768 | tf_op jit(solution)/shard_map/ppermute | solution.py:189
  45.8 5.6 %copy-start.18 = (bf16[64,640]{1,0:T(8,128)(2,1)}, bf16[64,640]{1,0:T(8,128)(2,1)S(1)}, u32[]{:S(2)}) copy-start(bf16[64,640]{1,0:T(8,128)(2,1)S(1)} %collective-permute-done.7.refs_1_) | copy-start | bytes 245764
  49.0 2.4 %copy-start.19 = (bf16[64,640]{1,0:T(8,128)(2,1)}, bf16[64,640]{1,0:T(8,128)(2,1)S(1)}, u32[]{:S(2)}) copy-start(bf16[64,640]{1,0:T(8,128)(2,1)S(1)} %collective-permute-done.8.refs_2_) | copy-start | bytes 245764
  55.5 4.5 %collective-permute-start.10 = (bf16[64,512]{1,0:T(8,128)(2,1)}, bf16[64,512]{1,0:T(8,128)(2,1)S(1)}, u32[]{:S(2)}, u32[]{:S(2)}) collective-permute-start(bf16[64,512]{1,0:T(8,128)(2,1)} %merge.1.refs_8_), channel_id=1, source_target_pairs={{0,2},{1,3},{2,0},{3,1},{4,6},{5,7},{6,4},{7,5},{8,10},{9,11},{10,... | collective-permute-start | bytes 196616 | tf_op jit(solution)/shard_map/ppermute | solution.py:189
  55.5 5.4 %collective-permute-start.11 = (bf16[64,512]{1,0:T(8,128)(2,1)}, bf16[64,512]{1,0:T(8,128)(2,1)S(1)}, u32[]{:S(2)}, u32[]{:S(2)}) collective-permute-start(bf16[64,512]{1,0:T(8,128)(2,1)} %merge.1.refs_8_), channel_id=1, source_target_pairs={{0,4},{1,5},{2,6},{3,7},{4,0},{5,1},{6,2},{7,3},{8,12},{9,13},{10,... | collective-permute-start | bytes 196616 | tf_op jit(solution)/shard_map/ppermute | solution.py:189
  57.0 6.3 %collective-permute-start.12 = (bf16[64,512]{1,0:T(8,128)(2,1)}, bf16[64,512]{1,0:T(8,128)(2,1)S(1)}, u32[]{:S(2)}, u32[]{:S(2)}) collective-permute-start(bf16[64,512]{1,0:T(8,128)(2,1)} %merge.1.refs_8_), channel_id=1, source_target_pairs={{0,6},{1,7},{2,4},{3,5},{4,2},{5,3},{6,0},{7,1},{8,14},{9,15},{10,... | collective-permute-start | bytes 196616 | tf_op jit(solution)/shard_map/ppermute | solution.py:189
  60.0 14.6 %copy-start.24 = (s32[8]{0:T(128)}, s32[8]{0:T(128)S(1)}, u32[]{:S(2)}) copy-start(s32[8]{0:T(128)S(1)} %select_reduce_fusion.3) | copy-start | bytes 100
  60.0 6.7 %copy-start.11 = (bf16[64,512]{1,0:T(8,128)(2,1)}, bf16[64,512]{1,0:T(8,128)(2,1)S(1)}, u32[]{:S(2)}) copy-start(bf16[64,512]{1,0:T(8,128)(2,1)S(1)} %collective-permute-done.10.refs_9_) | copy-start | bytes 196612
  60.8 5.8 %copy-start.12 = (bf16[64,512]{1,0:T(8,128)(2,1)}, bf16[64,512]{1,0:T(8,128)(2,1)S(1)}, u32[]{:S(2)}) copy-start(bf16[64,512]{1,0:T(8,128)(2,1)S(1)} %collective-permute-done.11.refs_10_) | copy-start | bytes 196612
  63.3 3.4 %copy-start.13 = (bf16[64,512]{1,0:T(8,128)(2,1)}, bf16[64,512]{1,0:T(8,128)(2,1)S(1)}, u32[]{:S(2)}) copy-start(bf16[64,512]{1,0:T(8,128)(2,1)S(1)} %collective-permute-done.12.refs_11_) | copy-start | bytes 196612
  64.2 1.8 collective-permute-start.13
  66.7 12.5 %copy-start.27 = (f32[512]{0:T(512)S(1)}, f32[512]{0:T(512)}, u32[]{:S(2)}) copy-start(f32[512]{0:T(512)} %param.26) | copy-start | bytes 6148
  71.1 5.9 %collective-permute-start.16 = (bf16[64,512]{1,0:T(8,128)(2,1)}, bf16[64,512]{1,0:T(8,128)(2,1)S(1)}, u32[]{:S(2)}, u32[]{:S(2)}) collective-permute-start(bf16[64,512]{1,0:T(8,128)(2,1)} %project.1), channel_id=1, source_target_pairs={{0,24},{8,16},{16,8},{24,0},{1,25},{9,17},{17,9},{25,1},{2,26},{10... | collective-permute-start | bytes 196616 | tf_op jit(solution)/shard_map/ppermute | solution.py:189
  72.3 5.8 %collective-permute-start.15 = (bf16[64,512]{1,0:T(8,128)(2,1)}, bf16[64,512]{1,0:T(8,128)(2,1)S(1)}, u32[]{:S(2)}, u32[]{:S(2)}) collective-permute-start(bf16[64,512]{1,0:T(8,128)(2,1)} %project.1), channel_id=1, source_target_pairs={{0,16},{8,24},{16,0},{24,8},{1,17},{9,25},{17,1},{25,9},{2,18},{10... | collective-permute-start | bytes 196616 | tf_op jit(solution)/shard_map/ppermute | solution.py:189
  73.1 5.0 %collective-permute-start.14 = (bf16[64,512]{1,0:T(8,128)(2,1)}, bf16[64,512]{1,0:T(8,128)(2,1)S(1)}, u32[]{:S(2)}, u32[]{:S(2)}) collective-permute-start(bf16[64,512]{1,0:T(8,128)(2,1)} %project.1), channel_id=1, source_target_pairs={{0,8},{8,0},{16,24},{24,16},{1,9},{9,1},{17,25},{25,17},{2,10},{10... | collective-permute-start | bytes 196616 | tf_op jit(solution)/shard_map/ppermute | solution.py:189
  79.1 9.1 %collective-permute-start.17 = (f32[2,128]{1,0:T(2,128)S(1)}, f32[2,128]{1,0:T(2,128)S(1)}, u32[]{:S(2)}, u32[]{:S(2)}) collective-permute-start(f32[2,128]{1,0:T(2,128)S(1)} %bitcast.40), channel_id=1, source_target_pairs={{0,1},{1,0},{2,3},{3,2},{4,5},{5,4},{6,7},{7,6},{8,9},{9,8},{10,11... | collective-permute-start | bytes 3080 | tf_op jit(solution)/shard_map/ppermute | solution.py:189
  88.2 11.8 %collective-permute-start.18 = (bf16[576,1024]{1,0:T(8,128)(2,1)}, bf16[576,1024]{1,0:T(8,128)(2,1)S(1)}, u32[]{:S(2)}, u32[]{:S(2)}) collective-permute-start(bf16[576,1024]{1,0:T(8,128)(2,1)} %widen.4), channel_id=1, source_target_pairs={{0,1},{1,0},{2,3},{3,2},{4,5},{5,4},{6,7},{7,6},{8,9},{9,8},{10,11... | collective-permute-start | bytes 3538952 | tf_op jit(solution)/shard_map/ppermute | solution.py:189
  88.7 11.2 %collective-permute-start.21 = (f32[2,128]{1,0:T(2,128)S(1)}, f32[2,128]{1,0:T(2,128)S(1)}, u32[]{:S(2)}, u32[]{:S(2)}) collective-permute-start(f32[2,128]{1,0:T(2,128)S(1)} %bitcast_add_fusion), channel_id=1, source_target_pairs={{0,6},{1,7},{2,4},{3,5},{4,2},{5,3},{6,0},{7,1},{8,14},{9,15},{10,... | collective-permute-start | bytes 3080 | tf_op jit(solution)/shard_map/ppermute | solution.py:189
  91.6 8.4 %collective-permute-start.19 = (f32[2,128]{1,0:T(2,128)S(1)}, f32[2,128]{1,0:T(2,128)S(1)}, u32[]{:S(2)}, u32[]{:S(2)}) collective-permute-start(f32[2,128]{1,0:T(2,128)S(1)} %bitcast_add_fusion), channel_id=1, source_target_pairs={{0,2},{1,3},{2,0},{3,1},{4,6},{5,7},{6,4},{7,5},{8,10},{9,11},{10,... | collective-permute-start | bytes 3080 | tf_op jit(solution)/shard_map/ppermute | solution.py:189
  91.6 8.4 %collective-permute-start.20 = (f32[2,128]{1,0:T(2,128)S(1)}, f32[2,128]{1,0:T(2,128)S(1)}, u32[]{:S(2)}, u32[]{:S(2)}) collective-permute-start(f32[2,128]{1,0:T(2,128)S(1)} %bitcast_add_fusion), channel_id=1, source_target_pairs={{0,4},{1,5},{2,6},{3,7},{4,0},{5,1},{6,2},{7,3},{8,12},{9,13},{10,... | collective-permute-start | bytes 3080 | tf_op jit(solution)/shard_map/ppermute | solution.py:189
  108.7 17.7 %collective-permute-start.22 = (bf16[576,1024]{1,0:T(8,128)(2,1)}, bf16[576,1024]{1,0:T(8,128)(2,1)S(1)}, u32[]{:S(2)}, u32[]{:S(2)}) collective-permute-start(bf16[576,1024]{1,0:T(8,128)(2,1)} %widen.6), channel_id=1, source_target_pairs={{0,1},{1,0},{2,3},{3,2},{4,5},{5,4},{6,7},{7,6},{8,9},{9,8},{10,11... | collective-permute-start | bytes 3538952 | tf_op jit(solution)/shard_map/ppermute | solution.py:189
  108.7 15.7 %collective-permute-start.28 = (bf16[288,1024]{1,0:T(8,128)(2,1)S(1)}, bf16[288,1024]{1,0:T(8,128)(2,1)S(1)}, u32[]{:S(2)}, u32[]{:S(2)}) collective-permute-start(bf16[288,1024]{1,0:T(8,128)(2,1)S(1)} %get-tuple-element.42), channel_id=1, source_target_pairs={{0,2},{1,3},{2,0},{3,1},{4,6},{5,7},{6,4},{7,5},{8,10},{9,11},{10,... | collective-permute-start | bytes 1769480 | tf_op jit(solution)/shard_map/ppermute | solution.py:189
  116.8 9.6 %copy-start.1 = (bf16[576,1024]{1,0:T(8,128)(2,1)S(1)}, bf16[576,1024]{1,0:T(8,128)(2,1)}, u32[]{:S(2)}) copy-start(bf16[576,1024]{1,0:T(8,128)(2,1)} %widen.7) | copy-start | bytes 3538948
  124.7 15.9 %collective-permute-start.29 = (bf16[144,1024]{1,0:T(8,128)(2,1)S(1)}, bf16[144,1024]{1,0:T(8,128)(2,1)S(1)}, u32[]{:S(2)}, u32[]{:S(2)}) collective-permute-start(bf16[144,1024]{1,0:T(8,128)(2,1)S(1)} %constant_dynamic-slice_fusion.4), channel_id=1, source_target_pairs={{0,4},{1,5},{2,6},{3,7},{4,0},{5,1},{6,2},{7,3},{8,12},{9,13},{10,... | collective-permute-start | bytes 884744 | tf_op jit(solution)/shard_map/ppermute | solution.py:189
  126.9 1.9 copy-start.23
  126.9 1.9 copy-start.26
  127.0 21.0 %collective-permute-start.23 = (bf16[288,1024]{1,0:T(8,128)(2,1)S(1)}, bf16[288,1024]{1,0:T(8,128)(2,1)S(1)}, u32[]{:S(2)}, u32[]{:S(2)}) collective-permute-start(bf16[288,1024]{1,0:T(8,128)(2,1)S(1)} %get-tuple-element.39), channel_id=1, source_target_pairs={{0,2},{1,3},{2,0},{3,1},{4,6},{5,7},{6,4},{7,5},{8,10},{9,11},{10,... | collective-permute-start | bytes 1769480 | tf_op jit(solution)/shard_map/ppermute | solution.py:189
  140.7 7.6 %copy-start.17 = (pred[144,256]{1,0:T(8,128)(4,1)S(1)}, pred[144,256]{1,0:T(8,128)(4,1)}, u32[]{:S(2)}) copy-start(pred[144,256]{1,0:T(8,128)(4,1)} %compare_reduce_fusion) | copy-start | bytes 110596
  148.3 14.7 %collective-permute-start.24 = (bf16[144,1024]{1,0:T(8,128)(2,1)S(1)}, bf16[144,1024]{1,0:T(8,128)(2,1)S(1)}, u32[]{:S(2)}, u32[]{:S(2)}) collective-permute-start(bf16[144,1024]{1,0:T(8,128)(2,1)S(1)} %constant_dynamic-slice_fusion.5), channel_id=1, source_target_pairs={{0,4},{1,5},{2,6},{3,7},{4,0},{5,1},{6,2},{7,3},{8,12},{9,13},{10,... | collective-permute-start | bytes 884744 | tf_op jit(solution)/shard_map/ppermute | solution.py:189
  163.3 12.0 %collective-permute-start.30 = (bf16[144,512]{1,0:T(8,128)(2,1)S(1)}, bf16[144,512]{1,0:T(8,128)(2,1)S(1)}, u32[]{:S(2)}, u32[]{:S(2)}) collective-permute-start(bf16[144,512]{1,0:T(8,128)(2,1)S(1)} %get-tuple-element.45), channel_id=1, source_target_pairs={{0,4},{1,5},{2,6},{3,7},{4,0},{5,1},{6,2},{7,3},{8,12},{9,13},{10,... | collective-permute-start | bytes 442376 | tf_op jit(solution)/shard_map/ppermute | solution.py:189
  163.4 15.0 %collective-permute-start.25 = (bf16[144,512]{1,0:T(8,128)(2,1)S(1)}, bf16[144,512]{1,0:T(8,128)(2,1)S(1)}, u32[]{:S(2)}, u32[]{:S(2)}) collective-permute-start(bf16[144,512]{1,0:T(8,128)(2,1)S(1)} %get-tuple-element.82), channel_id=1, source_target_pairs={{0,4},{1,5},{2,6},{3,7},{4,0},{5,1},{6,2},{7,3},{8,12},{9,13},{10,... | collective-permute-start | bytes 442376 | tf_op jit(solution)/shard_map/ppermute | solution.py:189
  175.3 9.9 %collective-permute-start.31 = (bf16[288,512]{1,0:T(8,128)(2,1)S(1)}, bf16[288,512]{1,0:T(8,128)(2,1)S(1)}, u32[]{:S(2)}, u32[]{:S(2)}) collective-permute-start(bf16[288,512]{1,0:T(8,128)(2,1)S(1)} %pad_maximum_fusion.4), channel_id=1, source_target_pairs={{0,2},{1,3},{2,0},{3,1},{4,6},{5,7},{6,4},{7,5},{8,10},{9,11},{10,... | collective-permute-start | bytes 884744 | tf_op jit(solution)/shard_map/ppermute | solution.py:189
  178.5 12.5 %collective-permute-start.26 = (bf16[288,512]{1,0:T(8,128)(2,1)S(1)}, bf16[288,512]{1,0:T(8,128)(2,1)S(1)}, u32[]{:S(2)}, u32[]{:S(2)}) collective-permute-start(bf16[288,512]{1,0:T(8,128)(2,1)S(1)} %pad_maximum_fusion.3), channel_id=1, source_target_pairs={{0,2},{1,3},{2,0},{3,1},{4,6},{5,7},{6,4},{7,5},{8,10},{9,11},{10,... | collective-permute-start | bytes 884744 | tf_op jit(solution)/shard_map/ppermute | solution.py:189
  185.4 5.7 %copy-start.2 = (bf16[576,512]{1,0:T(8,128)(2,1)}, bf16[576,512]{1,0:T(8,128)(2,1)S(1)}, u32[]{:S(2)}) copy-start(bf16[576,512]{1,0:T(8,128)(2,1)S(1)} %pad_maximum_fusion.2.own_ref) | copy-start | bytes 1769476
  185.4 5.8 %copy-start.25 = (s32[8]{0:T(128)S(1)}, s32[8]{0:T(128)}, u32[]{:S(2)}) copy-start(s32[8]{0:T(128)} %copy-done.24) | copy-start | bytes 100
  185.4 7.4 %collective-permute-start.32 = (bf16[576,512]{1,0:T(8,128)(2,1)S(1)}, bf16[576,512]{1,0:T(8,128)(2,1)S(1)}, u32[]{:S(2)}, u32[]{:S(2)}) collective-permute-start(bf16[576,512]{1,0:T(8,128)(2,1)S(1)} %pad_maximum_fusion.2.own_ref), channel_id=1, source_target_pairs={{0,1},{1,0},{2,3},{3,2},{4,5},{5,4},{6,7},{7,6},{8,9},{9,8},{10,11... | collective-permute-start | bytes 1769480 | tf_op jit(solution)/shard_map/ppermute | solution.py:189
  191.2 10.8 %copy-start.3 = (bf16[576,512]{1,0:T(8,128)(2,1)}, bf16[576,512]{1,0:T(8,128)(2,1)S(1)}, u32[]{:S(2)}) copy-start(bf16[576,512]{1,0:T(8,128)(2,1)S(1)} %pad_maximum_fusion.1.own_ref) | copy-start | bytes 1769476
  191.2 10.8 %collective-permute-start.27 = (bf16[576,512]{1,0:T(8,128)(2,1)S(1)}, bf16[576,512]{1,0:T(8,128)(2,1)S(1)}, u32[]{:S(2)}, u32[]{:S(2)}) collective-permute-start(bf16[576,512]{1,0:T(8,128)(2,1)S(1)} %pad_maximum_fusion.1.own_ref), channel_id=1, source_target_pairs={{0,1},{1,0},{2,3},{3,2},{4,5},{5,4},{6,7},{7,6},{8,9},{9,8},{10,11... | collective-permute-start | bytes 1769480 | tf_op jit(solution)/shard_map/ppermute | solution.py:189
  192.8 1.0 copy-start.6
  202.0 0.8 copy-start.7
  211.0 8.0 %copy-start.5 = (bf16[64,512]{1,0:T(8,128)(2,1)S(1)}, bf16[64,512]{1,0:T(8,128)(2,1)}, u32[]{:S(2)}) copy-start(bf16[64,512]{1,0:T(8,128)(2,1)} %project.1) | copy-start | bytes 196612
  212.2 5.6 %collective-permute-start.35 = (bf16[64,512]{1,0:T(8,128)(2,1)S(1)}, bf16[64,512]{1,0:T(8,128)(2,1)S(1)}, u32[]{:S(2)}, u32[]{:S(2)}) collective-permute-start(bf16[64,512]{1,0:T(8,128)(2,1)S(1)} %get-tuple-element.67), channel_id=1, source_target_pairs={{0,24},{8,16},{16,8},{24,0},{1,25},{9,17},{17,9},{25,1},{2,26},{10... | collective-permute-start | bytes 196616 | tf_op jit(solution)/shard_map/ppermute | solution.py:189
  213.4 5.6 %collective-permute-start.34 = (bf16[64,512]{1,0:T(8,128)(2,1)S(1)}, bf16[64,512]{1,0:T(8,128)(2,1)S(1)}, u32[]{:S(2)}, u32[]{:S(2)}) collective-permute-start(bf16[64,512]{1,0:T(8,128)(2,1)S(1)} %get-tuple-element.68), channel_id=1, source_target_pairs={{0,16},{8,24},{16,0},{24,8},{1,17},{9,25},{17,1},{25,9},{2,18},{10... | collective-permute-start | bytes 196616 | tf_op jit(solution)/shard_map/ppermute | solution.py:189
  214.7 4.4 %collective-permute-start.33 = (bf16[64,512]{1,0:T(8,128)(2,1)S(1)}, bf16[64,512]{1,0:T(8,128)(2,1)S(1)}, u32[]{:S(2)}, u32[]{:S(2)}) collective-permute-start(bf16[64,512]{1,0:T(8,128)(2,1)S(1)} %get-tuple-element.66), channel_id=1, source_target_pairs={{0,8},{8,0},{16,24},{24,16},{1,9},{9,1},{17,25},{25,17},{2,10},{10... | collective-permute-start | bytes 196616 | tf_op jit(solution)/shard_map/ppermute | solution.py:189
  (3 other events, 2.0 us)
